TPU v7x, 32 devices: a whole 2x2x4 slice. The times are simulated.
32 devices in a mesh: img: 8 (over z, y), row: 2 (over x), col: 2 (over core).
Axes of the slice: x: 2, y: 2, z: 4, core: 2. Of those that a mesh axis runs over, the one named last changes fastest.
Arguments:
- latents: bfloat16 [24, 4, 64, 64], P('img', None, 'row', 'col'), may hold values from -6 to 6
- time_bin: int32 [24], P('img'), may hold values from 0 to 99
- class_label: int32 [24], P('img'), may hold values from 0 to 1000
- live: int32 [24], P('img'), may hold values from 0 to 1, as said below
- time_table: bfloat16 [100, 384], replicated, may hold values from -4 to 4
- class_table: bfloat16 [1001, 384], replicated, may hold values from -4 to 4
- patch_weight: bfloat16 [16, 384], replicated, may hold values from -1.5 to 1.5
- patch_bias: bfloat16 [384], replicated, may hold values from -3 to 3
- ada_weight: bfloat16 [384, 2304], replicated, may hold values from -0.3125 to 0.3125
- ada_bias: bfloat16 [2304], replicated, may hold values from -3 to 3
- qkv_weight: bfloat16 [384, 1152], replicated, may hold values from -0.3125 to 0.3125
- qv_bias: bfloat16 [768], replicated, may hold values from -2 to 2
- proj_weight: bfloat16 [384, 384], replicated, may hold values from -1.25 to 1.25
- proj_bias: bfloat16 [384], replicated, may hold values from -2 to 2
- fc1_weight: bfloat16 [384, 1536], replicated, may hold values from -0.3125 to 0.3125
- fc1_bias: bfloat16 [1536], replicated, may hold values from -3 to 3
- fc2_weight: bfloat16 [1536, 384], replicated, may hold values from -0.21875 to 0.21875
- fc2_bias: bfloat16 [384], replicated, may hold values from -2 to 2
- final_ada_weight: bfloat16 [384, 768], replicated, may hold values from -0.3125 to 0.3125
- final_ada_bias: bfloat16 [768], replicated, may hold values from -3 to 3
- out_weight: bfloat16 [384, 16], replicated, may hold values from -0.3125 to 0.3125
- out_bias: bfloat16 [16], replicated, may hold values from -3 to 3
- cotangent: bfloat16 [24, 4, 64, 64], P('img', None, 'row', 'col'), may hold values from -6 to 6
Outputs:
- out_latents: bfloat16 [24, 4, 64, 64], P('img', None, 'row', 'col')
- latent_grad: float32 [24, 4, 64, 64], P('img', None, 'row', 'col')
- time_grad: float32 [100, 384], replicated
- class_grad: float32 [1001, 384], replicated
- patch_weight_grad: float32 [16, 384], replicated
- patch_bias_grad: float32 [384], replicated
- ada_weight_grad: float32 [384, 2304], replicated
- ada_bias_grad: float32 [2304], replicated
- qkv_weight_grad: float32 [384, 1152], replicated
- qv_bias_grad: float32 [768], replicated
- proj_weight_grad: float32 [384, 384], replicated
- proj_bias_grad: float32 [384], replicated
- fc1_weight_grad: float32 [384, 1536], replicated
- fc1_bias_grad: float32 [1536], replicated
- fc2_weight_grad: float32 [1536, 384], replicated
- fc2_bias_grad: float32 [384], replicated
- final_ada_weight_grad: float32 [384, 768], replicated
- final_ada_bias_grad: float32 [768], replicated
- out_weight_grad: float32 [384, 16], replicated
- out_bias_grad: float32 [16], replicated
Inputs may be any that keep to these rules, and one draw needn't show every extreme that they name: Within each aligned block of 3 slots (those of one index of img) the live slots come first; every block has at least one and some block is full.
All inputs are finite; a program needn't handle non-finite values.
Results may differ from a plain program's by a relative error of at most 0.011.
Values may be sent and summed in bfloat16 or wider, within the bound.
A program may use at most 192 MiB of HBM per device.

v0:
```python
import jax
import jax.numpy as jnp
from jax import lax
from jax.sharding import PartitionSpec as P

HEADS = 6
LATENT = 64


def passed_along(block, axis, distance):
    devices = range(lax.axis_size(axis))
    route = [((i - distance) % len(devices), i) for i in devices]
    return lax.ppermute(block, axis, route)


def positions(grid, width):
    quarter = width // 4
    omega = 1.0 / 10000.0 ** (jnp.arange(quarter, dtype=jnp.float32) / quarter)
    places = jnp.arange(grid, dtype=jnp.float32)
    angles = places[:, None] * omega[None, :]
    single = jnp.concatenate([jnp.sin(angles), jnp.cos(angles)], axis=1)
    first = jnp.broadcast_to(single[:, None, :], (grid, grid, width // 2))
    second = jnp.broadcast_to(single[None, :, :], (grid, grid, width // 2))
    return jnp.concatenate([first, second], axis=2)


def to_patches(tile):
    slots, chans, height, wide = tile.shape
    shaped = tile.reshape(slots, chans, height // 2, 2, wide // 2, 2).transpose(0, 2, 4, 1, 3, 5)
    return shaped.reshape(slots, height // 2 * (wide // 2), chans * 4)


def from_patches(rows, chans, height, wide):
    slots = rows.shape[0]
    shaped = rows.reshape(slots, height // 2, wide // 2, chans, 2, 2).transpose(0, 3, 1, 4, 2, 5)
    return shaped.reshape(slots, chans, height, wide)


def modulate(value, shift, scale):
    centred = value - jnp.mean(value, axis=-1, keepdims=True)
    spread = jnp.mean(centred * centred, axis=-1, keepdims=True)
    return centred * lax.rsqrt(spread + 1e-06) * (1.0 + scale[:, None, :]) + shift[:, None, :]


def swish(v):
    return v * jax.nn.sigmoid(v)


def gelu_tanh(v):
    return jax.nn.gelu(v, approximate=True)


def mat(value, weight):
    return jnp.einsum("spd,de->spe", value, weight, preferred_element_type=jnp.float32)


def mat_back(grad, weight):
    return jnp.einsum("spe,de->spd", grad, weight, preferred_element_type=jnp.float32)


def outer(value, grad):
    return jnp.einsum("spd,spe->de", value, grad, preferred_element_type=jnp.float32)


def split_heads(value, heads):
    slots, tokens, width = value.shape
    return value.reshape(slots, tokens, heads, width // heads)


def cond_tables(cond, grad_mod, grad_fmod, time_ids, class_ids, ada_w, final_w, bins, classes):
    highest = lax.Precision.HIGHEST
    cact = swish(cond)
    ada_weight_grad = jnp.dot(cact.T, grad_mod, precision=highest)
    ada_bias_grad = jnp.sum(grad_mod, axis=0)
    final_ada_weight_grad = jnp.dot(cact.T, grad_fmod, precision=highest)
    final_ada_bias_grad = jnp.sum(grad_fmod, axis=0)
    grad_cact = jnp.dot(grad_mod, ada_w.T, precision=highest) + jnp.dot(
        grad_fmod, final_w.T, precision=highest
    )
    _, swish_back = jax.vjp(swish, cond)
    grad_cond = swish_back(grad_cact)[0]
    onehot_time = (time_ids[:, None] == jnp.arange(bins, dtype=jnp.int32)[None, :]).astype(
        jnp.float32
    )
    onehot_class = (class_ids[:, None] == jnp.arange(classes, dtype=jnp.int32)[None, :]).astype(
        jnp.float32
    )
    time_grad = jnp.dot(onehot_time.T, grad_cond, precision=highest)
    class_grad = jnp.dot(onehot_class.T, grad_cond, precision=highest)
    return (
        time_grad,
        class_grad,
        ada_weight_grad,
        ada_bias_grad,
        final_ada_weight_grad,
        final_ada_bias_grad,
    )


def attend(query, keys, values, heads):
    slots, tokens, width = query.shape
    scale = 1.0 / (width // heads) ** 0.5
    scores = (
        jnp.einsum(
            "sqhd,skhd->shqk",
            split_heads(query, heads),
            split_heads(keys, heads),
            preferred_element_type=jnp.float32,
        )
        * scale
    )
    top = jnp.max(scores, axis=-1, keepdims=True)
    log_total = top + jnp.log(jnp.sum(jnp.exp(scores - top), axis=-1, keepdims=True))
    weights = jnp.exp(scores - log_total).astype(jnp.bfloat16)
    result = jnp.einsum(
        "shqk,skhd->sqhd", weights, split_heads(values, heads), preferred_element_type=jnp.float32
    )
    return (result.reshape(slots, tokens, width), log_total)


def attend_back(query, keys, values, log_total, grad_out, heads):
    slots, tokens, width = query.shape
    scale = 1.0 / (width // heads) ** 0.5
    query_h = split_heads(query, heads)
    keys_h = split_heads(keys, heads)
    grad_h = split_heads(grad_out, heads)
    scores = (
        jnp.einsum("sqhd,skhd->shqk", query_h, keys_h, preferred_element_type=jnp.float32) * scale
    )
    weights = jnp.exp(scores - log_total)
    grad_w = jnp.einsum(
        "sqhd,skhd->shqk", grad_h, split_heads(values, heads), preferred_element_type=jnp.float32
    )
    inner = jnp.sum(weights * grad_w, axis=-1, keepdims=True)
    grad_s = (weights * (grad_w - inner)).astype(jnp.bfloat16)
    grad_q = (
        jnp.einsum("shqk,skhd->sqhd", grad_s, keys_h, preferred_element_type=jnp.float32) * scale
    )
    grad_k = (
        jnp.einsum("shqk,sqhd->skhd", grad_s, query_h, preferred_element_type=jnp.float32) * scale
    )
    grad_v = jnp.einsum(
        "shqk,sqhd->skhd", weights.astype(jnp.bfloat16), grad_h, preferred_element_type=jnp.float32
    )
    many = keys.shape[1]
    return (
        grad_q.reshape(slots, tokens, width),
        grad_k.reshape(slots, many, width),
        grad_v.reshape(slots, many, width),
    )


def local(
    latents,
    time_bin,
    class_label,
    live,
    time_table,
    class_table,
    patch_weight,
    patch_bias,
    ada_weight,
    ada_bias,
    qkv_weight,
    qv_bias,
    proj_weight,
    proj_bias,
    fc1_weight,
    fc1_bias,
    fc2_weight,
    fc2_bias,
    final_ada_weight,
    final_ada_bias,
    out_weight,
    out_bias,
    cotangent,
):
    highest = lax.Precision.HIGHEST
    slots, chans, tile_rows, tile_cols = latents.shape
    grid_rows = tile_rows // 2
    grid_cols = tile_cols // 2
    width = qkv_weight.shape[0]
    heads = HEADS
    live_f = live.astype(jnp.float32)
    bins = time_table.shape[0]
    classes = class_table.shape[0]
    above = passed_along(latents[:, :, -1:, :], "row", 1)
    shifted = jnp.concatenate([above, latents[:, :, :-1, :]], axis=2)
    beside = passed_along(shifted[:, :, :, -1:], "col", 1)
    shifted = jnp.concatenate([beside, shifted[:, :, :, :-1]], axis=3)
    patches = to_patches(shifted.astype(jnp.float32))
    table = positions(LATENT // 2, width)
    local_pos = lax.dynamic_slice(
        table,
        (lax.axis_index("row") * grid_rows, lax.axis_index("col") * grid_cols, jnp.int32(0)),
        (grid_rows, grid_cols, width),
    ).reshape(grid_rows * grid_cols, width)
    patch_w = patch_weight.astype(jnp.float32)
    tok0 = (
        jnp.einsum("spk,kd->spd", patches, patch_w, precision=highest)
        + patch_bias.astype(jnp.float32)
        + local_pos[None]
    )
    onehot_time = (time_bin[:, None] == jnp.arange(bins, dtype=jnp.int32)[None, :]).astype(
        jnp.float32
    )
    onehot_class = (class_label[:, None] == jnp.arange(classes, dtype=jnp.int32)[None, :]).astype(
        jnp.float32
    )
    cond = jnp.dot(onehot_time, time_table.astype(jnp.float32), precision=highest) + jnp.dot(
        onehot_class, class_table.astype(jnp.float32), precision=highest
    )
    cact = swish(cond)
    ada_w = ada_weight.astype(jnp.float32)
    final_w = final_ada_weight.astype(jnp.float32)
    mod = jnp.dot(cact, ada_w, precision=highest) + ada_bias.astype(jnp.float32)
    sh1, sc1, g1, sh2, sc2, g2 = jnp.split(mod, 6, axis=1)
    fmod = jnp.dot(cact, final_w, precision=highest) + final_ada_bias.astype(jnp.float32)
    shf, scf = jnp.split(fmod, 2, axis=1)
    x1 = modulate(tok0, sh1, sc1).astype(jnp.bfloat16)
    qv_f = qv_bias.astype(jnp.float32)
    bias_full = jnp.concatenate([qv_f[:width], jnp.zeros((width,), jnp.float32), qv_f[width:]])
    qkv = (mat(x1, qkv_weight) + bias_full).astype(jnp.bfloat16)
    query = qkv[:, :, :width]
    key = qkv[:, :, width : 2 * width]
    value = qkv[:, :, 2 * width :]
    all_keys, all_values = (
        lax.all_gather(key, ("row", "col"), axis=1, tiled=True),
        lax.all_gather(value, ("row", "col"), axis=1, tiled=True),
    )
    att, log_total = attend(query, all_keys, all_values, heads)
    att_b = att.astype(jnp.bfloat16)
    branch = mat(att_b, proj_weight) + proj_bias.astype(jnp.float32)
    resid = tok0 + g1[:, None, :] * branch
    x2 = modulate(resid, sh2, sc2).astype(jnp.bfloat16)
    hidden_in = mat(x2, fc1_weight) + fc1_bias.astype(jnp.float32)
    hidden = gelu_tanh(hidden_in).astype(jnp.bfloat16)
    mlp = mat(hidden, fc2_weight) + fc2_bias.astype(jnp.float32)
    x3 = resid + g2[:, None, :] * mlp
    xf = modulate(x3, shf, scf).astype(jnp.bfloat16)
    rows = (mat(xf, out_weight) + out_bias.astype(jnp.float32)) * live_f[:, None, None]
    out_tile = from_patches(rows, chans, tile_rows, tile_cols).astype(jnp.bfloat16)
    lead_row = passed_along(out_tile[:, :, :1, :], "row", -1)
    moved = jnp.concatenate([out_tile[:, :, 1:, :], lead_row], axis=2)
    lead_col = passed_along(moved[:, :, :, :1], "col", -1)
    out_latents = jnp.concatenate([moved[:, :, :, 1:], lead_col], axis=3)
    tail_col = passed_along(cotangent[:, :, :, -1:], "col", 1)
    back = jnp.concatenate([tail_col, cotangent[:, :, :, :-1]], axis=3)
    tail_row = passed_along(back[:, :, -1:, :], "row", 1)
    back = jnp.concatenate([tail_row, back[:, :, :-1, :]], axis=2)
    grad_y = to_patches(back) * live.astype(jnp.bfloat16)[:, None, None]
    out_weight_grad = outer(xf, grad_y)
    out_bias_grad = jnp.sum(grad_y.astype(jnp.float32), axis=(0, 1))
    grad_xf = mat_back(grad_y, out_weight)
    _, final_back = jax.vjp(modulate, x3, shf, scf)
    grad_x3, grad_shf, grad_scf = final_back(grad_xf)
    grad_mlp = (g2[:, None, :] * grad_x3).astype(jnp.bfloat16)
    grad_g2 = jnp.sum(mlp * grad_x3, axis=1)
    fc2_weight_grad = outer(hidden, grad_mlp)
    fc2_bias_grad = jnp.sum(grad_mlp.astype(jnp.float32), axis=(0, 1))
    grad_hidden = mat_back(grad_mlp, fc2_weight)
    _, gelu_back = jax.vjp(gelu_tanh, hidden_in)
    grad_in = gelu_back(grad_hidden)[0].astype(jnp.bfloat16)
    fc1_weight_grad = outer(x2, grad_in)
    fc1_bias_grad = jnp.sum(grad_in.astype(jnp.float32), axis=(0, 1))
    grad_x2 = mat_back(grad_in, fc1_weight)
    _, mid_back = jax.vjp(modulate, resid, sh2, sc2)
    grad_part, grad_sh2, grad_sc2 = mid_back(grad_x2)
    grad_resid = grad_x3 + grad_part
    grad_branch = (g1[:, None, :] * grad_resid).astype(jnp.bfloat16)
    grad_g1 = jnp.sum(branch * grad_resid, axis=1)
    proj_weight_grad = outer(att_b, grad_branch)
    proj_bias_grad = jnp.sum(grad_branch.astype(jnp.float32), axis=(0, 1))
    grad_att = mat_back(grad_branch, proj_weight).astype(jnp.bfloat16)
    back_keys, back_values = (
        lax.all_gather(key, ("row", "col"), axis=1, tiled=True),
        lax.all_gather(value, ("row", "col"), axis=1, tiled=True),
    )
    grad_q, grad_kall, grad_vall = attend_back(
        query, back_keys, back_values, log_total, grad_att, heads
    )
    grad_k, grad_v = (
        lax.psum_scatter(
            grad_kall.astype(jnp.bfloat16), ("row", "col"), scatter_dimension=1, tiled=True
        ).astype(jnp.float32),
        lax.psum_scatter(
            grad_vall.astype(jnp.bfloat16), ("row", "col"), scatter_dimension=1, tiled=True
        ).astype(jnp.float32),
    )
    grad_qkv = jnp.concatenate([grad_q, grad_k, grad_v], axis=-1).astype(jnp.bfloat16)
    qkv_weight_grad = outer(x1, grad_qkv)
    qkv_sums = jnp.sum(grad_qkv.astype(jnp.float32), axis=(0, 1))
    qv_bias_grad = jnp.concatenate([qkv_sums[:width], qkv_sums[2 * width :]])
    grad_x1 = mat_back(grad_qkv, qkv_weight)
    _, first_back = jax.vjp(modulate, tok0, sh1, sc1)
    grad_part, grad_sh1, grad_sc1 = first_back(grad_x1)
    grad_tok0 = grad_resid + grad_part
    patch_weight_grad = jnp.einsum("spk,spd->kd", patches, grad_tok0, precision=highest)
    patch_bias_grad = jnp.sum(grad_tok0, axis=(0, 1))
    grad_patches = jnp.einsum("spd,kd->spk", grad_tok0, patch_w, precision=highest)
    grad_tile = from_patches(grad_patches, chans, tile_rows, tile_cols)
    home_col = passed_along(grad_tile[:, :, :, :1], "col", -1)
    grad_tile = jnp.concatenate([grad_tile[:, :, :, 1:], home_col], axis=3)
    home_row = passed_along(grad_tile[:, :, :1, :], "row", -1)
    latent_grad = jnp.concatenate([grad_tile[:, :, 1:, :], home_row], axis=2)
    grad_mod = jnp.concatenate([grad_sh1, grad_sc1, grad_g1, grad_sh2, grad_sc2, grad_g2], axis=1)
    grad_fmod = jnp.concatenate([grad_shf, grad_scf], axis=1)
    local_parts = cond_tables(
        cond, grad_mod, grad_fmod, time_bin, class_label, ada_w, final_w, bins, classes
    )
    summed = lax.psum(
        (
            local_parts[0],
            local_parts[1],
            patch_weight_grad,
            patch_bias_grad,
            local_parts[2],
            local_parts[3],
            qkv_weight_grad,
            qv_bias_grad,
            proj_weight_grad,
            proj_bias_grad,
            fc1_weight_grad,
            fc1_bias_grad,
            fc2_weight_grad,
            fc2_bias_grad,
            local_parts[4],
            local_parts[5],
            out_weight_grad,
            out_bias_grad,
        ),
        ("img", "row", "col"),
    )
    return (
        out_latents,
        latent_grad,
        summed[0],
        summed[1],
        summed[2],
        summed[3],
        summed[4],
        summed[5],
        summed[6],
        summed[7],
        summed[8],
        summed[9],
        summed[10],
        summed[11],
        summed[12],
        summed[13],
        summed[14],
        summed[15],
        summed[16],
        summed[17],
    )


def solution(mesh):
    placed = (
        P("img", None, "row", "col"),
        P("img"),
        P("img"),
        P("img"),
        P(),
        P(),
        P(),
        P(),
        P(),
        P(),
        P(),
        P(),
        P(),
        P(),
        P(),
        P(),
        P(),
        P(),
        P(),
        P(),
        P(),
        P(),
        P("img", None, "row", "col"),
    )
    return jax.shard_map(
        local,
        mesh=mesh,
        in_specs=placed,
        out_specs=(
            P("img", None, "row", "col"),
            P("img", None, "row", "col"),
            P(),
            P(),
            P(),
            P(),
            P(),
            P(),
            P(),
            P(),
            P(),
            P(),
            P(),
            P(),
            P(),
            P(),
            P(),
            P(),
            P(),
            P(),
        ),
        check_vma=False,
    )
```

profile of v0, /device:TPU:0, one launch (start us, length us, event | category | flops | bytes accessed | tf_op | source)
XLA Modules:
  0.0 634.2 jit_solution(4318728474660087629)
XLA Ops:
  8.1 3.0 collective-permute-start
  19.5 1.8 copy.122
  28.5 3.0 collective-permute-done.5
  32.3 1.8 copy.131
  35.7 14.2 %all-gather.5.cloned.1.call-done = bf16[3,1024,384]{2,1,0:T(8,128)(2,1)} async-done(((bf16[3,256,384]{2,1,0:T(8,128)(2,1)}), bf16[3,1024,384]{2,1,0:T(8,128)(2,1)}) %all-gather.5.cloned.1.call-update) | async-done | bytes 2359312 | tf_op jit(solution)/shard_map/all_gather | solution.py:228
  49.9 4.3 copy.125
  54.1 9.9 %multiply_reduce_fusion.1 = (f32[3,6,256]{2,1,0:T(8,128)S(1)}, f32[3,6,256,1024]{3,2,1,0:T(8,128)}) fusion(bf16[3,256,6,64]{1,3,2,0:T(8,128)(2,1)S(1)} %bitcast.145, bf16[3,1024,6,64]{1,3,2,0:T(8,128)(2,1)} %bitcast.131), kind=kOutput, calls=%fused_computation.4 | convolution fusion | flops 613412352 | bytes 21841920 | tf_op jit(solution)/shard_map/sqhd,skhd->shqk/dot_general | solution.py:104
  64.1 9.8 %exponential_reduce_fusion = f32[3,6,256]{2,1,0:T(8,128)S(1)} fusion(f32[3,6,256,1024]{3,2,1,0:T(8,128)} %get-tuple-element.124, f32[3,6,256]{2,1,0:T(8,128)S(1)} %get-tuple-element.123), kind=kLoop, calls=%fused_computation.3 | loop fusion | flops 14151168 | bytes 18911232 | tf_op jit(solution)/shard_map/reduce_sum | solution.py:113
  73.9 2.2 all-gather.3.cloned.1.call-done
  76.1 4.3 copy.123
  80.4 9.3 %fusion.13 = bf16[3,6,64,256]{3,2,1,0:T(8,128)(2,1)S(1)} fusion(bf16[3,1024,6,64]{1,3,2,0:T(8,128)(2,1)} %bitcast.133, f32[3,6,256,1024]{3,2,1,0:T(8,128)} %get-tuple-element.124, f32[3,6,256]{2,1,0:T(8,128)S(1)} %log_add_fusion), kind=kOutput, calls=%fused_computation.39 | convolution fusion | flops 618430464 | bytes 21841920 | tf_op jit(solution)/shard_map/shqk,skhd->sqhd/dot_general | solution.py:115
  89.8 1.6 fusion.75
  94.1 2.1 fusion.74
  99.7 4.6 convert_reduce_fusion
  107.0 2.1 convert_reduce_fusion.4
  112.6 10.6 %convolution_convert_fusion = bf16[3,6,64,1024]{3,2,1,0:T(8,128)(2,1)} fusion(bf16[3,256,6,64]{1,3,2,0:T(8,128)(2,1)S(1)} %bitcast.139, f32[3,6,256,1024]{3,2,1,0:T(8,128)} %get-tuple-element.124, f32[3,6,256]{2,1,0:T(8,128)} %copy-done.32), kind=kOutput, calls=%fused_computation.25 | convolution fusion | flops 619315200 | bytes 21841920 | tf_op jit(solution)/shard_map/shqk,sqhd->skhd/dot_general | solution.py:142
  123.2 4.3 copy.134
  127.6 14.0 %multiply_reduce_fusion = (f32[3,6,256]{2,1,0:T(8,128)S(1)}, f32[3,6,256,1024]{3,2,1,0:T(8,128)}) fusion(f32[3,6,256,1024]{3,2,1,0:T(8,128)} %get-tuple-element.124, f32[3,6,256]{2,1,0:T(8,128)} %copy-done.32, bf16[3,256,6,64]{1,3,2,0:T(8,128)(2,1)S(1)} %bitcast.140, bf16[3,1024,6,64]{1,3,2,0:T(8,128)(2,1)} %bitcast.134), kind=kOutput, calls=%fused_computation.1 | convolution fusion | flops 622849536 | bytes 40734720 | tf_op jit(solution)/shard_map/sqhd,skhd->shqk/dot_general | solution.py:131
  141.6 13.5 %multiply_convert_fusion = bf16[3,6,256,1024]{3,2,1,0:T(8,128)(2,1)S(1)} fusion(f32[3,6,256,1024]{3,2,1,0:T(8,128)} %get-tuple-element.131, f32[3,6,256,1024]{3,2,1,0:T(8,128)} %get-tuple-element.124, f32[3,6,256]{2,1,0:T(8,128)S(1)} %get-tuple-element.130, f32[3,6,256]{2,1,0:T(8,128)S(1)} %copy-done.33), kind=kLoop, calls=%fused_computation | loop fusion | flops 23592960 | bytes 47222784 | tf_op jit(solution)/shard_map/convert_element_type | solution.py:135
  155.2 3.6 multiply_convert_fusion.1
  159.5 4.3 copy.133
  164.4 2.2 convert_reduce_fusion.2
  167.4 9.1 %fusion.16 = bf16[3,6,64,256]{3,2,1,0:T(8,128)(2,1)} fusion(bf16[3,1024,6,64]{1,3,2,0:T(8,128)(2,1)} %bitcast.132, bf16[3,6,256,1024]{3,2,1,0:T(8,128)(2,1)} %copy-done.1), kind=kOutput, calls=%fused_computation.40 | convolution fusion | flops 604569600 | bytes 12386304 | tf_op jit(solution)/shard_map/shqk,skhd->sqhd/dot_general | solution.py:137
  176.5 2.2 copy.135
  180.1 2.6 convolution_bitcast_fusion.5
  185.2 2.2 fusion.53
  187.4 2.7 convolution_bitcast_fusion.1
  190.1 6.1 convolution_bitcast_fusion
  197.0 2.8 multiply_reduce_fusion.7
  200.0 1.5 multiply_reduce_fusion.6
  202.7 2.2 fusion.72
  208.7 5.9 fusion.68
  217.0 2.3 fusion.51
  219.8 2.3 fusion.38
  222.8 3.6 convolution_bitcast_fusion.2
  232.1 2.1 slice.97
  234.2 1.9 copy.128
  238.0 2.7 copy.136
  241.9 1.6 pad_maximum_fusion.5
  245.0 2.2 copy.137
  247.2 1.6 copy.138
  248.8 1.7 collective-permute-start.7
  250.7 1.9 collective-permute-done.7
  253.2 95.9 %all-reduce.5.cloned.1.call-done = (f32[16,384]{1,0:T(8,128)}, f32[384]{0:T(512)}, f32[2304]{0:T(1024)}, f32[768]{0:T(1024)}, f32[384]{0:T(512)}, /*index=5*/f32...) async-done(((f32[16,384]{1,0:T(8,128)}, f32[384]{0:T(512)}, f32[2304]{0:T(1024)}, f32[768]{0:T(1024)}, f32[384]{0:T(512)}, ...) | async-done | bytes 75344 | tf_op jit(solution)/shard_map/psum | solution.py:311
  349.2 257.1 %all-reduce.7.cloned.1.call-done = (f32[100,384]{1,0:T(8,128)}, f32[1001,384]{1,0:T(8,128)}, f32[384,2304]{1,0:T(8,128)}, f32[384,1152]{1,0:T(8,128)}, f32[384,3...) async-done(((f32[100,384]{1,0:T(8,128)}, f32[1001,384]{1,0:T(8,128)}, f32[384,2304]{1,0:T(8,128)}, f32[384,1152]{1,0:T(8,128)}, ...) | async-done | bytes 13487632 | tf_op jit(solution)/shard_map/psum | solution.py:311
  606.3 1.6 copy.170
  607.9 2.6 copy.171
  611.7 4.2 copy.174
  (337 shorter events, 69.7 us)
Async XLA Ops:
  7.2 7.9 %copy-start = (bf16[384,2304]{1,0:T(8,128)(2,1)S(1)}, bf16[384,2304]{1,0:T(8,128)(2,1)}, u32[]{:S(2)}) copy-start(bf16[384,2304]{1,0:T(8,128)(2,1)} %param.31) | copy-start | bytes 5308420
  7.2 42.7 %all-gather.5.cloned.1.call-start = ((), (), s32[]{:S(2)}) async-start(), calls=%async_computation.3 | async-start | bytes 2949120 | tf_op jit(solution)/shard_map/all_gather | solution.py:228
  8.1 8.4 %collective-permute-start = (bf16[3,4,1,32]{3,2,1,0:T(2,128)(2,1)S(1)}, bf16[3,4,1,32]{3,2,1,0:T(2,128)(2,1)S(1)}, u32[]{:S(2)}, u32[]{:S(2)}) collective-permute-start(bf16[3,4,1,32]{3,2,1,0:T(2,128)(2,1)S(1)} %slice.69), channel_id=1, source_target_pairs={{2,0},{0,2},{3,1},{1,3},{6,4},{4,6},{7,5},{5,7},{10,8},{8,10},{11,... | collective-permute-start | bytes 2312 | tf_op jit(solution)/shard_map/ppermute | solution.py:13
  15.9 6.5 %copy-start.53 = (f32[3,384]{1,0:T(4,128)}, f32[3,384]{1,0:T(4,128)S(1)}, u32[]{:S(2)}) copy-start(f32[3,384]{1,0:T(4,128)S(1)} %get-tuple-element.109) | copy-start | bytes 13828
  15.9 6.5 %copy-start.79 = (f32[3,384]{1,0:T(4,128)}, f32[3,384]{1,0:T(4,128)S(1)}, u32[]{:S(2)}) copy-start(f32[3,384]{1,0:T(4,128)S(1)} %get-tuple-element.108) | copy-start | bytes 13828
  16.0 75.8 %copy-start.49 = (f32[3,384]{1,0:T(4,128)}, f32[3,384]{1,0:T(4,128)S(1)}, u32[]{:S(2)}) copy-start(f32[3,384]{1,0:T(4,128)S(1)} %get-tuple-element.106) | copy-start | bytes 13828
  16.0 91.1 %copy-start.42 = (f32[3,384]{1,0:T(4,128)}, f32[3,384]{1,0:T(4,128)S(1)}, u32[]{:S(2)}) copy-start(f32[3,384]{1,0:T(4,128)S(1)} %get-tuple-element.107) | copy-start | bytes 13828
  17.4 1.4 collective-permute-start.1
  17.5 4.0 copy-start.60
  25.3 50.8 %all-gather.3.cloned.1.call-start = ((), (), s32[]{:S(2)}) async-start(), calls=%async_computation.2 | async-start | bytes 2949120 | tf_op jit(solution)/shard_map/all_gather | solution.py:229
  26.1 170.2 %reduce-scatter.5.cloned.1.call-start = ((), (), s32[]{:S(2)}) async-start(), calls=%async_computation.5 | async-start | bytes 2949120 | tf_op jit(solution)/shard_map/reduce_scatter | solution.py:286
  26.4 1.4 collective-permute-start.4
  27.6 70.6 %copy-start.58 = (f32[3,384]{1,0:T(4,128)}, f32[3,384]{1,0:T(4,128)S(1)}, u32[]{:S(2)}) copy-start(f32[3,384]{1,0:T(4,128)S(1)} %get-tuple-element.111) | copy-start | bytes 13828
  27.9 3.7 collective-permute-start.5
  28.5 68.1 %copy-start.88 = (bf16[3]{0:T(256)(128)(2,1)}, bf16[3]{0:T(256)(128)(2,1)S(1)}, u32[]{:S(2)}) copy-start(bf16[3]{0:T(256)(128)(2,1)S(1)} %get-tuple-element.117) | copy-start | bytes 22
  28.5 71.2 %copy-start.76 = (f32[1536]{0:T(1024)}, f32[1536]{0:T(1024)S(1)}, u32[]{:S(2)}) copy-start(f32[1536]{0:T(1024)S(1)} %convert_element_type.143) | copy-start | bytes 18436
  34.3 62.3 %copy-start.44 = (bf16[3,256,16]{1,2,0:T(8,128)(2,1)}, bf16[3,256,16]{1,2,0:T(8,128)(2,1)S(1)}, u32[]{:S(2)}) copy-start(bf16[3,256,16]{1,2,0:T(8,128)(2,1)S(1)} %reshape.226) | copy-start | bytes 73732
  35.7 18.5 %copy-start.12 = (bf16[3,256,384]{1,2,0:T(8,128)(2,1)}, bf16[3,256,384]{1,2,0:T(8,128)(2,1)S(1)}, u32[]{:S(2)}) copy-start(bf16[3,256,384]{1,2,0:T(8,128)(2,1)S(1)} %copy.124) | copy-start | bytes 1769476
  73.9 6.5 %copy-start.32 = (f32[3,6,256]{2,1,0:T(8,128)}, f32[3,6,256]{2,1,0:T(8,128)S(1)}, u32[]{:S(2)}) copy-start(f32[3,6,256]{2,1,0:T(8,128)S(1)} %log_add_fusion) | copy-start | bytes 55300
  80.4 9.4 %copy-start.3 = (f32[3,256,384]{2,1,0:T(8,128)S(1)}, f32[3,256,384]{2,1,0:T(8,128)}, u32[]{:S(2)}) copy-start(f32[3,256,384]{2,1,0:T(8,128)} %copy-done.2) | copy-start | bytes 3538948
  80.4 9.4 %copy-start.28 = (bf16[384,384]{1,0:T(8,128)(2,1)S(1)}, bf16[384,384]{1,0:T(8,128)(2,1)}, u32[]{:S(2)}) copy-start(bf16[384,384]{1,0:T(8,128)(2,1)} %param.35) | copy-start | bytes 884740
  94.1 5.6 copy-start.16
  99.7 4.6 copy-start.36
  127.5 69.5 %reduce-scatter.3.cloned.1.call-start = ((), (), s32[]{:S(2)}) async-start(), calls=%async_computation.4 | async-start | bytes 2949120 | tf_op jit(solution)/shard_map/reduce_scatter | solution.py:283
  127.6 14.0 %copy-start.33 = (f32[3,6,256]{2,1,0:T(8,128)S(1)}, f32[3,6,256]{2,1,0:T(8,128)}, u32[]{:S(2)}) copy-start(f32[3,6,256]{2,1,0:T(8,128)} %copy-done.32) | copy-start | bytes 55300
  141.6 13.5 %copy-start.13 = (bf16[3,256,384]{1,2,0:T(8,128)(2,1)S(1)}, bf16[3,256,384]{1,2,0:T(8,128)(2,1)}, u32[]{:S(2)}) copy-start(bf16[3,256,384]{1,2,0:T(8,128)(2,1)} %copy-done.12) | copy-start | bytes 1769476
  155.1 4.4 copy-start.1
  163.8 185.4 %all-reduce.5.cloned.1.call-start = ((), (), s32[]{:S(2)}) async-start(), calls=%async_computation.6 | async-start | bytes 168960 | tf_op jit(solution)/shard_map/psum | solution.py:311
  176.5 6.2 copy-start.11
  178.7 4.0 copy-start.15
  180.1 3.9 copy-start.51
  180.1 3.9 copy-start.52
  182.7 4.7 copy-start.24
  190.1 6.9 %copy-start.4 = (f32[3,256,384]{2,1,0:T(8,128)S(1)}, f32[3,256,384]{2,1,0:T(8,128)}, u32[]{:S(2)}) copy-start(f32[3,256,384]{2,1,0:T(8,128)} %copy-done.2) | copy-start | bytes 3538948
  190.1 6.9 %copy-start.20 = (bf16[3,256,384]{2,1,0:T(8,128)(2,1)S(1)}, bf16[3,256,384]{2,1,0:T(8,128)(2,1)}, u32[]{:S(2)}) copy-start(bf16[3,256,384]{2,1,0:T(8,128)(2,1)} %copy.135) | copy-start | bytes 1769476
  190.1 6.9 %copy-start.46 = (f32[3,256]{1,0:T(4,128)S(1)}, f32[3,256]{1,0:T(4,128)}, u32[]{:S(2)}) copy-start(f32[3,256]{1,0:T(4,128)} %copy-done.45) | copy-start | bytes 9220
  202.7 4.0 copy-start.68
  208.7 5.9 copy-start.34
  208.7 5.9 copy-start.35
  222.8 383.5 %all-reduce.7.cloned.1.call-start = ((), (), s32[]{:S(2)}) async-start(), calls=%async_computation.7 | async-start | bytes 27009024 | tf_op jit(solution)/shard_map/psum | solution.py:311
  231.8 4.7 copy-start.8
  231.8 4.7 copy-start.61
  231.8 4.3 collective-permute-start.2
  236.3 5.7 collective-permute-start.3
  241.4 5.7 collective-permute-start.6
  248.8 3.7 collective-permute-start.7
  611.7 4.2 copy-start.75
  611.7 4.8 copy-start.27
  (68 other events, 136.3 us)
Sparse Core Ops, SparseCore 0:
  25.4 24.3 all-gather.4
  52.0 24.0 all-gather.2
  127.6 33.0 reduce-scatter.4
  163.9 33.0 reduce-scatter.2
  222.9 126.2 all-reduce.4
  357.7 248.5 all-reduce.6
where the time goes:
time: 640 us; the launch traced here: 634 us
  waiting for transfers between devices  377 us (59%)
  matrix products  112 us (18%)
  local copies, waits for them, and re-layouts  78.9 us (12%)
  other arithmetic  44.1 us (7%)
  between operations  15.4 us (2%)
  starting transfers between devices  6.54 us (1%)
    psum x2, waiting for transfers between devices, local(): lax.psum((local_parts[0], local_parts[1], patch_weight_grad, patch_bias_g...  353 us
    unnamed x227, local copies, waits for them, and re-layouts  32 us
    dot_general x5, matrix products, outer(): jnp.einsum('spd,spe->de', value, grad, preferred_element_type=jnp.float32)  16.3 us
    all_gather x1, waiting for transfers between devices, local(): lax.all_gather(key, ('row', 'col'), axis=1, tiled=True)  14.2 us
    dot_general x1, matrix products, attend_back(): jnp.einsum('sqhd,skhd->shqk', grad_h, split_heads(values, heads), preferr...  14 us
    convert_element_type x1, other arithmetic, attend_back(): grad_s = (weights * (grad_w - inner)).astype(jnp.bfloat16)  13.5 us
  transfers between devices with their start and end apart: 14, of which 9 were waited for; matrix products, arithmetic and copies ran while one was open for 20% of the time, Pallas kernels for 0%

commit v1 on v0

v1 whole, which is shorter than its diff:
```python
import functools

import jax
import jax.numpy as jnp
import numpy as np
from jax import lax
from jax.experimental import pallas as pl
from jax.experimental.pallas import tpu as pltpu
from jax.sharding import PartitionSpec as P

F32 = jnp.float32
BF16 = jnp.bfloat16
HEADS = 6
LATENT = 64
MESH = pl.DeviceIdType.MESH
VMEM = pl.BlockSpec(memory_space=pltpu.VMEM)
SMEM = pl.BlockSpec(memory_space=pltpu.SMEM)
ROUNDS = 3


def nn(a, b):
    return lax.dot_general(a, b, (((1,), (0,)), ((), ())), preferred_element_type=F32)


def nt(a, b):
    return lax.dot_general(a, b, (((1,), (1,)), ((), ())), preferred_element_type=F32)


def tn(a, b):
    return lax.dot_general(a, b, (((0,), (0,)), ((), ())), preferred_element_type=F32)


def parts(v, many):
    out = []
    for _ in range(many):
        piece = v.astype(BF16)
        out.append(piece)
        v = v - piece.astype(F32)
    return out


def iota(shape, dim):
    return lax.broadcasted_iota(jnp.int32, shape, dim)


def flag(cond):
    return jnp.where(cond, 1.0, 0.0)


def swish(v):
    return v / (1.0 + jnp.exp(-v))


def position_tables(grid, width):
    quarter = width // 4
    omega = np.float32(1.0) / np.power(
        np.float32(10000.0), np.arange(quarter, dtype=np.float32) / np.float32(quarter)
    )
    angles = np.arange(grid, dtype=np.float32)[:, None] * omega[None, :].astype(np.float32)
    single = np.concatenate([np.sin(angles), np.cos(angles)], axis=1).astype(np.float32)
    blank = np.zeros_like(single)
    return np.concatenate([single, blank], axis=1), np.concatenate([blank, single], axis=1)


def plane_maps(slots, chans, side, halves):
    rows = slots * chans * side
    lanes = halves * halves
    spread = []
    keep = flag(iota((rows, lanes), 0) % side // 2 == iota((rows, lanes), 1) // halves)
    pick = []
    for j in range(2):
        col = iota((side, lanes), 0)
        spread.append(flag(col == iota((side, lanes), 1) % halves * 2 + j).astype(BF16))
        many = slots * chans * 4
        out, src = iota((many, rows), 0), iota((many, rows), 1)
        same = (out // 4 == src // side) & (out % 4 // 2 == src % 2) & (out % 2 == j)
        pick.append(flag(same).astype(BF16))
    return keep, spread, pick


def shift_masks(halves):
    row, lane = iota((16, halves * halves), 0), iota((16, halves * halves), 1)
    return row % 4 >= 2, row % 2 == 1, lane, halves


def shift_in(planes, masks):
    odd_row, odd_col, lane, side = masks
    full = side * side
    down = [
        jnp.where(
            odd_row,
            jnp.where(lane < side, pltpu.roll(planes[s ^ 2], side, 1), pltpu.roll(planes[s], side, 1)),
            planes[s],
        )
        for s in range(4)
    ]
    return [
        jnp.where(
            odd_col,
            jnp.where(
                lane % side == 0, pltpu.roll(down[s ^ 1], full - side + 1, 1), pltpu.roll(down[s], 1, 1)
            ),
            down[s],
        )
        for s in range(4)
    ]


def shift_out(planes, masks):
    odd_row, odd_col, lane, side = masks
    full = side * side
    up = [
        jnp.where(
            odd_row,
            jnp.where(
                lane >= full - side,
                pltpu.roll(planes[s ^ 2], full - side, 1),
                pltpu.roll(planes[s], full - side, 1),
            ),
            planes[s],
        )
        for s in range(4)
    ]
    return [
        jnp.where(
            odd_col,
            jnp.where(
                lane % side == side - 1, pltpu.roll(up[s ^ 1], side - 1, 1), pltpu.roll(up[s], full - 1, 1)
            ),
            up[s],
        )
        for s in range(4)
    ]


def mate(slot):
    row, col = lax.axis_index("row"), lax.axis_index("col")
    return {"row": row ^ (slot >> 1), "col": col ^ (slot & 1)}


def greet(devices):
    barrier = pltpu.get_barrier_semaphore()
    for device in devices:
        pl.semaphore_signal(barrier, inc=1, device_id=device, device_id_type=MESH)
    pl.semaphore_wait(barrier, len(devices))


def gather_kernel(lat_ref, cot_ref, out_ref, send_sem, recv_sem):
    slots, chans, side, _ = lat_ref.shape
    greet([mate(s) for s in (1, 2, 3)])
    keep, spread, pick = plane_maps(slots, chans, side, side // 2)
    for k, ref in enumerate((lat_ref, cot_ref)):
        tile = ref[...].reshape(slots * chans * side, side)
        total = None
        for j in range(2):
            wide = (nn(tile, spread[j]) * keep).astype(BF16)
            term = nn(pick[j], wide)
            total = term if total is None else total + term
        out_ref[0, k] = total.astype(BF16)
    copies = []
    for s in (1, 2, 3):
        copy = pltpu.make_async_remote_copy(
            src_ref=out_ref.at[0],
            dst_ref=out_ref.at[s],
            send_sem=send_sem.at[s - 1],
            recv_sem=recv_sem.at[s - 1],
            device_id=mate(s),
            device_id_type=MESH,
        )
        copy.start()
        copies.append(copy)
    for copy in copies:
        copy.wait()


def gather_planes(latents, cotangent):
    slots, chans, side, _ = latents.shape
    return pl.pallas_call(
        gather_kernel,
        out_shape=jax.ShapeDtypeStruct((4, 2, slots * chans * 4, side * side // 4), BF16),
        in_specs=[VMEM] * 2,
        out_specs=VMEM,
        scratch_shapes=[pltpu.SemaphoreType.DMA((3,)), pltpu.SemaphoreType.DMA((3,))],
        compiler_params=pltpu.CompilerParams(collective_id=0, has_side_effects=True),
        name="gather_planes",
    )(latents, cotangent)


def norm(v):
    share = 1.0 / v.shape[-1]
    centred = v - jnp.sum(v, axis=-1, keepdims=True) * share
    spread = jnp.sum(centred * centred, axis=-1, keepdims=True) * share
    inv = lax.rsqrt(spread + 1e-06)
    return centred * inv, inv


def norm_back(hat, inv, grad):
    share = 1.0 / hat.shape[-1]
    first = jnp.sum(grad, axis=-1, keepdims=True) * share
    second = jnp.sum(grad * hat, axis=-1, keepdims=True) * share
    return inv * (grad - first - hat * second)


def col_sum(v):
    return jnp.sum(v, axis=0, keepdims=True)


BIAS_PATCH, BIAS_QV, BIAS_PROJ, BIAS_FC1, BIAS_FC2, BIAS_ADA, BIAS_OUT = 0, 384, 1152, 1536, 3072, 3456, 6528
ROW_PATCH, ROW_OUT, ROW_PATCH_B, ROW_PROJ_B, ROW_FC2_B, ROW_Q_B, ROW_V_B, ROW_FC1_B, ROW_OUT_B = (
    0, 16, 32, 33, 34, 35, 36, 37, 41,
)
SMALL_ROWS = 48
MOD_ROWS = 32


def step_kernel(
    time_ref, class_ref, live_ref, planes_ref, bias_ref, pos_a_ref, pos_b_ref,
    time_table_ref, class_table_ref, patch_w_ref, ada_ref, fada_ref, qkv_ref, proj_ref, fc1_ref, fc2_ref, out_w_ref,
    grads_ref, small_ref, mod_out_ref, edge_ref,
    mod_s, pos_s, pt_s, gy_s, wp_s, wo_s, x1_s, hat_s, inv_s, k_s, v_s, q_s, e_s, s_s, linv_s, delta_s,
    of_s, ob_s, h_s, gp_s, du_s, dm_s, x2t_s, da_s, dx_s, dot_s, dom_s, dk_s, dv_s, dq_s, acc_s, dx1_s, edge_s,
):
    d = qkv_ref.shape[0]
    slots = x1_s.shape[0] // 4
    toks = x1_s.shape[1]
    pairs = HEADS // 2
    ff = fc1_ref.shape[1]
    blocks = ff // d
    half = 16
    live = [live_ref[i].astype(F32) for i in range(slots)]
    bins, classes = time_table_ref.shape[0], class_table_ref.shape[0]

    def onehot(ids_ref, many):
        row, lane = iota((16, many), 0), iota((16, many), 1)
        hit = jnp.zeros((16, many), F32)
        for i in range(slots):
            hit = hit + flag((row == i) & (lane == ids_ref[i]))
        return hit.astype(BF16)

    cond = nn(onehot(time_ref, bins), time_table_ref[...]) + nn(
        onehot(class_ref, classes), class_table_ref[...]
    )
    cond = cond[:8]
    act = parts(swish(cond), 3)
    act = jnp.concatenate([p.astype(F32) for p in act] + [jnp.zeros((8, d), F32)], axis=0).astype(BF16)
    for p in range(8):
        w = ada_ref[:, p * d : (p + 1) * d] if p < 6 else fada_ref[:, (p - 6) * d : (p - 5) * d]
        m = nn(act, w)
        mod_s[p] = m[0:8] + m[8:16] + m[16:24] + bias_ref[:, BIAS_ADA + p * d : BIAS_ADA + (p + 1) * d]

    small_ref[...] = jnp.zeros_like(small_ref)
    row, lane = iota((8, d), 0), iota((8, d), 1)
    ids = jnp.zeros((8, d), F32)
    for i in range(slots):
        ids = ids + jnp.where((row == 3) & (lane == i), 0.25 * time_ref[i].astype(F32), 0.0)
        ids = ids + jnp.where((row == 3) & (lane == slots + i), 0.25 * class_ref[i].astype(F32), 0.0)
    mod_out_ref[24:32, :] = jnp.where(row < 3, 0.25 * cond, 0.0) + ids

    swap = flag(iota((16, 16), 0) == (iota((16, 16), 1) ^ 3)).astype(BF16)
    wp_s[...] = nn(swap, patch_w_ref[...]).astype(BF16)
    wo_s[...] = nt(swap, out_w_ref[...]).astype(BF16)
    out_bias = bias_ref[:, BIAS_OUT : BIAS_OUT + 128]
    pick = flag(iota((16, 128), 1) == (iota((16, 128), 0) ^ 3))
    out_bias = jnp.sum(pick * out_bias, axis=1, keepdims=True)

    my_row, my_col = lax.axis_index("row"), lax.axis_index("col")
    for s in range(4):
        ta = pos_a_ref[pl.ds(pl.multiple_of((my_row ^ (s >> 1)) * half, half), half), :]
        tb = pos_b_ref[pl.ds(pl.multiple_of((my_col ^ (s & 1)) * half, half), half), :]
        tb = tb + bias_ref[:, BIAS_PATCH : BIAS_PATCH + d]
        for a in range(half):
            pos_s[s, a * half : (a + 1) * half, :] = ta[a : a + 1, :] + tb

    masks = shift_masks(half)
    for i in range(slots):
        lat = shift_in([planes_ref[s, 0, i * 16 : (i + 1) * 16, :].astype(F32) for s in range(4)], masks)
        cot = shift_in([planes_ref[s, 1, i * 16 : (i + 1) * 16, :].astype(F32) for s in range(4)], masks)
        for s in range(4):
            pt_s[i * 4 + s] = lat[s].astype(BF16)
        gy_s[i] = (cot[0] * live[i]).astype(BF16)

    def tokens(t, carry):
        img, slot = t // 4, t % 4
        tok = tn(pt_s[t], wp_s[...]) + pos_s[slot]
        hat, inv = norm(tok)
        hat_s[t] = hat
        inv_s[t] = inv
        x1 = (hat * (1.0 + mod_s[1, pl.ds(img, 1), :]) + mod_s[0, pl.ds(img, 1), :]).astype(BF16)
        x1_s[t] = x1
        keys = nn(x1, qkv_ref[:, d : 2 * d]).astype(BF16)
        vals = (nn(x1, qkv_ref[:, 2 * d :]) + bias_ref[:, BIAS_QV + d : BIAS_QV + 2 * d]).astype(BF16)
        for p in range(pairs):
            k_s[img * pairs + p, slot] = keys[:, p * 128 : (p + 1) * 128]
            v_s[img * pairs + p, slot] = vals[:, p * 128 : (p + 1) * 128]
        return carry

    lax.fori_loop(0, slots * 4, tokens, 0)

    lane128 = iota((1, 128), 1) // 64
    head_mask = [flag(lane128 == h) for h in range(2)]

    def image(img, carry):
        at = pl.ds(img, 1)
        query = nn(x1_s[img * 4], qkv_ref[:, :d]) + bias_ref[:, BIAS_QV : BIAS_QV + d]
        query = query.astype(BF16).astype(F32) * 0.125
        for p in range(pairs):
            for h in range(2):
                q_s[img * HEADS + p * 2 + h] = (query[:, p * 128 : (p + 1) * 128] * head_mask[h]).astype(BF16)

        def attend(p, inner):
            idx = img * pairs + p
            for h in range(2):
                head = idx * 2 + h
                top = None
                for c in range(4):
                    s = nt(k_s[idx, c], q_s[head])
                    s_s[c] = s
                    m = jnp.max(s, axis=0, keepdims=True)
                    top = m if top is None else jnp.maximum(top, m)
                total, acc = None, None
                for c in range(4):
                    e = jnp.exp(s_s[c] - top)
                    l = col_sum(e)
                    total = l if total is None else total + l
                    eb = e.astype(BF16)
                    e_s[head, c] = eb
                    o = tn(v_s[idx, c], eb)[h * 64 : (h + 1) * 64]
                    acc = o if acc is None else acc + o
                linv = 1.0 / total
                linv_s[head] = linv
                of_s[img, pl.ds(pl.multiple_of(p * 128 + h * 64, 64), 64), :] = acc * linv
            return inner

        lax.fori_loop(0, pairs, attend, 0)

        def mod_row(p):
            return mod_s[p, at, :]

        ot = of_s[img].astype(BF16)
        ob_s[img] = ot
        branch = tn(ot, proj_ref[...]) + bias_ref[:, BIAS_PROJ : BIAS_PROJ + d]
        tok = tn(pt_s[img * 4], wp_s[...]) + pos_s[0]
        g1 = mod_row(2)
        resid = tok + g1 * branch
        hat2, inv2 = norm(resid)
        x2 = (hat2 * (1.0 + mod_row(4)) + mod_row(3)).astype(BF16)
        x2t_s[img] = x2.T
        mlp = jnp.zeros((toks, d), F32)
        k0, k1 = 0.7978845608028654, 0.044715
        for b in range(blocks):
            at_b = slice(b * d, (b + 1) * d)
            u = nn(x2, fc1_ref[:, at_b]) + bias_ref[:, BIAS_FC1 + b * d : BIAS_FC1 + (b + 1) * d]
            sq = u * u
            t = jnp.tanh(k0 * u * (1.0 + k1 * sq))
            cdf = 0.5 * (1.0 + t)
            hidden = (u * cdf).astype(BF16)
            h_s[img, :, at_b] = hidden
            gp_s[:, at_b] = cdf + (0.5 * k0) * u * (1.0 - t * t) * (1.0 + (3.0 * k1) * sq)
            mlp = mlp + nn(hidden, fc2_ref[at_b, :])
        mlp = mlp + bias_ref[:, BIAS_FC2 : BIAS_FC2 + d]
        g2 = mod_row(5)
        x3 = resid + g2 * mlp
        hatf, invf = norm(x3)
        scf = 1.0 + mod_row(7)
        xf = (hatf * scf + mod_row(6)).astype(BF16)
        live_i = live_ref[img].astype(F32)
        edge_s[4, img] = (nt(wo_s[...], xf) + out_bias) * live_i
        gy = gy_s[img]
        small_ref[ROW_OUT : ROW_OUT + 16, :] += nn(gy, xf)
        ones = jnp.ones((8, toks), BF16)
        small_ref[ROW_OUT_B : ROW_OUT_B + 1, 0:16] += nt(ones, gy)[0:1]
        dxf = tn(gy, wo_s[...])

        def put_mod(p, v):
            mod_out_ref[pl.ds(p * slots + img, 1), :] = v

        put_mod(6, col_sum(dxf))
        put_mod(7, col_sum(dxf * hatf))
        dx3 = norm_back(hatf, invf, dxf * scf)
        dm = (g2 * dx3).astype(BF16)
        dm_s[img] = dm
        put_mod(5, col_sum(mlp * dx3))
        small_ref[ROW_FC2_B : ROW_FC2_B + 1, :] += col_sum(dm.astype(F32))
        dx2 = jnp.zeros((toks, d), F32)
        for b in range(blocks):
            at_b = slice(b * d, (b + 1) * d)
            du = (nt(dm, fc2_ref[at_b, :]) * gp_s[:, at_b]).astype(BF16)
            du_s[img, :, at_b] = du
            small_ref[ROW_FC1_B + b : ROW_FC1_B + b + 1, :] += col_sum(du.astype(F32))
            dx2 = dx2 + nt(du, fc1_ref[:, at_b])
        put_mod(3, col_sum(dx2))
        put_mod(4, col_sum(dx2 * hat2))
        dx = dx3 + norm_back(hat2, inv2, dx2 * (1.0 + mod_row(4)))
        dx_s[img] = dx
        put_mod(2, col_sum(branch * dx))
        da = (g1 * dx).astype(BF16)
        da_s[img] = da
        small_ref[ROW_PROJ_B : ROW_PROJ_B + 1, :] += col_sum(da.astype(F32))
        dot = nt(proj_ref[...], da)
        blank = jnp.zeros((64, toks), F32)
        for hd in range(HEADS):
            head = img * HEADS + hd
            piece = dot[hd * 64 : (hd + 1) * 64]
            linv = linv_s[head]
            delta_s[head] = col_sum(piece * of_s[img, hd * 64 : (hd + 1) * 64, :]) * linv
            piece = piece * linv
            wide = jnp.concatenate([piece, blank] if hd % 2 == 0 else [blank, piece], axis=0).astype(BF16)
            dot_s[head] = wide
            dom_s[head] = wide.T
        return carry

    lax.fori_loop(0, slots, image, 0)

    for b in range(blocks):
        at_b = slice(b * d, (b + 1) * d)
        total = None
        for img in range(slots):
            term = tn(h_s[img, :, at_b], dm_s[img])
            total = term if total is None else total + term
        grads_ref[b * d : (b + 1) * d, :] = total.astype(BF16)
        total = None
        for img in range(slots):
            term = nn(x2t_s[img], du_s[img, :, at_b])
            total = term if total is None else total + term
        grads_ref[ff + b * d : ff + (b + 1) * d, :] = total.astype(BF16)
    total = None
    for img in range(slots):
        term = nn(ob_s[img], da_s[img])
        total = term if total is None else total + term
    grads_ref[2 * ff : 2 * ff + d, :] = total.astype(BF16)

    def attend_back(idx, carry):
        dqt = [None, None]
        for c in range(4):
            dk, dv = None, None
            kt = k_s[idx, c].T
            for h in range(2):
                head = idx * 2 + h
                e = e_s[head, c]
                dp = nn(v_s[idx, c], dot_s[head])
                ds = (e.astype(F32) * (dp - delta_s[head])).astype(BF16)
                dk_h, dv_h = nn(ds, q_s[head]), nn(e, dom_s[head])
                dk = dk_h if dk is None else dk + dk_h
                dv = dv_h if dv is None else dv + dv_h
                dq_h = nn(kt[h * 64 : (h + 1) * 64], ds)
                dqt[h] = dq_h if dqt[h] is None else dqt[h] + dq_h
            dk_s[idx, c] = dk.astype(BF16)
            dv_s[idx, c] = dv.astype(BF16)
        dq_s[idx] = (jnp.concatenate(dqt, axis=0) * 0.125).T.astype(BF16)
        return carry

    lax.fori_loop(0, slots * pairs, attend_back, 0)

    acc_s[...] = jnp.zeros_like(acc_s)
    for p in (0, 1):
        mod_out_ref[p * slots : (p + 1) * slots, :] = jnp.zeros((slots, d), F32)

    def tokens_back(t, carry):
        img, slot = t // 4, t % 4

        def joined(ref):
            return jnp.concatenate([ref[img * pairs + p, slot] for p in range(pairs)], axis=1)

        dk, dv = joined(dk_s), joined(dv_s)
        x1t = x1_s[t].T
        acc_s[1] += nn(x1t, dk)
        acc_s[2] += nn(x1t, dv)
        small_ref[ROW_V_B : ROW_V_B + 1, :] += col_sum(dv.astype(F32))
        dx1_s[...] = nt(dk, qkv_ref[:, d : 2 * d]) + nt(dv, qkv_ref[:, 2 * d :])

        @pl.when(slot == 0)
        def _():
            dq = jnp.concatenate([dq_s[img * pairs + p] for p in range(pairs)], axis=1)
            acc_s[0] += nn(x1t, dq)
            small_ref[ROW_Q_B : ROW_Q_B + 1, :] += col_sum(dq.astype(F32))
            dx1_s[...] += nt(dq, qkv_ref[:, :d])

        dx1 = dx1_s[...]
        hat = hat_s[t]
        mod_out_ref[pl.ds(img, 1), :] += col_sum(dx1)
        mod_out_ref[pl.ds(slots + img, 1), :] += col_sum(dx1 * hat)
        dx1_s[...] = norm_back(hat, inv_s[t], dx1 * (1.0 + mod_s[1, pl.ds(img, 1), :]))

        @pl.when(slot == 0)
        def _():
            dx1_s[...] += dx_s[img]

        dtok = dx1_s[...]
        small_ref[ROW_PATCH_B : ROW_PATCH_B + 1, :] += col_sum(dtok)
        hi, lo = parts(dtok, 2)
        small_ref[ROW_PATCH : ROW_PATCH + 16, :] += nn(pt_s[t], hi) + nn(pt_s[t], lo)
        edge_s[slot, img] = nt(wp_s[...], hi) + nt(wp_s[...], lo)
        return carry

    lax.fori_loop(0, slots * 4, tokens_back, 0)
    for k in range(3):
        grads_ref[2 * ff + (k + 1) * d : 2 * ff + (k + 2) * d, :] = acc_s[k].astype(BF16)

    blank = jnp.zeros((16, toks), F32)
    for i in range(slots):
        lat = shift_out([edge_s[s, i] for s in range(4)], masks)
        out = shift_out([edge_s[4, i], blank, blank, blank], masks)
        for s in range(4):
            edge_ref[s, 0, i * 16 : (i + 1) * 16, :] = lat[s]
            edge_ref[s, 1, i * 16 : (i + 1) * 16, :] = out[s]


def step(time_bin, class_label, live, planes, bias, pos_a, pos_b, *weights):
    qkv_weight, fc1_weight = weights[5], weights[7]
    d, ff = qkv_weight.shape[0], fc1_weight.shape[1]
    slots, toks = time_bin.shape[0], planes.shape[-1]
    pairs = HEADS // 2
    heads = slots * HEADS
    out_shape = (
        jax.ShapeDtypeStruct((2 * ff + 4 * d, d), BF16),
        jax.ShapeDtypeStruct((SMALL_ROWS, d), F32),
        jax.ShapeDtypeStruct((MOD_ROWS, d), F32),
        jax.ShapeDtypeStruct((4,) + planes.shape[1:], F32),
    )
    scratch = [
        ((8, 8, d), F32), ((4, toks, d), F32), ((slots * 4, 16, toks), BF16), ((slots, 16, toks), BF16),
        ((16, d), BF16), ((16, d), BF16), ((slots * 4, toks, d), BF16), ((slots * 4, toks, d), F32),
        ((slots * 4, toks, 1), F32), ((slots * pairs, 4, toks, 128), BF16), ((slots * pairs, 4, toks, 128), BF16),
        ((heads, toks, 128), BF16), ((heads, 4, toks, toks), BF16), ((4, toks, toks), F32),
        ((heads, 1, toks), F32), ((heads, 1, toks), F32), ((slots, d, toks), F32), ((slots, d, toks), BF16),
        ((slots, toks, ff), BF16), ((toks, ff), F32), ((slots, toks, ff), BF16), ((slots, toks, d), BF16),
        ((slots, d, toks), BF16), ((slots, toks, d), BF16), ((slots, toks, d), F32), ((heads, 128, toks), BF16),
        ((heads, toks, 128), BF16), ((slots * pairs, 4, toks, 128), BF16), ((slots * pairs, 4, toks, 128), BF16),
        ((slots * pairs, toks, 128), BF16), ((3, d, d), F32), ((toks, d), F32), ((5, slots, 16, toks), F32),
    ]
    return pl.pallas_call(
        step_kernel,
        out_shape=out_shape,
        in_specs=[SMEM] * 3 + [VMEM] * (4 + len(weights)),
        out_specs=(VMEM,) * 4,
        scratch_shapes=[pltpu.VMEM(shape, kind) for shape, kind in scratch],
        compiler_params=pltpu.CompilerParams(vmem_limit_bytes=64 * 1024 * 1024 - 65536),
        name="step",
    )(time_bin, class_label, live, planes, bias, pos_a, pos_b, *weights)


def axes_of(images):
    bits = max(images.bit_length() - 1, 0)
    return ("col", 0), ("row", 0), [("img", k) for k in range(bits)]


def other(axis):
    name, bit = axis
    return {name: lax.axis_index(name) ^ (1 << bit)}


def side_of(axis):
    name, bit = axis
    return (lax.axis_index(name) >> bit) & 1


def orders(images):
    col, row, img = axes_of(images)
    first, rest = img[:ROUNDS], img[ROUNDS:]
    scatter = [
        [col, row] + first,
        [col] + first[:1] + [row] + first[1:],
        [col] + first[1:] + [row] + first[:1],
    ]
    return scatter, rest


def reduce_kernel(images, grads_ref, small_ref, mod_ref, edge_ref, grads_out, small_out, mod_out, edge_out, *scratch):
    scatter, rest = orders(images)
    groups = len(scatter)
    depth = len(scatter[0])
    turns = depth + len(rest)
    col, row, img_bits = axes_of(images)
    all_axes = [col, row] + img_bits
    recv = scratch[: turns]
    work = scratch[turns : 2 * turns]
    srecv, swork, erecv, send, got, gsend, ggot, ssend, sgot, msend, mgot, esend, egot = scratch[2 * turns :]
    greet([other(a) for a in all_axes] + [mate(3)])

    rows = grads_ref.shape[0] // groups
    live = []

    def copy(src, dst, s, r, device):
        c = pltpu.make_async_remote_copy(
            src_ref=src, dst_ref=dst, send_sem=s, recv_sem=r, device_id=device, device_id_type=MESH
        )
        c.start()
        live.append(c)
        return c

    planes = [copy(edge_ref.at[s], erecv.at[s - 1], esend.at[s - 1], egot.at[s - 1], mate(s)) for s in (1, 2, 3)]

    swork[0, : small_ref.shape[0], :] = small_ref[...]
    swork[0, small_ref.shape[0] :, :] = mod_ref[...]
    cut = small_ref.shape[0]

    flight = [None] * groups
    base = [g * rows for g in range(groups)]
    inside = [jnp.int32(0)] * groups

    def view(g, k, start, many):
        if k == 0:
            return grads_ref.at[pl.ds(pl.multiple_of(base[g] + start, 16), many), :]
        return work[k - 1].at[g, pl.ds(pl.multiple_of(start, 16), many), :]

    def start_round(g, k):
        axis = (scatter[g] + rest)[k]
        if k < depth:
            many = rows >> (k + 1)
            src = view(g, k, (1 - side_of(axis)) * many, many)
        else:
            many = rows >> depth
            src = view(g, k, 0, many)
        flight[g] = copy(src, recv[k].at[g], send.at[g, k], got.at[g, k], other(axis))

    def end_round(g, k):
        axis = (scatter[g] + rest)[k]
        flight[g].wait_recv()
        if k < depth:
            many = rows >> (k + 1)
            start = side_of(axis) * many
            inside[g] = inside[g] + start
        else:
            many, start = rows >> depth, 0
        mine = view(g, k, start, many)[...]
        work[k][g] = (mine.astype(F32) + recv[k][g].astype(F32)).astype(BF16)

    small = [None]

    def start_small(k):
        axis = all_axes[k]
        if k < 2:
            small[0] = [copy(swork.at[k], srecv.at[k], ssend.at[k], sgot.at[k], other(axis))]
        else:
            b = 1 << axis[1]
            start = lax.axis_index("img") // b * b
            at = mod_out.at[pl.ds(start, b)]
            small[0] = [
                copy(swork.at[k, 0:cut], srecv.at[k, 0:cut], ssend.at[k], sgot.at[k], other(axis)),
                copy(at, at, msend.at[k], mgot.at[k], other(axis)),
            ]

    def end_small(k):
        small[0][0].wait_recv()
        if k < 2:
            swork[k + 1] = swork[k] + srecv[k]
            if k == 1:
                mod_out[pl.ds(lax.axis_index("img"), 1)] = swork[k + 1, cut:, :][None]
        else:
            small[0][1].wait_recv()
            swork[k + 1, 0:cut] = swork[k, 0:cut] + srecv[k, 0:cut]

    for k in range(max(turns, len(all_axes))):
        for g in range(groups):
            if 0 < k <= turns:
                end_round(g, k - 1)
            if k < turns:
                start_round(g, k)
        if 0 < k <= len(all_axes):
            end_small(k - 1)
        if k < len(all_axes):
            start_small(k)
    for g in range(groups):
        end_round(g, turns - 1)

    piece = rows >> depth
    offset = list(inside)
    for g in range(groups):
        at = pl.ds(pl.multiple_of(base[g] + offset[g], 16), piece)
        grads_out[at, :] = work[turns - 1][g]
    for k in range(depth):
        for g in range(groups):
            axis = scatter[g][depth - 1 - k]
            many = piece << k
            if k > 0:
                flight[g].wait_recv()
                offset[g] = offset[g] - side_of(scatter[g][depth - k]) * (many // 2)
            at = grads_out.at[pl.ds(pl.multiple_of(base[g] + offset[g], 16), many), :]
            flight[g] = copy(at, at, gsend.at[g, k], ggot.at[g, k], other(axis))
    end_small(len(all_axes) - 1)
    small_out[...] = swork[len(all_axes), 0:cut]
    for c in planes:
        c.wait_recv()
    edge_out[...] = (edge_ref[0] + erecv[1]) + (erecv[0] + erecv[2])
    for g in range(groups):
        flight[g].wait_recv()
    for c in live:
        c.wait_send()


def reduce_all(images, grads, small, mod, edge):
    scatter, rest = orders(images)
    groups, depth = len(scatter), len(scatter[0])
    turns = depth + len(rest)
    steps = 2 + len(axes_of(images)[2])
    d = grads.shape[1]
    rows = grads.shape[0] // groups
    lens = [rows >> (k + 1) for k in range(depth)] + [rows >> depth] * len(rest)
    pieces = [pltpu.VMEM((groups, n, d), BF16) for n in lens]
    dma = pltpu.SemaphoreType.DMA
    both = small.shape[0] + mod.shape[0]
    return pl.pallas_call(
        functools.partial(reduce_kernel, images),
        out_shape=(
            jax.ShapeDtypeStruct(grads.shape, BF16),
            jax.ShapeDtypeStruct(small.shape, F32),
            jax.ShapeDtypeStruct((images,) + mod.shape, F32),
            jax.ShapeDtypeStruct(edge.shape[1:], F32),
        ),
        in_specs=[VMEM] * 4,
        out_specs=(VMEM,) * 4,
        scratch_shapes=pieces
        + pieces
        + [
            pltpu.VMEM((steps, both, d), F32),
            pltpu.VMEM((steps + 1, both, d), F32),
            pltpu.VMEM((3,) + edge.shape[1:], F32),
            dma((groups, turns)),
            dma((groups, turns)),
            dma((groups, depth)),
            dma((groups, depth)),
            dma((steps,)),
            dma((steps,)),
            dma((steps,)),
            dma((steps,)),
            dma((3,)),
            dma((3,)),
        ],
        compiler_params=pltpu.CompilerParams(
            collective_id=1, has_side_effects=True, vmem_limit_bytes=56 * 1024 * 1024
        ),
        name="reduce_all",
    )(grads, small, mod, edge)


def finish_kernel(
    bins, classes, grads_ref, small_ref, mod_ref, edge_ref, ada_ref, fada_ref,
    out_ref, lat_ref, time_ref, class_ref, patch_ref, ada_g_ref, qkv_g_ref, proj_g_ref, fc1_g_ref, fc2_g_ref, fada_g_ref,
    out_g_ref, bias_ref,
):
    d = ada_ref.shape[0]
    ff = fc1_g_ref.shape[1]
    slots, chans, side, _ = lat_ref.shape
    groups = mod_ref.shape[0]
    images = groups * slots
    held = -(-images // 32) * 32

    fc2_g_ref[...] = grads_ref[0:ff, :].astype(F32)
    for b in range(ff // d):
        fc1_g_ref[:, b * d : (b + 1) * d] = grads_ref[ff + b * d : ff + (b + 1) * d, :].astype(F32)
    proj_g_ref[...] = grads_ref[2 * ff : 2 * ff + d, :].astype(F32)
    for k in range(3):
        qkv_g_ref[:, k * d : (k + 1) * d] = grads_ref[2 * ff + (k + 1) * d : 2 * ff + (k + 2) * d, :].astype(F32)

    swap = flag(iota((16, 16), 0) == (iota((16, 16), 1) ^ 3)).astype(BF16)
    total = None
    for p in parts(small_ref[ROW_PATCH : ROW_PATCH + 16, :], 3):
        term = nn(swap, p)
        total = term if total is None else total + term
    patch_ref[...] = total
    total = None
    for p in parts(small_ref[ROW_OUT : ROW_OUT + 16, :], 3):
        term = tn(p, swap)
        total = term if total is None else total + term
    out_g_ref[...] = total
    for row, at in (
        (ROW_PATCH_B, BIAS_PATCH), (ROW_Q_B, BIAS_QV), (ROW_V_B, BIAS_QV + d), (ROW_PROJ_B, BIAS_PROJ),
        (ROW_FC1_B, BIAS_FC1), (ROW_FC1_B + 1, BIAS_FC1 + d), (ROW_FC1_B + 2, BIAS_FC1 + 2 * d),
        (ROW_FC1_B + 3, BIAS_FC1 + 3 * d), (ROW_FC2_B, BIAS_FC2),
    ):
        bias_ref[:, at : at + d] = small_ref[row : row + 1, :]
    total = None
    spot = flag(iota((128, 16), 0) == (iota((128, 16), 1) ^ 3)).astype(BF16)
    tail = jnp.broadcast_to(small_ref[ROW_OUT_B : ROW_OUT_B + 1, 0:128], (8, 128))
    back = flag((iota((128, 128), 0) == (iota((128, 128), 1) ^ 3)) & (iota((128, 128), 1) < 16)).astype(BF16)
    for p in parts(tail, 3):
        term = nn(p, back)
        total = term if total is None else total + term
    bias_ref[:, BIAS_OUT : BIAS_OUT + 128] = total[0:1]

    everything = mod_ref[...].reshape(groups * MOD_ROWS, d)
    pieces = parts(everything, 3)
    out_row, src = iota((held, groups * MOD_ROWS), 0), iota((held, groups * MOD_ROWS), 1)

    def of(p):
        sel = flag(
            (out_row < images) & (src // MOD_ROWS == out_row // slots) & (src % MOD_ROWS == p * slots + out_row % slots)
        ).astype(BF16)
        return nn(sel, pieces[0]) + nn(sel, pieces[1]) + nn(sel, pieces[2])

    cond = of(8)
    sel = flag((out_row < images) & (src // MOD_ROWS == out_row // slots) & (src % MOD_ROWS == 9 * slots)).astype(BF16)
    ids = nn(sel, pieces[0]) + nn(sel, pieces[1]) + nn(sel, pieces[2])
    img_row, lane = iota((held, d), 0), iota((held, d), 1)
    time_id = jnp.sum(jnp.where(lane == img_row % slots, ids, 0.0), axis=1, keepdims=True)
    class_id = jnp.sum(jnp.where(lane == slots + img_row % slots, ids, 0.0), axis=1, keepdims=True)

    act = swish(cond)
    a1, a2, a3 = parts(act, 3)
    left = jnp.concatenate([a1, a1, a2, a2, a1, a3], axis=0).T
    dact = jnp.zeros((held, d), F32)
    for p in range(8):
        dmod = of(p)
        d1, d2, d3 = parts(dmod, 3)
        right = jnp.concatenate([d1, d2, d1, d2, d3, d1], axis=0)
        grad = nn(left, right)
        if p < 6:
            ada_g_ref[:, p * d : (p + 1) * d] = grad
            w = ada_ref[:, p * d : (p + 1) * d]
        else:
            fada_g_ref[:, (p - 6) * d : (p - 5) * d] = grad
            w = fada_ref[:, (p - 6) * d : (p - 5) * d]
        bias_ref[:, BIAS_ADA + p * d : BIAS_ADA + (p + 1) * d] = col_sum(dmod)
        m = nt(jnp.concatenate([d1, d2, d3], axis=0), w)
        dact = dact + (m[0:held] + m[held : 2 * held] + m[2 * held :])
    sig = 1.0 / (1.0 + jnp.exp(-cond))
    dcond = dact * (sig * (1.0 + cond * (1.0 - sig)))
    stack = jnp.concatenate(parts(dcond, 3), axis=0)
    for ref, ids_col, many in ((time_ref, time_id, bins), (class_ref, class_id, classes)):
        wide = -(-many // 128) * 128
        at = iota((held, wide), 1).astype(F32)
        hit = flag((at == ids_col) & (iota((held, wide), 0) < images)).astype(BF16)
        hits = jnp.concatenate([hit, hit, hit], axis=0)
        ref[...] = tn(hits, stack)[:many]

    half = side // 2
    keep, spread, pick = plane_maps(slots, chans, side, half)
    for k, ref in ((0, lat_ref), (1, out_ref)):
        total = None
        splits = parts(edge_ref[k], 3 if k == 0 else 1)
        for piece in splits:
            for j in range(2):
                wide = (tn(pick[j], piece) * keep).astype(BF16)
                term = nt(wide, spread[j])
                total = term if total is None else total + term
        ref[...] = total.reshape(ref.shape).astype(ref.dtype)


def finish(bins, classes, latents, grads, small, mod, edge, ada_weight, fada_weight, ff):
    d = ada_weight.shape[0]
    f = lambda *shape: jax.ShapeDtypeStruct(shape, F32)
    out_shape = (
        jax.ShapeDtypeStruct(latents.shape, BF16), f(*latents.shape), f(bins, d), f(classes, d), f(16, d),
        f(d, 6 * d), f(d, 3 * d), f(d, d), f(d, ff), f(ff, d), f(d, 2 * d), f(d, 16), f(1, BIAS_OUT + 128),
    )
    return pl.pallas_call(
        functools.partial(finish_kernel, bins, classes),
        out_shape=out_shape,
        in_specs=[VMEM] * 6,
        out_specs=(VMEM,) * len(out_shape),
        compiler_params=pltpu.CompilerParams(vmem_limit_bytes=60 * 1024 * 1024),
        name="finish",
    )(grads, small, mod, edge, ada_weight, fada_weight)


def local(
    images, latents, time_bin, class_label, live, time_table, class_table, patch_weight, patch_bias, ada_weight, ada_bias,
    qkv_weight, qv_bias, proj_weight, proj_bias, fc1_weight, fc1_bias, fc2_weight, fc2_bias, final_ada_weight,
    final_ada_bias, out_weight, out_bias, cotangent,
):
    d, ff = qkv_weight.shape[0], fc1_weight.shape[1]
    bins, classes = time_table.shape[0], class_table.shape[0]
    bias = jnp.concatenate(
        [patch_bias, qv_bias, proj_bias, fc1_bias, fc2_bias, ada_bias, final_ada_bias, out_bias,
         jnp.zeros((128 - out_bias.shape[0],), BF16)]
    ).astype(F32)[None]
    pos_a, pos_b = position_tables(LATENT // 2, d)
    planes = gather_planes(latents, cotangent)
    grads, small, mod, edge = step(
        time_bin, class_label, live, planes, bias, jnp.asarray(pos_a), jnp.asarray(pos_b),
        time_table, class_table, patch_weight, ada_weight, final_ada_weight, qkv_weight, proj_weight, fc1_weight,
        fc2_weight, out_weight,
    )
    grads, small, mod, edge = reduce_all(images, grads, small, mod, edge)
    (out, lat_g, time_g, class_g, patch_g, ada_g, qkv_g, proj_g, fc1_g, fc2_g, fada_g, out_g, bias_g) = finish(
        bins, classes, latents, grads, small, mod, edge, ada_weight, final_ada_weight, ff
    )
    bias_g = bias_g[0]
    return (
        out, lat_g, time_g, class_g, patch_g, bias_g[BIAS_PATCH : BIAS_PATCH + d],
        ada_g, bias_g[BIAS_ADA : BIAS_ADA + 6 * d],
        qkv_g, bias_g[BIAS_QV : BIAS_QV + 2 * d],
        proj_g, bias_g[BIAS_PROJ : BIAS_PROJ + d],
        fc1_g, bias_g[BIAS_FC1 : BIAS_FC1 + ff],
        fc2_g, bias_g[BIAS_FC2 : BIAS_FC2 + d],
        fada_g, bias_g[BIAS_ADA + 6 * d : BIAS_ADA + 8 * d],
        out_g, bias_g[BIAS_OUT : BIAS_OUT + out_bias.shape[0]],
    )


def solution(mesh):
    tiles = P("img", None, "row", "col")
    return jax.shard_map(
        functools.partial(local, mesh.shape["img"]),
        mesh=mesh,
        in_specs=(tiles,) + (P("img"),) * 3 + (P(),) * 18 + (tiles,),
        out_specs=(tiles, tiles) + (P(),) * 18,
        check_vma=False,
    )
```

time: 640 us -> 188 us (0.29)
  waiting for transfers between devices: 377 us -> 0 us
  Pallas kernels: 0 us -> 170 us
  matrix products: 112 us -> 0 us
  local copies, waits for them, and re-layouts: 78.9 us -> 15 us
  other arithmetic: 44.1 us -> 0.64 us
  between operations: 15.4 us -> 0.69 us
  starting transfers between devices: 6.54 us -> 0 us
    psum x2 -> x0, waiting for transfers between devices: 353 us -> none  [local(): lax.psum((local_parts[0], local_parts[1], patch_weight_grad, patch_bias_g...]
    pallas_call x0 -> x4, Pallas kernels: none -> 170 us  [the longest x1 80.7 us: step(): pl.pallas_call(step_kernel, out_shape=out_shape, in_specs=[SMEM] * 3 + [V...]
    dot_general x34 -> x0, matrix products: 112 us -> none  [the longest x5 16.3 us: outer(): jnp.einsum('spd,spe->de', value, grad, preferred_element_type=jnp.float32)]
    unnamed x227 -> x2, local copies, waits for them, and re-layouts: 32 us -> 3.09 us
    reduce_sum x14 -> x0, other arithmetic: 24.6 us -> none  [the longest x1 9.84 us: attend(): jnp.sum(jnp.exp(scores - top), axis=-1, keepdims=True)]
    all_gather x2 -> x0, waiting for transfers between devices: 16.4 us -> none  [the longest x1 14.2 us: local(): lax.all_gather(key, ('row', 'col'), axis=1, tiled=True)]
    convert_element_type x9 -> x1, other arithmetic: 14.7 us -> 0.64 us  [local(): bias = jnp.concatenate([patch_bias, qv_bias, proj_bias, fc1_bias, fc2_bia...]
    convert_element_type x5 -> x0, local copies, waits for them, and re-layouts: 11.5 us -> none  [the longest x1 4.27 us: local(): grad_kall.astype(jnp.bfloat16)]
  transfers between devices with their start and end apart: 14 -> 0, of which waited for: 9 -> 0; matrix products, arithmetic and copies ran while one was open for 20% -> 0% of each run, Pallas kernels for 0% -> 0%
where the time goes in v1:
time: 188 us; the launch traced here: 187 us
  Pallas kernels  170 us (90%)
  local copies, waits for them, and re-layouts  15 us (8%)
    pallas_call x1, Pallas kernels, step(): pl.pallas_call(step_kernel, out_shape=out_shape, in_specs=[SMEM] * 3 + [V...  80.7 us
    pallas_call x1, Pallas kernels, reduce_all(): pl.pallas_call(functools.partial(reduce_kernel, images), out_shape=(jax.S...  69.1 us
    pallas_call x1, Pallas kernels, finish(): pl.pallas_call(functools.partial(finish_kernel, bins, classes), out_shape...  12.1 us
    pallas_call x1, Pallas kernels, gather_planes(): pl.pallas_call(gather_kernel, out_shape=jax.ShapeDtypeStruct((4, 2, slots...  8.6 us
    concatenate x8, local copies, waits for them, and re-layouts, local(): jnp.concatenate([patch_bias, qv_bias, proj_bias, fc1_bias, fc2_bias, ada_...  5.58 us

profile of v1, /device:TPU:0, one launch (start us, length us, event | category | flops | bytes accessed | tf_op | source)
XLA Modules:
  0.0 186.8 jit_solution(13349287527379308593)
XLA Ops:
  0.7 0.7 concatenate.26
  1.3 0.7 concatenate.28
  2.0 0.7 concatenate.30
  2.7 0.7 concatenate.27
  3.4 0.7 concatenate.32
  4.1 0.7 concatenate.29
  4.8 0.7 concatenate.31
  5.5 0.8 concatenate.34
  6.2 0.6 convert_element_type.10.bias_ref
  6.9 1.4 copy.45.out_w_ref
  8.3 8.6 %gather_planes.1.planes_ref = bf16[4,2,48,256]{3,2,1,0:T(8,128)(2,1)} custom-call(bf16[3,4,32,32]{3,2,1,0:T(8,128)(2,1)} %lat_ref.1, bf16[3,4,32,32]{3,2,1,0:T(8,128)(2,1)} %cot_ref.1), custom_call_target="tpu_custom_call" | custom-call | tf_op jit(solution)/shard_map/gather_planes/pallas_call | solution.py:178
  16.9 80.7 %step.1 = (bf16[4608,384]{1,0:T(8,128)(2,1)}, f32[48,384]{1,0:T(8,128)}, f32[32,384]{1,0:T(8,128)}, f32[4,2,48,256]{3,2,1,0:T(8,128)}) custom-call(s32[3]{0:T(128)} %time_ref.1, s32[3]{0:T(128)} %class_ref.1, s32[3]{0:T(128)} %live_ref.1, bf16[4,2,48,256]{3,2,1,0:T(8,128)(2,1)} %gather_planes.1.planes_ref, f32[1,6656]{1,0:T(1,128)} %convert_element_type.10.bias_ref, ...), custom_call_target="tpu_custom_call" | custom-call | tf_op jit(solution)/shard_map/step/pallas_call | solution.py:531
  97.6 69.1 %reduce_all.1 = (bf16[4608,384]{1,0:T(8,128)(2,1)}, f32[48,384]{1,0:T(8,128)}, f32[8,32,384]{2,1,0:T(8,128)}, f32[2,48,256]{2,1,0:T(8,128)}) custom-call(bf16[4608,384]{1,0:T(8,128)(2,1)} %get-tuple-element.41.grads_ref, f32[48,384]{1,0:T(8,128)} %get-tuple-element.42.small_ref, f32[32,384]{1,0:T(8,128)} %get-tuple-element.43.mod_ref, ...), custom_call_target="tpu_custom_call" | custom-call | tf_op jit(solution)/shard_map/reduce_all/pallas_call | solution.py:702
  166.7 12.1 %finish.1 = (bf16[3,4,32,32]{3,2,1,0:T(8,128)(2,1)}, f32[3,4,32,32]{3,2,1,0:T(8,128)}, f32[100,384]{1,0:T(8,128)}, f32[1001,384]{1,0:T(8,128)}, f32[16,384]{1,0:...) custom-call(bf16[4608,384]{1,0:T(8,128)(2,1)} %get-tuple-element.45., ...), custom_call_target="tpu_custom_call" | custom-call | tf_op jit(solution)/shard_map/finish/pallas_call | solution.py:846
  178.8 1.1 slice_bitcast_fusion
  179.9 1.3 slice_reduce_fusion.4
  181.2 1.3 slice_reduce_fusion.1
  182.5 1.3 slice_reduce_fusion.2
  183.8 1.3 slice_reduce_fusion
  185.1 1.6 copy.46
  (1 shorter events, 0.0 us)

commit v2 on v1

v2 whole, which is shorter than its diff:
```python
import functools

import jax
import jax.numpy as jnp
import numpy as np
from jax import lax
from jax.experimental import pallas as pl
from jax.experimental.pallas import tpu as pltpu
from jax.sharding import PartitionSpec as P

F32 = jnp.float32
BF16 = jnp.bfloat16
HEADS = 6
LATENT = 64
MESH = pl.DeviceIdType.MESH
VMEM = pl.BlockSpec(memory_space=pltpu.VMEM)
SMEM = pl.BlockSpec(memory_space=pltpu.SMEM)
ANY = pl.BlockSpec(memory_space=pl.ANY)


def nn(a, b):
    return lax.dot_general(a, b, (((1,), (0,)), ((), ())), preferred_element_type=F32)


def nt(a, b):
    return lax.dot_general(a, b, (((1,), (1,)), ((), ())), preferred_element_type=F32)


def tn(a, b):
    return lax.dot_general(a, b, (((0,), (0,)), ((), ())), preferred_element_type=F32)


def parts(v, many):
    out = []
    for _ in range(many):
        piece = v.astype(BF16)
        out.append(piece)
        v = v - piece.astype(F32)
    return out


def iota(shape, dim):
    return lax.broadcasted_iota(jnp.int32, shape, dim)


def flag(cond):
    return jnp.where(cond, 1.0, 0.0)


def swish(v):
    return v / (1.0 + jnp.exp(-v))


def position_tables(grid, width):
    quarter = width // 4
    omega = np.float32(1.0) / np.power(
        np.float32(10000.0), np.arange(quarter, dtype=np.float32) / np.float32(quarter)
    )
    angles = np.arange(grid, dtype=np.float32)[:, None] * omega[None, :].astype(np.float32)
    single = np.concatenate([np.sin(angles), np.cos(angles)], axis=1).astype(np.float32)
    blank = np.zeros_like(single)
    return np.concatenate([single, blank], axis=1), np.concatenate([blank, single], axis=1)


def plane_maps(slots, chans, side, halves):
    rows = slots * chans * side
    lanes = halves * halves
    spread = []
    keep = flag(iota((rows, lanes), 0) % side // 2 == iota((rows, lanes), 1) // halves)
    pick = []
    for j in range(2):
        col = iota((side, lanes), 0)
        spread.append(flag(col == iota((side, lanes), 1) % halves * 2 + j).astype(BF16))
        many = slots * chans * 4
        out, src = iota((many, rows), 0), iota((many, rows), 1)
        same = (out // 4 == src // side) & (out % 4 // 2 == src % 2) & (out % 2 == j)
        pick.append(flag(same).astype(BF16))
    return keep, spread, pick


def shift_masks(halves):
    row, lane = iota((16, halves * halves), 0), iota((16, halves * halves), 1)
    return row % 4 >= 2, row % 2 == 1, lane, halves


def shift_in(planes, masks):
    odd_row, odd_col, lane, side = masks
    full = side * side
    down = [
        jnp.where(
            odd_row,
            jnp.where(lane < side, pltpu.roll(planes[s ^ 2], side, 1), pltpu.roll(planes[s], side, 1)),
            planes[s],
        )
        for s in range(4)
    ]
    return [
        jnp.where(
            odd_col,
            jnp.where(
                lane % side == 0, pltpu.roll(down[s ^ 1], full - side + 1, 1), pltpu.roll(down[s], 1, 1)
            ),
            down[s],
        )
        for s in range(4)
    ]


def shift_out(planes, masks):
    odd_row, odd_col, lane, side = masks
    full = side * side
    up = [
        jnp.where(
            odd_row,
            jnp.where(
                lane >= full - side,
                pltpu.roll(planes[s ^ 2], full - side, 1),
                pltpu.roll(planes[s], full - side, 1),
            ),
            planes[s],
        )
        for s in range(4)
    ]
    return [
        jnp.where(
            odd_col,
            jnp.where(
                lane % side == side - 1, pltpu.roll(up[s ^ 1], side - 1, 1), pltpu.roll(up[s], full - 1, 1)
            ),
            up[s],
        )
        for s in range(4)
    ]


def mate(slot):
    row, col = lax.axis_index("row"), lax.axis_index("col")
    return {"row": row ^ (slot >> 1), "col": col ^ (slot & 1)}


def greet(devices):
    barrier = pltpu.get_barrier_semaphore()
    for device in devices:
        pl.semaphore_signal(barrier, inc=1, device_id=device, device_id_type=MESH)
    pl.semaphore_wait(barrier, len(devices))


def norm(v):
    share = 1.0 / v.shape[-1]
    centred = v - jnp.sum(v, axis=-1, keepdims=True) * share
    spread = jnp.sum(centred * centred, axis=-1, keepdims=True) * share
    inv = lax.rsqrt(spread + 1e-06)
    return centred * inv, inv


def norm_back(hat, inv, grad):
    share = 1.0 / hat.shape[-1]
    first = jnp.sum(grad, axis=-1, keepdims=True) * share
    second = jnp.sum(grad * hat, axis=-1, keepdims=True) * share
    return inv * (grad - first - hat * second)


def col_sum(v):
    return jnp.sum(v, axis=0, keepdims=True)


E_OUT, E_PROJ_B, E_FC2_B, E_Q_B, E_V_B, E_FC1_B, E_OUT_B, E_MOD, E_COND, E_IDS, E_ROWS = 0, 16, 17, 18, 19, 20, 24, 32, 50, 56, 64
L_PATCH, L_PATCH_B, L_MOD, L_ROWS = 0, 16, 18, 32


def tree(terms):
    while len(terms) > 1:
        terms = [terms[i] + terms[i + 1] for i in range(0, len(terms), 2)]
    return terms[0]


class Copies:
    def __init__(self, send_sem, recv_sem):
        self.send_sem, self.recv_sem, self.known = send_sem, recv_sem, {}

    def make(self, key, src, dst, device):
        at = self.known.setdefault(key, len(self.known))
        return pltpu.make_async_remote_copy(
            src_ref=src, dst_ref=dst, send_sem=self.send_sem.at[at], recv_sem=self.recv_sem.at[at],
            device_id=device, device_id_type=MESH,
        )


class Stage:
    def __init__(self, copies, reduce=None):
        self.copies, self.reduce = copies, reduce

    def start(self):
        for c in self.copies():
            c.start()

    def finish(self):
        for c in self.copies():
            c.wait_recv()
        if self.reduce is not None:
            self.reduce()

    def drain(self):
        for c in self.copies():
            c.wait_send()


def far(distance):
    return {"img": lax.axis_index("img") ^ distance}


def rows_at(start, many):
    return pl.ds(pl.multiple_of(start, 16), many)


def ways(images, plan):
    bits = images.bit_length() - 1
    return [way for way in plan if isinstance(way, str) or way[0] + way[1] <= bits]


def shared_bits(images, plan):
    return max([way[0] + way[1] for way in ways(images, plan) if not isinstance(way, str)] + [0])


def members(way):
    return {"col": 2, "row": 2, "four": 4}[way] if isinstance(way, str) else 1 << way[1]


def position(way):
    row, col = lax.axis_index("row"), lax.axis_index("col")
    if isinstance(way, str):
        return {"col": col, "row": row, "four": col * 2 + row}[way]
    return (lax.axis_index("img") >> way[0]) & ((1 << way[1]) - 1)


def partner(way, delta):
    row, col = lax.axis_index("row"), lax.axis_index("col")
    if way == "col":
        return {"col": 1 - col}
    if way == "row":
        return {"row": 1 - row}
    if way == "four":
        return {"row": row ^ (delta & 1), "col": col ^ (delta >> 1)}
    return far(delta << way[0])


def group_shapes(images, rows, plan):
    d, shapes = 384, []
    for way in ways(images, plan):
        many = members(way)
        rows //= many
        shapes += [(many - 1, rows, d), (rows, d)]
    high = images >> shared_bits(images, plan)
    if high > 1:
        shapes += [(high - 1, rows, d), (rows, d)]
    return shapes


def group_copies(images, plan):
    return 2 * sum(members(way) - 1 for way in ways(images, plan)) + (images >> shared_bits(images, plan)) - 1


def group_stages(name, images, base, rows, plan, grads, out, bufs, net):
    bufs = list(bufs)
    known = ways(images, plan)
    shared = shared_bits(images, plan)
    high = images >> shared

    def add(*refs):
        return tree([r.astype(F32) for r in refs]).astype(BF16)

    def scatter(k, way, held, many, got, total, last):
        count = members(way)

        def copies():
            return [
                net.make(f"{name}s{k}.{e}", held((position(way) ^ e) * many, many), got.at[e - 1], partner(way, e))
                for e in range(1, count)
            ]

        def reduce():
            total[...] = add(held(position(way) * many, many)[...], *[got[e] for e in range(count - 1)])
            if last:
                out[rows_at(base + start(len(known)), many), :] = total[...]

        return Stage(copies, reduce)

    sizes = [rows]
    for way in known:
        sizes.append(sizes[-1] // members(way))

    def start(level):
        total = 0
        for k in range(level):
            total = total + position(known[k]) * sizes[k + 1]
        return total

    stages = []

    def held(at, many):
        return grads.at[rows_at(base + at, many), :]

    for k, way in enumerate(known):
        got, total = bufs[:2]
        del bufs[:2]
        stages.append(scatter(k, way, held, sizes[k + 1], got, total, high == 1 and k == len(known) - 1))

        def held(at, many, total=total):
            return total.at[rows_at(at, many), :]

    if high > 1:
        got, final = bufs[:2]
        summed, many = total, sizes[-1]

        def copies():
            return [net.make(f"{name}h{e}", summed, got.at[e - 1], far(e << shared)) for e in range(1, high)]

        def reduce():
            final[...] = add(summed[...], *[got[e] for e in range(high - 1)])
            out[rows_at(base + start(len(known)), many), :] = final[...]

        stages.append(Stage(copies, reduce))

    def gather(k, way):
        def copies():
            at = out.at[rows_at(base + start(k + 1), sizes[k + 1]), :]
            return [net.make(f"{name}g{k}.{e}", at, at, partner(way, e)) for e in range(1, members(way))]

        return Stage(copies)

    for k in reversed(range(len(known))):
        stages.append(gather(k, known[k]))
    return stages


def sum_stages(name, images, block, got, total, out, net):
    def c0():
        return [net.make(name + "m" + str(s), block, got.at[s - 1], mate(s)) for s in (1, 2, 3)]

    def r0():
        t = tree([block[...], got[0], got[1], got[2]]).astype(BF16)
        total[...] = t
        out[lax.axis_index("img")] = t

    def c1():
        at = out.at[lax.axis_index("img")]
        return [net.make(name + "i" + str(d), total, at, far(d)) for d in range(1, images)]

    return [Stage(c0, r0), Stage(c1)]


def edge_stages(name, edge, got, out, k, net):
    def c0():
        return [net.make(name + str(s), edge.at[s], got.at[s - 1], mate(s)) for s in (1, 2, 3)]

    def r0():
        out[k] = tree([r.astype(F32) for r in (edge[0], got[1], got[0], got[2])])

    return [Stage(c0, r0)]


FF_PLANS = (("col", "row", (0, 2), (2, 1)), ("col", (0, 2), "row", (2, 1)))
PAIR_PLANS = (("col", "row", (0, 3)), ("col", (0, 2), "row", (2, 1)), ("four", (0, 3)))


def group_list(d, ff):
    base = 2 * ff
    out = [(0, ff, FF_PLANS[0]), (ff, ff, FF_PLANS[1])]
    for k in range(3):
        out.append((base + k * (d + d // 3), d + d // 3, PAIR_PLANS[k]))
    return out


def step_kernel(images, count, *refs):
    refs = list(refs)

    def take(n):
        out = refs[:n]
        del refs[:n]
        return out

    (time_ref, class_ref, live_ref, lat_ref, cot_ref, patch_b_ref, ada_b_ref, qv_b_ref, proj_b_ref, fc1_b_ref, fc2_b_ref,
     fada_b_ref, out_b_ref, pos_a_ref, pos_b_ref, patch_w_ref, out_wt_ref) = take(17)
    hbm = take(8)
    out_ref, early_out, late_out, planes_out = take(4)
    held = take(4)
    qkv_ref, proj_ref, fc1_ref, fc2_ref = held
    (planes_ref, mod_s, pt_s, gy_s, wp_s, wo_s, x1_s, x1t_s, hat_s, inv_s, k_s, v_s, q_s, e_s, sa_s, sb_s, top_s,
     linv_s, delta_s, of_s, a_s, b_s, dm_s, x2t_s, da_s, dx_s, edge_s,
     grads_ref, early_ref, late_ref, edge_y, edge_l, early_got, early_sum, late_got, late_sum, edge_y_got, edge_l_got) = take(38)
    load_sem, gather_send, gather_recv, send_sem, recv_sem = take(5)
    bufs = refs

    d = qkv_ref.shape[0]
    slots, chans, side, _ = lat_ref.shape
    toks = x1_s.shape[0]
    pairs = HEADS // 2
    ff = fc1_ref.shape[1]
    blocks = ff // d
    half = side // 2
    bins, classes = hbm[0].shape[0], hbm[1].shape[0]

    loads = [pltpu.make_async_copy(a, b, load_sem.at[4 + i]) for i, (a, b) in enumerate(zip(hbm[4:], held))]
    net = Copies(send_sem, recv_sem)
    groups = []
    for g, (base, rows, plan) in enumerate(group_list(d, ff)):
        n = len(group_shapes(images, rows, plan))
        groups.append(group_stages("g" + str(g), images, base, rows, plan, grads_ref, out_ref, bufs[:n], net))
        del bufs[:n]
    groups.append(sum_stages("e", images, early_ref, early_got, early_sum, early_out, net))
    groups.append(sum_stages("l", images, late_ref, late_got, late_sum, late_out, net))
    groups.append(edge_stages("y", edge_y, edge_y_got, planes_out, 1, net))
    groups.append(edge_stages("x", edge_l, edge_l_got, planes_out, 0, net))
    FC2, FC1, PAIR, EARLY, LATE, EDGE_Y, EDGE_L = 0, 1, 2, 5, 6, 7, 8

    def advance(g, k):
        if k > 0:
            groups[g][k - 1].finish()
        if k < len(groups[g]):
            groups[g][k].start()

    def row_of(ref, start, many):
        return ref[...].astype(F32).reshape(1, ref.shape[0])[:, start : start + many]

    early_ref[...] = jnp.zeros_like(early_ref)
    late_ref[...] = jnp.zeros_like(late_ref)

    swap = flag(iota((16, 16), 0) == (iota((16, 16), 1) ^ 3)).astype(BF16)
    wp_s[...] = nn(swap, patch_w_ref[...]).astype(BF16)
    wo_s[...] = nn(swap, out_wt_ref[...]).astype(BF16)
    out_bias = jnp.sum(
        flag(iota((16, 16), 1) == (iota((16, 16), 0) ^ 3)) * row_of(out_b_ref, 0, 16), axis=1, keepdims=True
    )

    inv_lane = iota((toks, 128), 1)

    def opening(time_table_ref, class_table_ref, ada_ref, fada_ref, pos_s):
        tables = [
            pltpu.make_async_copy(a, b, load_sem.at[i])
            for i, (a, b) in enumerate(zip(hbm[:4], (time_table_ref, class_table_ref, ada_ref, fada_ref)))
        ]
        for c in tables + loads:
            c.start()
        greet([mate(s) for s in (1, 2, 3)] + [far(k) for k in range(1, images)])
        keep, spread, pick = plane_maps(slots, chans, side, half)
        for k, ref in enumerate((lat_ref, cot_ref)):
            tile = ref[...].reshape(slots * chans * side, side)
            total = None
            for j in range(2):
                wide = (nn(tile, spread[j]) * keep).astype(BF16)
                term = nn(pick[j], wide)
                total = term if total is None else total + term
            planes_ref[0, k] = total.astype(BF16)
        gathers = []
        for s in (1, 2, 3):
            c = pltpu.make_async_remote_copy(
                src_ref=planes_ref.at[0], dst_ref=planes_ref.at[s], send_sem=gather_send.at[s - 1], recv_sem=gather_recv.at[s - 1],
                device_id=mate(s), device_id_type=MESH,
            )
            c.start()
            gathers.append(c)

        my_row, my_col = lax.axis_index("row"), lax.axis_index("col")
        patch_b = row_of(patch_b_ref, 0, d)
        for s in range(4):
            ta = pos_a_ref[pl.ds(pl.multiple_of((my_row ^ (s >> 1)) * half, half), half), :]
            tb = pos_b_ref[pl.ds(pl.multiple_of((my_col ^ (s & 1)) * half, half), half), :] + patch_b
            for a in range(half):
                pos_s[s, a * half : (a + 1) * half, :] = ta[a : a + 1, :] + tb

        def onehot(ids_ref, many):
            row, lane = iota((16, many), 0), iota((16, many), 1)
            hit = jnp.zeros((16, many), F32)
            for i in range(slots):
                hit = hit + flag((row == i) & (lane == ids_ref[i]))
            return hit.astype(BF16)

        for c in tables:
            c.wait()
        cond = nn(onehot(time_ref, bins), time_table_ref[...]) + nn(onehot(class_ref, classes), class_table_ref[...])
        cond = cond[:8]
        act = parts(swish(cond), 3)
        act = jnp.concatenate([p.astype(F32) for p in act] + [jnp.zeros((8, d), F32)], axis=0).astype(BF16)
        for p in range(8):
            w = ada_ref[:, p * d : (p + 1) * d] if p < 6 else fada_ref[:, (p - 6) * d : (p - 5) * d]
            m = nn(act, w)
            b = row_of(ada_b_ref, p * d, d) if p < 6 else row_of(fada_b_ref, (p - 6) * d, d)
            mod_s[p] = m[0:8] + m[8:16] + m[16:24] + b
        row, lane = iota((8, d), 0), iota((8, d), 1)
        ids = jnp.zeros((8, d), F32)
        for i in range(slots):
            for k, v in enumerate((time_ref[i], class_ref[i] // 256, class_ref[i] % 256)):
                ids = ids + jnp.where((row == 0) & (lane == k * slots + i), 0.25 * v.astype(F32), 0.0)
        high = cond.astype(BF16).astype(F32)
        early_ref[E_COND : E_COND + slots, :] = 0.25 * high[:slots]
        early_ref[E_COND + slots : E_COND + 2 * slots, :] = 0.25 * (cond - high)[:slots]
        early_ref[E_IDS : E_IDS + 1, :] = ids[0:1]

        for c in gathers:
            c.wait_recv()
        masks = shift_masks(half)
        live = [live_ref[i].astype(F32) for i in range(slots)]
        for i in range(slots):
            lat = shift_in([planes_ref[s, 0, i * 16 : (i + 1) * 16, :].astype(F32) for s in range(4)], masks)
            cot = shift_in([planes_ref[s, 1, i * 16 : (i + 1) * 16, :].astype(F32) for s in range(4)], masks)
            for s in range(4):
                pt_s[i * 4 + s] = lat[s].astype(BF16)
            gy_s[i] = (cot[0] * live[i]).astype(BF16)

        v_bias = row_of(qv_b_ref, d, d)

        def token_norm(t):
            img, slot = t // 4, t % 4
            tok = tn(pt_s[t], wp_s[...]) + pos_s[slot]
            dx_s[img] = tok
            hat, inv = norm(tok)
            hat_s[t] = hat
            inv_s[...] = jnp.where(inv_lane == t, inv, inv_s[...])
            x1_s[...] = (hat * (1.0 + mod_s[1, pl.ds(img, 1), :]) + mod_s[0, pl.ds(img, 1), :]).astype(BF16)

        token_norm(jnp.int32(3))
        loads[0].wait()

        def reverse(n):
            return n // 4 * 4 + 3 - n % 4

        def tokens(n, carry):
            t = reverse(n)
            img, slot = t // 4, t % 4
            x1 = x1_s[...]
            x1t_s[t] = x1.T
            keys = nn(x1, qkv_ref[:, d : 2 * d]).astype(BF16)
            vals = (nn(x1, qkv_ref[:, 2 * d :]) + v_bias).astype(BF16)
            for p in range(pairs):
                k_s[img * pairs + p, slot] = keys[:, p * 128 : (p + 1) * 128]
                v_s[img * pairs + p, slot] = vals[:, p * 128 : (p + 1) * 128]
            token_norm(reverse(jnp.minimum(n + 1, slots * 4 - 1)))
            return carry

        lax.fori_loop(0, slots * 4, tokens, 0)

        for c in gathers:
            c.wait_send()

    pl.run_scoped(
        opening,
        *[pltpu.VMEM(hbm[i].shape, BF16) for i in range(4)],
        pltpu.VMEM((4, toks, d), F32),
    )
    masks = shift_masks(half)

    lane128 = iota((1, 128), 1) // 64
    head_mask = [flag(lane128 == h) for h in range(2)]

    q_bias = row_of(qv_b_ref, 0, d)

    def queries(img, carry):
        query = tn(x1t_s[img * 4], qkv_ref[:, :d]) + q_bias
        query = query.astype(BF16).astype(F32) * 0.125
        for p in range(pairs):
            for h in range(2):
                q_s[img * HEADS + p * 2 + h] = (query[:, p * 128 : (p + 1) * 128] * head_mask[h]).astype(BF16)
        return carry

    lax.fori_loop(0, slots, queries, 0)

    def scores(idx, h, buf):
        top = None
        for c in range(4):
            s = nt(k_s[idx, c], q_s[idx * 2 + h])
            buf[2 * c] = s[:, :128]
            buf[2 * c + 1] = s[:, 128:]
            m = jnp.max(s, axis=0, keepdims=True)
            top = m if top is None else jnp.maximum(top, m)
        top_s[h] = top

    def softmax(idx, h, buf, vt):
        head = idx * 2 + h
        top, total, acc = top_s[h], None, None
        for c in range(4):
            e = jnp.exp(jnp.concatenate([buf[2 * c], buf[2 * c + 1]], axis=1) - top)
            l = col_sum(e)
            total = l if total is None else total + l
            eb = e.astype(BF16)
            e_s[head, c] = eb
            o = nn(vt[c][h * 64 : (h + 1) * 64], eb)
            acc = o if acc is None else acc + o
        linv = 1.0 / total
        linv_s[head] = linv
        of_s[head] = acc * linv

    scores(jnp.int32(0), 0, sa_s)

    def attend(idx, carry):
        vt = [v_s[idx, c].T for c in range(4)]
        scores(idx, 1, sb_s)
        softmax(idx, 0, sa_s, vt)
        scores(jnp.minimum(idx + 1, slots * pairs - 1), 0, sa_s)
        softmax(idx, 1, sb_s, vt)
        return carry

    lax.fori_loop(0, slots * pairs, attend, 0)
    for c in loads[1:]:
        c.wait()
    proj_b, fc1_b, fc2_b = row_of(proj_b_ref, 0, d), row_of(fc1_b_ref, 0, ff), row_of(fc2_b_ref, 0, d)

    def slope_at(j):
        return sa_s.at[j] if j < 8 else sb_s.at[j - 8]

    def closing(dot_s, dom_s, dq_s, dxq_s, acc_s, dx1_s):
        def image(img, carry):
            def mod_row(p):
                return mod_s[p, pl.ds(img, 1), :]

            ot = jnp.concatenate([of_s[img * HEADS + h] for h in range(HEADS)], axis=0).astype(BF16)
            branch = tn(ot, proj_ref[...]) + proj_b
            g1 = mod_row(2)
            resid = dx_s[img] + g1 * branch
            hat2, inv2 = norm(resid)
            x2 = (hat2 * (1.0 + mod_row(4)) + mod_row(3)).astype(BF16)
            x2t_s[img] = x2.T
            mlp = jnp.zeros((toks, d), F32)
            k0, k1 = 0.7978845608028654, 0.044715
            for b in range(blocks):
                at_b = slice(b * d, (b + 1) * d)
                u = nn(x2, fc1_ref[:, at_b]) + fc1_b[:, at_b]
                sq = u * u
                cdf = 0.5 + 0.5 * jnp.tanh(u * (k0 + (k0 * k1) * sq))
                hidden = u * cdf
                slope = cdf + hidden * (1.0 - cdf) * ((2.0 * k0) + (6.0 * k0 * k1) * sq)
                for j in range(3):
                    slope_at(b * 3 + j)[...] = slope[:, j * 128 : (j + 1) * 128]
                hidden = hidden.astype(BF16)
                for j in range(3):
                    a_s[img * 12 + b * 3 + j] = hidden[:, j * 128 : (j + 1) * 128]
                mlp = mlp + nn(hidden, fc2_ref[at_b, :])
            mlp = mlp + fc2_b
            g2 = mod_row(5)
            x3 = resid + g2 * mlp
            hatf, invf = norm(x3)
            scf = 1.0 + mod_row(7)
            xf = (hatf * scf + mod_row(6)).astype(BF16)
            edge_s[4, img] = (nt(wo_s[...], xf) + out_bias) * live_ref[img].astype(F32)
            gy = gy_s[img]
            early_ref[E_OUT : E_OUT + 16, :] += nn(gy, xf)
            early_ref[E_OUT_B : E_OUT_B + 1, 0:16] += nt(jnp.ones((8, toks), BF16), gy)[0:1]
            dxf = tn(gy, wo_s[...])

            def put_mod(p, v):
                early_ref[pl.ds(E_MOD + (p - 2) * slots + img, 1), :] = v

            put_mod(6, col_sum(dxf))
            put_mod(7, col_sum(dxf * hatf))
            dx3 = norm_back(hatf, invf, dxf * scf)
            dm = (g2 * dx3).astype(BF16)
            dm_s[img] = dm
            put_mod(5, col_sum(mlp * dx3))
            early_ref[E_FC2_B : E_FC2_B + 1, :] += col_sum(dm.astype(F32))
            dx2 = jnp.zeros((toks, d), F32)
            for b in range(blocks):
                at_b = slice(b * d, (b + 1) * d)
                slope = jnp.concatenate([slope_at(b * 3 + j)[...] for j in range(3)], axis=1)
                du = (nt(dm, fc2_ref[at_b, :]) * slope).astype(BF16)
                for j in range(3):
                    b_s[img * 12 + b * 3 + j] = du[:, j * 128 : (j + 1) * 128]
                early_ref[E_FC1_B + b : E_FC1_B + b + 1, :] += col_sum(du.astype(F32))
                dx2 = dx2 + nt(du, fc1_ref[:, at_b])
            put_mod(3, col_sum(dx2))
            put_mod(4, col_sum(dx2 * hat2))
            dx = dx3 + norm_back(hat2, inv2, dx2 * (1.0 + mod_row(4)))
            dx_s[img] = dx
            put_mod(2, col_sum(branch * dx))
            da = (g1 * dx).astype(BF16)
            da_s[img] = da
            early_ref[E_PROJ_B : E_PROJ_B + 1, :] += col_sum(da.astype(F32))
            dot = nt(proj_ref[...], da)
            blank = jnp.zeros((64, toks), F32)
            for hd in range(HEADS):
                head = img * HEADS + hd
                piece = dot[hd * 64 : (hd + 1) * 64]
                linv = linv_s[head]
                delta_s[head] = col_sum(piece * of_s[head]) * linv
                piece = piece * linv
                wide = jnp.concatenate([piece, blank] if hd % 2 == 0 else [blank, piece], axis=0).astype(BF16)
                dot_s[head] = wide
                dom_s[head] = wide.T
            return carry

        lax.fori_loop(0, slots, image, 0)

        def pair_row(k):
            return 2 * ff + k * (d + d // 3)

        def wide(ref, img, b):
            return jnp.concatenate([ref[img * 12 + b * 3 + j] for j in range(3)], axis=1)

        def fc2_grad(b, carry):
            total = tree([tn(wide(a_s, img, b), dm_s[img]) for img in range(2)])
            for img in range(2, slots):
                total = total + tn(wide(a_s, img, b), dm_s[img])
            grads_ref[rows_at(b * d, d), :] = total.astype(BF16)
            return carry

        def fc1_grad(b, carry):
            total = tree([nn(x2t_s[img], wide(b_s, img, b)) for img in range(2)])
            for img in range(2, slots):
                total = total + nn(x2t_s[img], wide(b_s, img, b))
            grads_ref[rows_at(ff + b * d, d), :] = total.astype(BF16)
            return carry

        lax.fori_loop(0, blocks, fc2_grad, 0)
        advance(FC2, 0)
        lax.fori_loop(0, blocks, fc1_grad, 0)
        advance(FC1, 0)
        total = None
        for img in range(slots):
            ot = jnp.concatenate([of_s[img * HEADS + h] for h in range(HEADS)], axis=0).astype(BF16)
            term = nn(ot, da_s[img])
            total = term if total is None else total + term
        for k in range(pairs):
            grads_ref[pair_row(k) + d : pair_row(k + 1), :] = total[k * (d // 3) : (k + 1) * (d // 3)].astype(BF16)
        blank = jnp.zeros((16, toks), F32)
        for i in range(slots):
            out = shift_out([edge_s[4, i], blank, blank, blank], masks)
            for s in range(4):
                edge_y[s, i * 16 : (i + 1) * 16, :] = out[s].astype(BF16)
        advance(EDGE_Y, 0)

        def when_at(i, plan):
            for at, events in plan.items():

                @pl.when(i == at)
                def _():
                    for g, k in events:
                        advance(g, k)

        back_plan, tail_plan = {}, {}

        def place(plan, at, g, k):
            plan.setdefault(at, []).append((g, k))

        deep = len(groups[FC2])
        for k in range(1, deep + 1):
            place(back_plan, k, FC2, k)
            place(back_plan, k, FC1, k)
        place(back_plan, 1, EDGE_Y, 1)
        for pair in range(pairs):
            for k in range(1, len(groups[PAIR + pair]) + 1):
                place(tail_plan, min(11, 2 * k - 1), PAIR + pair, k)
        place(tail_plan, 4, EARLY, 1)
        place(tail_plan, 8, EARLY, 2)

        acc_s[...] = jnp.zeros_like(acc_s)

        def attend_back(it, carry):
            when_at(it, back_plan)
            p, img = it // slots, it % slots
            idx = img * pairs + p
            dqt = [None, None]
            jobs = [(c, h) for c in range(4) for h in range(2)]

            def product(job):
                return nn(v_s[idx, job[0]], dot_s[idx * 2 + job[1]])

            dp = product(jobs[0])
            gathered = None
            sum_v = None
            for n, (c, h) in enumerate(jobs):
                head = idx * 2 + h
                ahead = product(jobs[n + 1]) if n + 1 < len(jobs) else None
                if h == 0:
                    kt = k_s[idx, c].T
                    dk, dv = None, None
                e = e_s[head, c]
                ds = (e.astype(F32) * (dp - delta_s[head])).astype(BF16)
                dk_h, dv_h = nn(ds, q_s[head]), nn(e, dom_s[head])
                dk = dk_h if dk is None else dk + dk_h
                dv = dv_h if dv is None else dv + dv_h
                dq_h = nn(kt[h * 64 : (h + 1) * 64], ds)
                dqt[h] = dq_h if dqt[h] is None else dqt[h] + dq_h
                dp = ahead
                if h == 1:
                    dk, dv = dk.astype(BF16), dv.astype(BF16)
                    a_s[idx * 4 + c] = dk
                    b_s[idx * 4 + c] = dv
                    sv = col_sum(dv.astype(F32))
                    sum_v = sv if sum_v is None else sum_v + sv
                    term = nn(x1t_s[img * 4 + c], jnp.concatenate([dk, dv], axis=1))
                    gathered = term if gathered is None else gathered + term
            dq = (jnp.concatenate(dqt, axis=0) * 0.125).T.astype(BF16)
            dq_s[idx] = dq
            lanes = pl.ds(pl.multiple_of(p * 128, 128), 128)
            early_ref[E_V_B : E_V_B + 1, lanes] += sum_v
            early_ref[E_Q_B : E_Q_B + 1, lanes] += col_sum(dq.astype(F32))
            acc_s[:, 128:] += gathered
            acc_s[:, :128] += nn(x1t_s[img * 4], dq)

            for pair in range(pairs):

                @pl.when(it == pair * slots + slots - 1)
                def _():
                    at = pair_row(pair)
                    grads_ref[at : at + d, :] = acc_s[...].astype(BF16)
                    acc_s[...] = jnp.zeros_like(acc_s)
                    advance(PAIR + pair, 0)

            return carry

        lax.fori_loop(0, slots * pairs, attend_back, 0)
        advance(EARLY, 0)

        def joined(ref, img, slot):
            return [ref[(img * pairs + p) * 4 + slot] for p in range(pairs)]

        def query_back(img, carry):
            dq = jnp.concatenate([dq_s[img * pairs + p] for p in range(pairs)], axis=1)
            dxq_s[img] = nt(dq, qkv_ref[:, :d])
            return carry

        lax.fori_loop(0, slots, query_back, 0)

        def product_back(t):
            img, slot = t // 4, t % 4
            dkv = jnp.concatenate(joined(a_s, img, slot) + joined(b_s, img, slot), axis=1)
            own = jnp.where(slot == 0, 1.0, 0.0)
            return nt(dkv, qkv_ref[:, d:]) + dxq_s[img] * own

        dx1_s[...] = product_back(jnp.int32(0))
        def tokens_back(t, carry):
            when_at(t, tail_plan)
            img, slot = t // 4, t % 4
            dx1 = dx1_s[...]
            ahead = product_back(jnp.minimum(t + 1, slots * 4 - 1))
            hat = hat_s[t]
            late_ref[pl.ds(L_MOD + img, 1), :] += col_sum(dx1)
            late_ref[pl.ds(L_MOD + slots + img, 1), :] += col_sum(dx1 * hat)
            own = jnp.where(slot == 0, 1.0, 0.0)
            dtok = norm_back(hat, jnp.sum(jnp.where(inv_lane == t, inv_s[...], 0.0), axis=1, keepdims=True), dx1 * (1.0 + mod_s[1, pl.ds(img, 1), :])) + dx_s[img] * own
            late_ref[L_PATCH_B : L_PATCH_B + 1, :] += col_sum(dtok)
            hi, lo = parts(dtok, 2)
            late_ref[L_PATCH : L_PATCH + 16, :] += nn(pt_s[t], hi) + nn(pt_s[t], lo)
            edge_s[slot, img] = nt(wp_s[...], hi) + nt(wp_s[...], lo)
            dx1_s[...] = ahead
            return carry

        lax.fori_loop(0, slots * 4, tokens_back, 0)

    pl.run_scoped(
        closing,
        pltpu.VMEM((slots * HEADS, 128, toks), BF16),
        pltpu.VMEM((slots * HEADS, toks, 128), BF16),
        pltpu.VMEM((slots * pairs, toks, 128), BF16),
        pltpu.VMEM((slots, toks, d), F32),
        pltpu.VMEM((d, d), F32),
        pltpu.VMEM((toks, d), F32),
    )

    advance(LATE, 0)
    for i in range(slots):
        lat = shift_out([edge_s[s, i] for s in range(4)], masks)
        for s in range(4):
            edge_l[s, i * 16 : (i + 1) * 16, :] = lat[s].astype(BF16)
    advance(EDGE_L, 0)
    advance(LATE, 1)
    advance(EDGE_L, 1)
    advance(LATE, 2)
    for stages in groups:
        for stage in stages:
            stage.drain()
    assert len(net.known) <= count


def step(images, smalls, bigs):
    time_bin, latents = smalls[0], smalls[3]
    qkv_weight, fc1_weight = bigs[4], bigs[6]
    d, ff = qkv_weight.shape[0], fc1_weight.shape[1]
    slots, chans, side, _ = latents.shape
    toks = side * side // 4
    planes = slots * chans * 4
    pairs = HEADS // 2
    heads = slots * HEADS
    out_shape = (
        jax.ShapeDtypeStruct((2 * ff + 4 * d, d), BF16),
        jax.ShapeDtypeStruct((images, E_ROWS, d), BF16),
        jax.ShapeDtypeStruct((images, L_ROWS, d), BF16),
        jax.ShapeDtypeStruct((2, planes, toks), F32),
    )
    scratch = [(w.shape, w.dtype) for w in bigs[4:]] + [
        ((4, 2, planes, toks), BF16), ((8, 8, d), F32), ((slots * 4, 16, toks), BF16),
        ((slots, 16, toks), BF16), ((16, d), BF16), ((16, d), BF16), ((toks, d), BF16), ((slots * 4, d, toks), BF16),
        ((slots * 4, toks, d), F32), ((toks, 128), F32), ((slots * pairs, 4, toks, 128), BF16),
        ((slots * pairs, 4, toks, 128), BF16), ((heads, toks, 128), BF16), ((heads, 4, toks, toks), BF16),
        ((8, toks, 128), F32), ((8, toks, 128), F32), ((2, 1, toks), F32), ((heads, 1, toks), F32), ((heads, 1, toks), F32),
        ((heads, 64, toks), F32), ((slots * 12, toks, 128), BF16), ((slots * 12, toks, 128), BF16),
        ((slots, toks, d), BF16), ((slots, d, toks), BF16), ((slots, toks, d), BF16),
        ((slots, toks, d), F32), ((5, slots, 16, toks), F32),
        ((2 * ff + 4 * d, d), BF16), ((E_ROWS, d), F32), ((L_ROWS, d), F32), ((4, planes, toks), BF16), ((4, planes, toks), BF16),
        ((3, E_ROWS, d), F32), ((E_ROWS, d), BF16), ((3, L_ROWS, d), F32), ((L_ROWS, d), BF16), ((3, planes, toks), BF16),
        ((3, planes, toks), BF16),
    ]
    dma = pltpu.SemaphoreType.DMA
    parts_of = group_list(d, ff)
    count = sum(group_copies(images, plan) for _, _, plan in parts_of) + 2 * (3 + images - 1) + 6
    moved = [(s, BF16) for _, rows, plan in parts_of for s in group_shapes(images, rows, plan)]
    return pl.pallas_call(
        functools.partial(step_kernel, images, count),
        out_shape=out_shape,
        in_specs=[SMEM] * 3 + [VMEM] * (len(smalls) - 3) + [ANY] * len(bigs),
        out_specs=(VMEM,) * 4,
        scratch_shapes=[pltpu.VMEM(shape, kind) for shape, kind in scratch]
        + [dma((len(bigs),)), dma((3,)), dma((3,)), dma((count,)), dma((count,))]
        + [pltpu.VMEM(shape, kind) for shape, kind in moved],
        compiler_params=pltpu.CompilerParams(
            collective_id=0, has_side_effects=True, vmem_limit_bytes=64 * 1024 * 1024 - 65536
        ),
        name="step",
    )(*smalls, *bigs)


def finish_kernel(
    bins, classes, grads_hbm, early_ref, late_ref, planes_ref, ada_hbm, fada_hbm,
    out_ref, lat_ref, time_ref, class_hbm, patch_ref, patch_b_ref, ada_g_hbm, ada_b_ref, qkv_g_hbm, qv_b_ref, proj_g_ref,
    proj_b_ref, fc1_g_hbm, fc1_b_ref, fc2_g_hbm, fc2_b_ref, fada_g_hbm, fada_b_ref, out_gt_ref, out_b_ref,
    grads_ref, ada_ref, fada_ref, class_ref, ada_g_ref, qkv_g_ref, fc1_g_ref, fc2_g_ref, fada_g_ref, in_sem, out_sem,
):
    d = ada_ref.shape[0]
    ff = fc1_g_ref.shape[1]
    blocks = ff // d
    pairs = HEADS // 2
    slots, chans, side, _ = lat_ref.shape
    groups = early_ref.shape[0]
    images = groups * slots
    held = -(-images // 32) * 32

    bounds = [0, ff, 2 * ff, 2 * ff + 4 * d]
    loads = [
        pltpu.make_async_copy(grads_hbm.at[a:b, :], grads_ref.at[a:b, :], in_sem.at[i])
        for i, (a, b) in enumerate(zip(bounds[:-1], bounds[1:]))
    ]
    loads += [pltpu.make_async_copy(ada_hbm, ada_ref, in_sem.at[3]), pltpu.make_async_copy(fada_hbm, fada_ref, in_sem.at[4])]
    for c in loads:
        c.start()
    stores = []

    def send(src, dst):
        c = pltpu.make_async_copy(src, dst, out_sem.at[len(stores)])
        c.start()
        stores.append(c)

    loads[0].wait()
    fc2_g_ref[...] = grads_ref[0:ff, :].astype(F32)
    send(fc2_g_ref, fc2_g_hbm)
    loads[1].wait()
    for b in range(blocks):
        fc1_g_ref[:, b * d : (b + 1) * d] = grads_ref[ff + b * d : ff + (b + 1) * d, :].astype(F32)
    send(fc1_g_ref, fc1_g_hbm)
    loads[2].wait()
    third = d // 3
    for p in range(pairs):
        at = 2 * ff + p * (d + third)
        proj_g_ref[p * third : (p + 1) * third, :] = grads_ref[at + d : at + d + third, :].astype(F32)
        for k in range(3):
            lanes = slice(k * d + p * 128, k * d + (p + 1) * 128)
            qkv_g_ref[:, lanes] = grads_ref[at : at + d, k * 128 : (k + 1) * 128].astype(F32)
    send(qkv_g_ref, qkv_g_hbm)

    all_early = early_ref[...].reshape(groups * E_ROWS, d)
    all_late = late_ref[...].reshape(groups * L_ROWS, d)

    def chosen(block, rows, at):
        out_row, src = iota((held, groups * rows), 0), iota((held, groups * rows), 1)
        sel = (out_row < images) & (src // rows == out_row // slots) & (src % rows == at(out_row % slots))
        return nn(flag(sel).astype(BF16), block)

    cond = chosen(all_early, E_ROWS, lambda i: E_COND + i) + chosen(all_early, E_ROWS, lambda i: E_COND + slots + i)
    ids = chosen(all_early, E_ROWS, lambda i: E_IDS)
    img_row, lane = iota((held, d), 0), iota((held, d), 1)

    def id_part(k):
        return jnp.sum(jnp.where(lane == k * slots + img_row % slots, ids, 0.0), axis=1, keepdims=True)

    time_id, class_id = id_part(0), 256.0 * id_part(1) + id_part(2)

    a1, a2, a3 = parts(swish(cond), 3)
    left = jnp.concatenate([a1, a2, a3], axis=0).T
    loads[3].wait()
    loads[4].wait()
    dact = jnp.zeros((held, d), F32)
    bias_rows = []
    for p in range(8):
        if p < 2:
            dmod = chosen(all_late, L_ROWS, lambda i: L_MOD + p * slots + i)
        else:
            dmod = chosen(all_early, E_ROWS, lambda i: E_MOD + (p - 2) * slots + i)
        dmod16 = dmod.astype(BF16)
        grad = nn(left, jnp.concatenate([dmod16] * 3, axis=0))
        if p < 6:
            ada_g_ref[:, p * d : (p + 1) * d] = grad
            w = ada_ref[:, p * d : (p + 1) * d]
        else:
            fada_g_ref[:, (p - 6) * d : (p - 5) * d] = grad
            w = fada_ref[:, (p - 6) * d : (p - 5) * d]
        bias_rows.append(col_sum(dmod))
        dact = dact + nt(dmod16, w)
        if p == 5:
            send(ada_g_ref, ada_g_hbm)
    send(fada_g_ref, fada_g_hbm)
    ada_b_ref[...] = jnp.concatenate(bias_rows[:6], axis=1).reshape(6 * d)
    fada_b_ref[...] = jnp.concatenate(bias_rows[6:], axis=1).reshape(2 * d)
    sig = 1.0 / (1.0 + jnp.exp(-cond))
    dcond = dact * (sig * (1.0 + cond * (1.0 - sig)))
    stack = jnp.concatenate(parts(dcond, 3), axis=0)
    for ref, ids_col, many in ((class_ref, class_id, classes), (time_ref, time_id, bins)):
        wide = -(-many // 128) * 128
        at = iota((held, wide), 1).astype(F32)
        hit = flag((at == ids_col) & (iota((held, wide), 0) < images)).astype(BF16)
        ref[...] = tn(jnp.concatenate([hit, hit, hit], axis=0), stack)[:many]
        if many == classes:
            send(class_ref, class_hbm)

    early, late = jnp.sum(early_ref[...].astype(F32), axis=0), jnp.sum(late_ref[...].astype(F32), axis=0)
    swap = flag(iota((16, 16), 0) == (iota((16, 16), 1) ^ 3)).astype(BF16)

    def swapped(v):
        return tree([nn(swap, p) for p in parts(v, 2)] + [nn(swap, parts(v, 3)[2]), jnp.zeros_like(v)])

    patch_ref[...] = swapped(late[L_PATCH : L_PATCH + 16])
    out_gt_ref[...] = swapped(early[E_OUT : E_OUT + 16])

    def line(v, row):
        return v[row : row + 1, :]

    patch_b_ref[...] = line(late, L_PATCH_B).reshape(d)
    qv_b_ref[...] = jnp.concatenate([line(early, E_Q_B), line(early, E_V_B)], axis=1).reshape(2 * d)
    proj_b_ref[...] = line(early, E_PROJ_B).reshape(d)
    fc1_b_ref[...] = jnp.concatenate([line(early, E_FC1_B + b) for b in range(blocks)], axis=1).reshape(ff)
    fc2_b_ref[...] = line(early, E_FC2_B).reshape(d)
    tail = jnp.broadcast_to(line(early, E_OUT_B)[:, 0:16], (16, 16))
    pick = flag(iota((16, 16), 1) == (iota((16, 16), 0) ^ 3))
    column = jnp.sum(tail * pick, axis=1, keepdims=True)
    out_b_ref[...] = col_sum(jnp.where(iota((16, 16), 0) == iota((16, 16), 1), column, 0.0)).reshape(16)

    half = side // 2
    keep, spread, pick = plane_maps(slots, chans, side, half)
    for k, ref in ((0, lat_ref), (1, out_ref)):
        total = None
        for piece in parts(planes_ref[k], 3 if k == 0 else 1):
            for j in range(2):
                wide = (tn(pick[j], piece) * keep).astype(BF16)
                term = nt(wide, spread[j])
                total = term if total is None else total + term
        ref[...] = total.reshape(ref.shape).astype(ref.dtype)
    for c in stores:
        c.wait()


def finish(bins, classes, latents, grads, early, late, planes, ada_weight, fada_weight, ff):
    d = ada_weight.shape[0]
    f = lambda *shape: jax.ShapeDtypeStruct(shape, F32)
    out_shape = (
        jax.ShapeDtypeStruct(latents.shape, BF16), f(*latents.shape), f(bins, d), f(classes, d), f(16, d), f(d),
        f(d, 6 * d), f(6 * d), f(d, 3 * d), f(2 * d), f(d, d), f(d), f(d, ff), f(ff), f(ff, d), f(d), f(d, 2 * d), f(2 * d),
        f(16, d), f(16),
    )
    large = (3, 6, 8, 12, 14, 16)
    dma = pltpu.SemaphoreType.DMA
    return pl.pallas_call(
        functools.partial(finish_kernel, bins, classes),
        out_shape=out_shape,
        in_specs=[ANY] + [VMEM] * 3 + [ANY] * 2,
        out_specs=tuple(ANY if i in large else VMEM for i in range(len(out_shape))),
        scratch_shapes=[pltpu.VMEM(x.shape, x.dtype) for x in (grads, ada_weight, fada_weight)]
        + [pltpu.VMEM(out_shape[i].shape, F32) for i in large]
        + [dma((5,)), dma((len(large),))],
        compiler_params=pltpu.CompilerParams(vmem_limit_bytes=60 * 1024 * 1024),
        name="finish",
    )(grads, early, late, planes, ada_weight, fada_weight)


def local(
    images, latents, time_bin, class_label, live, time_table, class_table, patch_weight, patch_bias, ada_weight, ada_bias,
    qkv_weight, qv_bias, proj_weight, proj_bias, fc1_weight, fc1_bias, fc2_weight, fc2_bias, final_ada_weight,
    final_ada_bias, out_weight, out_bias, cotangent,
):
    d, ff = qkv_weight.shape[0], fc1_weight.shape[1]
    pos_a, pos_b = position_tables(LATENT // 2, d)
    smalls = (
        time_bin, class_label, live, latents, cotangent, patch_bias, ada_bias, qv_bias, proj_bias, fc1_bias, fc2_bias,
        final_ada_bias, out_bias, jnp.asarray(pos_a), jnp.asarray(pos_b), patch_weight, out_weight.T,
    )
    bigs = (time_table, class_table, ada_weight, final_ada_weight, qkv_weight, proj_weight, fc1_weight, fc2_weight)
    grads, early, late, planes = step(images, smalls, bigs)
    outs = list(
        finish(
            time_table.shape[0], class_table.shape[0], latents, grads, early, late, planes, ada_weight, final_ada_weight, ff
        )
    )
    outs[18] = outs[18].T
    return tuple(outs)


def solution(mesh):
    assert mesh.shape["row"] == 2 and mesh.shape["col"] == 2
    tiles = P("img", None, "row", "col")
    return jax.shard_map(
        functools.partial(local, mesh.shape["img"]),
        mesh=mesh,
        in_specs=(tiles,) + (P("img"),) * 3 + (P(),) * 18 + (tiles,),
        out_specs=(tiles, tiles) + (P(),) * 18,
        check_vma=False,
    )
```

time: 188 us -> 155 us (0.82)
  Pallas kernels: 170 us -> 154 us
  local copies, waits for them, and re-layouts: 15 us -> 0 us
    pallas_call x3 -> x1, Pallas kernels: 158 us -> 144 us  [step(): pl.pallas_call(functools.partial(step_kernel, images, count), out_shape=o...]
    slice x5 -> x0, local copies, waits for them, and re-layouts: 6.34 us -> none  [the longest x1 1.33 us: local(): bias_g[BIAS_ADA:BIAS_ADA + 6 * d]]
    concatenate x8 -> x0, local copies, waits for them, and re-layouts: 5.58 us -> none  [local(): jnp.concatenate([patch_bias, qv_bias, proj_bias, fc1_bias, fc2_bias, ada_...]
    unnamed x2 -> x0, local copies, waits for them, and re-layouts: 3.09 us -> none
where the time goes in v2:
time: 155 us
  Pallas kernels  154 us (99%)
    pallas_call x1, Pallas kernels, step(): pl.pallas_call(functools.partial(step_kernel, images, count), out_shape=o...  144 us
    pallas_call x1, Pallas kernels, finish(): pl.pallas_call(functools.partial(finish_kernel, bins, classes), out_shape...  10.3 us

profile of v2, /device:TPU:0, one launch (start us, length us, event | category | flops | bytes accessed | tf_op | source)
XLA Modules:
  0.0 154.9 jit_solution(8660904941061031810)
XLA Ops:
  0.7 143.8 %step.1 = (bf16[4608,384]{1,0:T(8,128)(2,1)}, bf16[8,64,384]{2,1,0:T(8,128)(2,1)}, bf16[8,32,384]{2,1,0:T(8,128)(2,1)}, f32[2,48,256]{2,1,0:T(8,128)}) custom-call(s32[3]{0:T(128)} %refs_0_.1, s32[3]{0:T(128)} %refs_1_.1, s32[3]{0:T(128)} %refs_2_.1, bf16[3,4,32,32]{3,2,1,0:T(8,128)(2,1)} %refs_3_.1, bf16[3,4,32,32]{3,2,1,0:T(8,128)(2,1)} %refs_4_.1, ...), custom_call_target="tpu_custom_call" | custom-call | tf_op jit(solution)/shard_map/step/pallas_call | solution.py:905
  144.5 10.3 %finish.1 = (bf16[3,4,32,32]{3,2,1,0:T(8,128)(2,1)}, f32[3,4,32,32]{3,2,1,0:T(8,128)}, f32[100,384]{1,0:T(8,128)}, f32[1001,384]{1,0:T(8,128)}, f32[16,384]{1,0:...) custom-call(bf16[4608,384]{1,0:T(8,128)(2,1)} %get-tuple-element.44., ...), custom_call_target="tpu_custom_call" | custom-call | tf_op jit(solution)/shard_map/finish/pallas_call | solution.py:1067

commit v3 on v2

--- a/solution.py
+++ b/solution.py
@@ -164,8 +164,8 @@
     return jnp.sum(v, axis=0, keepdims=True)
 
 
-E_OUT, E_PROJ_B, E_FC2_B, E_Q_B, E_V_B, E_FC1_B, E_OUT_B, E_MOD, E_COND, E_IDS, E_ROWS = 0, 16, 17, 18, 19, 20, 24, 32, 50, 56, 64
-L_PATCH, L_PATCH_B, L_MOD, L_ROWS = 0, 16, 18, 32
+E_OUT, E_PROJ_B, E_FC2_B, E_FC1_B, E_OUT_B, E_MOD, E_COND, E_IDS, E_ROWS = 0, 16, 17, 18, 22, 23, 41, 47, 48
+L_PATCH, L_PATCH_B, L_MOD, L_Q_B, L_V_B, L_ROWS = 0, 16, 17, 23, 24, 32
 
 
 def tree(terms):
@@ -215,33 +215,41 @@
 
 def ways(images, plan):
     bits = images.bit_length() - 1
-    return [way for way in plan if isinstance(way, str) or way[0] + way[1] <= bits]
+    kept = ["".join(x for x in way if not x.isdigit() or int(x) < bits) for way in plan]
+    return [way for way in kept if way]
 
 
 def shared_bits(images, plan):
-    return max([way[0] + way[1] for way in ways(images, plan) if not isinstance(way, str)] + [0])
+    return max([int(x) + 1 for way in ways(images, plan) for x in way if x.isdigit()] + [0])
 
 
 def members(way):
-    return {"col": 2, "row": 2, "four": 4}[way] if isinstance(way, str) else 1 << way[1]
+    return 1 << len(way)
 
 
 def position(way):
-    row, col = lax.axis_index("row"), lax.axis_index("col")
-    if isinstance(way, str):
-        return {"col": col, "row": row, "four": col * 2 + row}[way]
-    return (lax.axis_index("img") >> way[0]) & ((1 << way[1]) - 1)
+    total = 0
+    for x in way:
+        if x.isdigit():
+            side = (lax.axis_index("img") >> int(x)) & 1
+        else:
+            side = lax.axis_index({"c": "col", "r": "row"}[x])
+        total = 2 * total + side
+    return total
 
 
 def partner(way, delta):
-    row, col = lax.axis_index("row"), lax.axis_index("col")
-    if way == "col":
-        return {"col": 1 - col}
-    if way == "row":
-        return {"row": 1 - row}
-    if way == "four":
-        return {"row": row ^ (delta & 1), "col": col ^ (delta >> 1)}
-    return far(delta << way[0])
+    device, flips = {}, 0
+    for k, x in enumerate(reversed(way)):
+        if delta >> k & 1:
+            if x.isdigit():
+                flips |= 1 << int(x)
+            else:
+                name = {"c": "col", "r": "row"}[x]
+                device[name] = 1 - lax.axis_index(name)
+    if flips:
+        device["img"] = lax.axis_index("img") ^ flips
+    return device
 
 
 def group_shapes(images, rows, plan):
@@ -338,7 +346,7 @@
         return [net.make(name + "m" + str(s), block, got.at[s - 1], mate(s)) for s in (1, 2, 3)]
 
     def r0():
-        t = tree([block[...], got[0], got[1], got[2]]).astype(BF16)
+        t = tree([r.astype(F32) for r in (block[...], got[0], got[1], got[2])]).astype(BF16)
         total[...] = t
         out[lax.axis_index("img")] = t
 
@@ -359,16 +367,24 @@
     return [Stage(c0, r0)]
 
 
-FF_PLANS = (("col", "row", (0, 2), (2, 1)), ("col", (0, 2), "row", (2, 1)))
-PAIR_PLANS = (("col", "row", (0, 3)), ("col", (0, 2), "row", (2, 1)), ("four", (0, 3)))
-
+PLANS = (("c", "r0", "12"), ("c", "01", "r2"), ("c", "r1", "02"))
+FC, PAIR, EARLY, LATE, EDGE_Y, EDGE_L = 0, 6, 9, 10, 11, 12
+IMAGE_EVENTS = ((1, 0, 1), (1, 1, 1), (2, 2, 1))
+GRAD_EVENTS = ((1, 0, 2), (2, 1, 2), (3, 2, 2))
+BACK_EVENTS = (
+    (1, 3, 1), (1, 4, 1), (1, 5, 1), (2, 0, 3), (2, 1, 3), (2, 2, 3), (2, EDGE_Y, 1), (3, 3, 2), (3, 4, 2), (3, 5, 2),
+    (4, 0, 4), (4, 1, 4), (4, 2, 4), (4, PAIR, 1), (5, 3, 3), (5, 4, 3), (5, 5, 3), (5, EARLY, 1), (6, 0, 5), (6, 1, 5), (6, 2, 5),
+    (6, PAIR, 2), (7, 3, 4), (7, 4, 4), (7, 5, 4), (7, PAIR + 1, 1), (8, 0, 6), (8, 1, 6), (8, 2, 6), (8, PAIR, 3),
+)
+TAIL_EVENTS = (
+    (0, 3, 5), (0, 4, 5), (0, 5, 5), (1, EARLY, 2), (2, PAIR + 1, 2), (3, PAIR, 4), (4, PAIR + 2, 1), (5, 3, 6), (5, 4, 6), (5, 5, 6),
+    (7, PAIR + 1, 3), (8, PAIR, 5), (10, PAIR + 2, 2), (11, PAIR + 1, 4), (11, PAIR, 6),
+)
+END_EVENTS = ((PAIR + 2, 3), (PAIR + 1, 5), (PAIR + 2, 4), (PAIR + 1, 6))
 
 def group_list(d, ff):
-    base = 2 * ff
-    out = [(0, ff, FF_PLANS[0]), (ff, ff, FF_PLANS[1])]
-    for k in range(3):
-        out.append((base + k * (d + d // 3), d + d // 3, PAIR_PLANS[k]))
-    return out
+    rows = d + d // 3
+    return [(k * rows, rows, PLANS[k % 3]) for k in range((2 * ff + 4 * d) // rows)]
 
 
 def step_kernel(images, count, *refs):
@@ -387,7 +403,7 @@
     qkv_ref, proj_ref, fc1_ref, fc2_ref = held
     (planes_ref, mod_s, pt_s, gy_s, wp_s, wo_s, x1_s, x1t_s, hat_s, inv_s, k_s, v_s, q_s, e_s, sa_s, sb_s, top_s,
      linv_s, delta_s, of_s, a_s, b_s, dm_s, x2t_s, da_s, dx_s, edge_s,
-     grads_ref, early_ref, late_ref, edge_y, edge_l, early_got, early_sum, late_got, late_sum, edge_y_got, edge_l_got) = take(38)
+     grads_ref, early_ref, late_ref, early_16, late_16, edge_y, edge_l, early_got, early_sum, late_got, late_sum, edge_y_got, edge_l_got) = take(40)
     load_sem, gather_send, gather_recv, send_sem, recv_sem = take(5)
     bufs = refs
 
@@ -407,12 +423,10 @@
         n = len(group_shapes(images, rows, plan))
         groups.append(group_stages("g" + str(g), images, base, rows, plan, grads_ref, out_ref, bufs[:n], net))
         del bufs[:n]
-    groups.append(sum_stages("e", images, early_ref, early_got, early_sum, early_out, net))
-    groups.append(sum_stages("l", images, late_ref, late_got, late_sum, late_out, net))
+    groups.append(sum_stages("e", images, early_16, early_got, early_sum, early_out, net))
+    groups.append(sum_stages("l", images, late_16, late_got, late_sum, late_out, net))
     groups.append(edge_stages("y", edge_y, edge_y_got, planes_out, 1, net))
     groups.append(edge_stages("x", edge_l, edge_l_got, planes_out, 0, net))
-    FC2, FC1, PAIR, EARLY, LATE, EDGE_Y, EDGE_L = 0, 1, 2, 5, 6, 7, 8
-
     def advance(g, k):
         if k > 0:
             groups[g][k - 1].finish()
@@ -604,10 +618,45 @@
         c.wait()
     proj_b, fc1_b, fc2_b = row_of(proj_b_ref, 0, d), row_of(fc1_b_ref, 0, ff), row_of(fc2_b_ref, 0, d)
 
-    def slope_at(j):
-        return sa_s.at[j] if j < 8 else sb_s.at[j - 8]
-
-    def closing(dot_s, dom_s, dq_s, dxq_s, acc_s, dx1_s):
+    def closing(hat2_s, dot_s, dom_s, dq_s, dxq_s, acc_s, dx1_s):
+        def pair_row(k):
+            return 2 * ff + k * (d + d // 3)
+
+        def wide(ref, img, b):
+            return jnp.concatenate([ref[img * 12 + b * 3 + j] for j in range(3)], axis=1)
+
+        def fc2_grad(b, carry):
+            total = tree([tn(wide(a_s, img, b), dm_s[img]) for img in range(2)])
+            for img in range(2, slots):
+                total = total + tn(wide(a_s, img, b), dm_s[img])
+            grads_ref[rows_at(b * d, d), :] = total.astype(BF16)
+            started(b, FC)
+            return carry
+
+        def started(b, first):
+            for k in range(1, blocks):
+
+                @pl.when(b == k)
+                def _():
+                    advance(first + k - 1, 0)
+
+        def when_at(i, plan):
+            for at, events in plan.items():
+
+                @pl.when(i == at)
+                def _():
+                    for g, k in events:
+                        advance(g, k)
+
+        image_plan, grad_plan, back_plan, tail_plan = {}, {}, {}, {}
+        for plan, events in ((image_plan, IMAGE_EVENTS), (grad_plan, GRAD_EVENTS), (back_plan, BACK_EVENTS), (tail_plan, TAIL_EVENTS)):
+            for at, g, k in events:
+                if k <= len(groups[g]):
+                    plan.setdefault(at, []).append((g, k))
+
+        def inv_at(t):
+            return jnp.sum(jnp.where(inv_lane == t, inv_s[...], 0.0), axis=1, keepdims=True)
+
         def image(img, carry):
             def mod_row(p):
                 return mod_s[p, pl.ds(img, 1), :]
@@ -617,6 +666,8 @@
             g1 = mod_row(2)
             resid = dx_s[img] + g1 * branch
             hat2, inv2 = norm(resid)
+            hat2_s[img] = hat2
+            inv_s[...] = jnp.where(inv_lane == slots * 4 + img, inv2, inv_s[...])
             x2 = (hat2 * (1.0 + mod_row(4)) + mod_row(3)).astype(BF16)
             x2t_s[img] = x2.T
             mlp = jnp.zeros((toks, d), F32)
@@ -628,8 +679,9 @@
                 cdf = 0.5 + 0.5 * jnp.tanh(u * (k0 + (k0 * k1) * sq))
                 hidden = u * cdf
                 slope = cdf + hidden * (1.0 - cdf) * ((2.0 * k0) + (6.0 * k0 * k1) * sq)
+                slope = slope.astype(BF16)
                 for j in range(3):
-                    slope_at(b * 3 + j)[...] = slope[:, j * 128 : (j + 1) * 128]
+                    b_s[img * 12 + b * 3 + j] = slope[:, j * 128 : (j + 1) * 128]
                 hidden = hidden.astype(BF16)
                 for j in range(3):
                     a_s[img * 12 + b * 3 + j] = hidden[:, j * 128 : (j + 1) * 128]
@@ -656,10 +708,27 @@
             dm_s[img] = dm
             put_mod(5, col_sum(mlp * dx3))
             early_ref[E_FC2_B : E_FC2_B + 1, :] += col_sum(dm.astype(F32))
+            dx_s[img] = dx3
+            return carry
+
+        lax.fori_loop(0, slots, image, 0)
+        lax.fori_loop(0, blocks, fc2_grad, 0)
+
+        def image_back(img, carry):
+            when_at(img, image_plan)
+
+            def mod_row(p):
+                return mod_s[p, pl.ds(img, 1), :]
+
+            def put_mod(p, v):
+                early_ref[pl.ds(E_MOD + (p - 2) * slots + img, 1), :] = v
+
+            g1, dm, hat2 = mod_row(2), dm_s[img], hat2_s[img]
+            inv2 = inv_at(slots * 4 + img)
             dx2 = jnp.zeros((toks, d), F32)
             for b in range(blocks):
                 at_b = slice(b * d, (b + 1) * d)
-                slope = jnp.concatenate([slope_at(b * 3 + j)[...] for j in range(3)], axis=1)
+                slope = jnp.concatenate([b_s[img * 12 + b * 3 + j] for j in range(3)], axis=1).astype(F32)
                 du = (nt(dm, fc2_ref[at_b, :]) * slope).astype(BF16)
                 for j in range(3):
                     b_s[img * 12 + b * 3 + j] = du[:, j * 128 : (j + 1) * 128]
@@ -667,8 +736,10 @@
                 dx2 = dx2 + nt(du, fc1_ref[:, at_b])
             put_mod(3, col_sum(dx2))
             put_mod(4, col_sum(dx2 * hat2))
-            dx = dx3 + norm_back(hat2, inv2, dx2 * (1.0 + mod_row(4)))
+            dx = dx_s[img] + norm_back(hat2, inv2, dx2 * (1.0 + mod_row(4)))
             dx_s[img] = dx
+            ot = jnp.concatenate([of_s[img * HEADS + h] for h in range(HEADS)], axis=0).astype(BF16)
+            branch = tn(ot, proj_ref[...]) + proj_b
             put_mod(2, col_sum(branch * dx))
             da = (g1 * dx).astype(BF16)
             da_s[img] = da
@@ -686,32 +757,18 @@
                 dom_s[head] = wide.T
             return carry
 
-        lax.fori_loop(0, slots, image, 0)
-
-        def pair_row(k):
-            return 2 * ff + k * (d + d // 3)
-
-        def wide(ref, img, b):
-            return jnp.concatenate([ref[img * 12 + b * 3 + j] for j in range(3)], axis=1)
-
-        def fc2_grad(b, carry):
-            total = tree([tn(wide(a_s, img, b), dm_s[img]) for img in range(2)])
-            for img in range(2, slots):
-                total = total + tn(wide(a_s, img, b), dm_s[img])
-            grads_ref[rows_at(b * d, d), :] = total.astype(BF16)
-            return carry
+        lax.fori_loop(0, slots, image_back, 0)
 
         def fc1_grad(b, carry):
+            when_at(b, grad_plan)
             total = tree([nn(x2t_s[img], wide(b_s, img, b)) for img in range(2)])
             for img in range(2, slots):
                 total = total + nn(x2t_s[img], wide(b_s, img, b))
             grads_ref[rows_at(ff + b * d, d), :] = total.astype(BF16)
+            started(b, FC + blocks - 1)
             return carry
 
-        lax.fori_loop(0, blocks, fc2_grad, 0)
-        advance(FC2, 0)
         lax.fori_loop(0, blocks, fc1_grad, 0)
-        advance(FC1, 0)
         total = None
         for img in range(slots):
             ot = jnp.concatenate([of_s[img * HEADS + h] for h in range(HEADS)], axis=0).astype(BF16)
@@ -724,31 +781,9 @@
             out = shift_out([edge_s[4, i], blank, blank, blank], masks)
             for s in range(4):
                 edge_y[s, i * 16 : (i + 1) * 16, :] = out[s].astype(BF16)
+        early_16[...] = early_ref[...].astype(BF16)
         advance(EDGE_Y, 0)
-
-        def when_at(i, plan):
-            for at, events in plan.items():
-
-                @pl.when(i == at)
-                def _():
-                    for g, k in events:
-                        advance(g, k)
-
-        back_plan, tail_plan = {}, {}
-
-        def place(plan, at, g, k):
-            plan.setdefault(at, []).append((g, k))
-
-        deep = len(groups[FC2])
-        for k in range(1, deep + 1):
-            place(back_plan, k, FC2, k)
-            place(back_plan, k, FC1, k)
-        place(back_plan, 1, EDGE_Y, 1)
-        for pair in range(pairs):
-            for k in range(1, len(groups[PAIR + pair]) + 1):
-                place(tail_plan, min(11, 2 * k - 1), PAIR + pair, k)
-        place(tail_plan, 4, EARLY, 1)
-        place(tail_plan, 8, EARLY, 2)
+        advance(EARLY, 0)
 
         acc_s[...] = jnp.zeros_like(acc_s)
 
@@ -790,8 +825,8 @@
             dq = (jnp.concatenate(dqt, axis=0) * 0.125).T.astype(BF16)
             dq_s[idx] = dq
             lanes = pl.ds(pl.multiple_of(p * 128, 128), 128)
-            early_ref[E_V_B : E_V_B + 1, lanes] += sum_v
-            early_ref[E_Q_B : E_Q_B + 1, lanes] += col_sum(dq.astype(F32))
+            late_ref[L_V_B : L_V_B + 1, lanes] += sum_v
+            late_ref[L_Q_B : L_Q_B + 1, lanes] += col_sum(dq.astype(F32))
             acc_s[:, 128:] += gathered
             acc_s[:, :128] += nn(x1t_s[img * 4], dq)
 
@@ -807,7 +842,6 @@
             return carry
 
         lax.fori_loop(0, slots * pairs, attend_back, 0)
-        advance(EARLY, 0)
 
         def joined(ref, img, slot):
             return [ref[(img * pairs + p) * 4 + slot] for p in range(pairs)]
@@ -835,7 +869,7 @@
             late_ref[pl.ds(L_MOD + img, 1), :] += col_sum(dx1)
             late_ref[pl.ds(L_MOD + slots + img, 1), :] += col_sum(dx1 * hat)
             own = jnp.where(slot == 0, 1.0, 0.0)
-            dtok = norm_back(hat, jnp.sum(jnp.where(inv_lane == t, inv_s[...], 0.0), axis=1, keepdims=True), dx1 * (1.0 + mod_s[1, pl.ds(img, 1), :])) + dx_s[img] * own
+            dtok = norm_back(hat, inv_at(t), dx1 * (1.0 + mod_s[1, pl.ds(img, 1), :])) + dx_s[img] * own
             late_ref[L_PATCH_B : L_PATCH_B + 1, :] += col_sum(dtok)
             hi, lo = parts(dtok, 2)
             late_ref[L_PATCH : L_PATCH + 16, :] += nn(pt_s[t], hi) + nn(pt_s[t], lo)
@@ -847,6 +881,7 @@
 
     pl.run_scoped(
         closing,
+        pltpu.VMEM((slots, toks, d), F32),
         pltpu.VMEM((slots * HEADS, 128, toks), BF16),
         pltpu.VMEM((slots * HEADS, toks, 128), BF16),
         pltpu.VMEM((slots * pairs, toks, 128), BF16),
@@ -855,15 +890,24 @@
         pltpu.VMEM((toks, d), F32),
     )
 
+    late_16[...] = late_ref[...].astype(BF16)
     advance(LATE, 0)
     for i in range(slots):
         lat = shift_out([edge_s[s, i] for s in range(4)], masks)
         for s in range(4):
             edge_l[s, i * 16 : (i + 1) * 16, :] = lat[s].astype(BF16)
     advance(EDGE_L, 0)
-    advance(LATE, 1)
-    advance(EDGE_L, 1)
-    advance(LATE, 2)
+    state = {g: 1 for g in (LATE, EDGE_L)}
+    for g in (*range(FC, PAIR + 3), EARLY, EDGE_Y):
+        done = [k for events in (IMAGE_EVENTS, GRAD_EVENTS, BACK_EVENTS, TAIL_EVENTS) for _, h, k in events if h == g]
+        assert done == list(range(1, len(done) + 1))
+        state[g] = len(done) + 1
+    order = [LATE, EDGE_L, LATE] + [g for g, _ in END_EVENTS]
+    order += [g for g in state for _ in range(len(groups[g]))]
+    for g in order:
+        if state[g] <= len(groups[g]):
+            advance(g, state[g])
+            state[g] += 1
     for stages in groups:
         for stage in stages:
             stage.drain()
@@ -894,8 +938,8 @@
         ((heads, 64, toks), F32), ((slots * 12, toks, 128), BF16), ((slots * 12, toks, 128), BF16),
         ((slots, toks, d), BF16), ((slots, d, toks), BF16), ((slots, toks, d), BF16),
         ((slots, toks, d), F32), ((5, slots, 16, toks), F32),
-        ((2 * ff + 4 * d, d), BF16), ((E_ROWS, d), F32), ((L_ROWS, d), F32), ((4, planes, toks), BF16), ((4, planes, toks), BF16),
-        ((3, E_ROWS, d), F32), ((E_ROWS, d), BF16), ((3, L_ROWS, d), F32), ((L_ROWS, d), BF16), ((3, planes, toks), BF16),
+        ((2 * ff + 4 * d, d), BF16), ((E_ROWS, d), F32), ((L_ROWS, d), F32), ((E_ROWS, d), BF16), ((L_ROWS, d), BF16), ((4, planes, toks), BF16), ((4, planes, toks), BF16),
+        ((3, E_ROWS, d), BF16), ((E_ROWS, d), BF16), ((3, L_ROWS, d), BF16), ((L_ROWS, d), BF16), ((3, planes, toks), BF16),
         ((3, planes, toks), BF16),
     ]
     dma = pltpu.SemaphoreType.DMA
@@ -1031,7 +1075,7 @@
         return v[row : row + 1, :]
 
     patch_b_ref[...] = line(late, L_PATCH_B).reshape(d)
-    qv_b_ref[...] = jnp.concatenate([line(early, E_Q_B), line(early, E_V_B)], axis=1).reshape(2 * d)
+    qv_b_ref[...] = jnp.concatenate([line(late, L_Q_B), line(late, L_V_B)], axis=1).reshape(2 * d)
     proj_b_ref[...] = line(early, E_PROJ_B).reshape(d)
     fc1_b_ref[...] = jnp.concatenate([line(early, E_FC1_B + b) for b in range(blocks)], axis=1).reshape(ff)
     fc2_b_ref[...] = line(early, E_FC2_B).reshape(d)

time: 155 us -> 126 us (0.81)
  Pallas kernels: 154 us -> 125 us
    pallas_call x1, Pallas kernels: 144 us -> 115 us  [step(): pl.pallas_call(functools.partial(step_kernel, images, count), out_shape=o...]
where the time goes in v3:
time: 126 us
  Pallas kernels  125 us (99%)
    pallas_call x1, Pallas kernels, step(): pl.pallas_call(functools.partial(step_kernel, images, count), out_shape=o...  115 us
    pallas_call x1, Pallas kernels, finish(): pl.pallas_call(functools.partial(finish_kernel, bins, classes), out_shape...  10.2 us

profile of v3, /device:TPU:0, one launch (start us, length us, event | category | flops | bytes accessed | tf_op | source)
XLA Modules:
  0.0 126.1 jit_solution(17178732104227461673)
XLA Ops:
  0.7 115.0 %step.1 = (bf16[4608,384]{1,0:T(8,128)(2,1)}, bf16[8,48,384]{2,1,0:T(8,128)(2,1)}, bf16[8,32,384]{2,1,0:T(8,128)(2,1)}, f32[2,48,256]{2,1,0:T(8,128)}) custom-call(s32[3]{0:T(128)} %refs_0_.1, s32[3]{0:T(128)} %refs_1_.1, s32[3]{0:T(128)} %refs_2_.1, bf16[3,4,32,32]{3,2,1,0:T(8,128)(2,1)} %refs_3_.1, bf16[3,4,32,32]{3,2,1,0:T(8,128)(2,1)} %refs_4_.1, ...), custom_call_target="tpu_custom_call" | custom-call | tf_op jit(solution)/shard_map/step/pallas_call | solution.py:949
  115.7 10.2 %finish.1 = (bf16[3,4,32,32]{3,2,1,0:T(8,128)(2,1)}, f32[3,4,32,32]{3,2,1,0:T(8,128)}, f32[100,384]{1,0:T(8,128)}, f32[1001,384]{1,0:T(8,128)}, f32[16,384]{1,0:...) custom-call(bf16[4608,384]{1,0:T(8,128)(2,1)} %get-tuple-element.44., ...), custom_call_target="tpu_custom_call" | custom-call | tf_op jit(solution)/shard_map/finish/pallas_call | solution.py:1111

commit v4 on v3

--- a/solution.py
+++ b/solution.py
@@ -357,34 +357,30 @@
     return [Stage(c0, r0), Stage(c1)]
 
 
-def edge_stages(name, edge, got, out, k, net):
+def edge_stages(name, edge, got, out, net):
     def c0():
         return [net.make(name + str(s), edge.at[s], got.at[s - 1], mate(s)) for s in (1, 2, 3)]
 
     def r0():
-        out[k] = tree([r.astype(F32) for r in (edge[0], got[1], got[0], got[2])])
+        out[...] = tree([r.astype(F32) for r in (edge[0], got[1], got[0], got[2])])
 
     return [Stage(c0, r0)]
 
 
-PLANS = (("c", "r0", "12"), ("c", "01", "r2"), ("c", "r1", "02"))
-FC, PAIR, EARLY, LATE, EDGE_Y, EDGE_L = 0, 6, 9, 10, 11, 12
-IMAGE_EVENTS = ((1, 0, 1), (1, 1, 1), (2, 2, 1))
-GRAD_EVENTS = ((1, 0, 2), (2, 1, 2), (3, 2, 2))
-BACK_EVENTS = (
-    (1, 3, 1), (1, 4, 1), (1, 5, 1), (2, 0, 3), (2, 1, 3), (2, 2, 3), (2, EDGE_Y, 1), (3, 3, 2), (3, 4, 2), (3, 5, 2),
-    (4, 0, 4), (4, 1, 4), (4, 2, 4), (4, PAIR, 1), (5, 3, 3), (5, 4, 3), (5, 5, 3), (5, EARLY, 1), (6, 0, 5), (6, 1, 5), (6, 2, 5),
-    (6, PAIR, 2), (7, 3, 4), (7, 4, 4), (7, 5, 4), (7, PAIR + 1, 1), (8, 0, 6), (8, 1, 6), (8, 2, 6), (8, PAIR, 3),
-)
-TAIL_EVENTS = (
-    (0, 3, 5), (0, 4, 5), (0, 5, 5), (1, EARLY, 2), (2, PAIR + 1, 2), (3, PAIR, 4), (4, PAIR + 2, 1), (5, 3, 6), (5, 4, 6), (5, 5, 6),
-    (7, PAIR + 1, 3), (8, PAIR, 5), (10, PAIR + 2, 2), (11, PAIR + 1, 4), (11, PAIR, 6),
-)
-END_EVENTS = ((PAIR + 2, 3), (PAIR + 1, 5), (PAIR + 2, 4), (PAIR + 1, 6))
+SLOW = (("c", "r", "0", "12"), ("c", "0", "1", "r2"), ("c", "1", "r", "02"))
+FAST = (("c", "r0", "12"), ("c", "01", "r2"), ("c", "r1", "02"))
+FC, PAIR, EARLY, LATE, EDGE_L = 0, 3, 6, 7, 8
+IMAGE_EVENTS = ((2, 0, 1),)
+GRAD_EVENTS = ()
+BACK_EVENTS = ((1, 0, 2), (1, 1, 1), (1, 2, 1), (3, 0, 3), (3, 6, 1), (4, 1, 2), (4, 2, 2), (5, 0, 4), (5, 3, 1), (6, 1, 3), (6, 2, 3), (7, 0, 5), (7, 3, 2), (8, 1, 4), (8, 2, 4), (8, 4, 1), (8, 6, 2))
+TAIL_EVENTS = ((0, 0, 6), (0, 3, 3), (2, 1, 5), (2, 2, 5), (4, 5, 1), (8, 0, 7), (8, 1, 6), (8, 2, 6), (8, 3, 4), (8, 4, 2), (11, 0, 8), (11, 5, 2))
+END_EVENTS = (4, 3, 5, 1, 2, 7, 8, 4, 3, 1, 2, 5, 7, 4, 5, 4, 5)
+
 
 def group_list(d, ff):
-    rows = d + d // 3
-    return [(k * rows, rows, PLANS[k % 3]) for k in range((2 * ff + 4 * d) // rows)]
+    large, rows = 2 * ff // 3, d + d // 3
+    out = [(k * large, large, SLOW[k]) for k in range(3)]
+    return out + [(2 * ff + k * rows, rows, FAST[k]) for k in range(3)]
 
 
 def step_kernel(images, count, *refs):
@@ -401,9 +397,9 @@
     out_ref, early_out, late_out, planes_out = take(4)
     held = take(4)
     qkv_ref, proj_ref, fc1_ref, fc2_ref = held
-    (planes_ref, mod_s, pt_s, gy_s, wp_s, wo_s, x1_s, x1t_s, hat_s, inv_s, k_s, v_s, q_s, e_s, sa_s, sb_s, top_s,
+    (planes_ref, mod_s, pt_s, gy_s, wp_s, wo_s, x1_s, x1_b, x1t_s, hat_s, inv_s, k_s, v_s, q_s, e_s, sa_s, sb_s, top_s,
      linv_s, delta_s, of_s, a_s, b_s, dm_s, x2t_s, da_s, dx_s, edge_s,
-     grads_ref, early_ref, late_ref, early_16, late_16, edge_y, edge_l, early_got, early_sum, late_got, late_sum, edge_y_got, edge_l_got) = take(40)
+     grads_ref, early_ref, late_ref, early_16, late_16, edge_l, early_got, early_sum, late_got, late_sum, edge_l_got) = take(39)
     load_sem, gather_send, gather_recv, send_sem, recv_sem = take(5)
     bufs = refs
 
@@ -425,8 +421,7 @@
         del bufs[:n]
     groups.append(sum_stages("e", images, early_16, early_got, early_sum, early_out, net))
     groups.append(sum_stages("l", images, late_16, late_got, late_sum, late_out, net))
-    groups.append(edge_stages("y", edge_y, edge_y_got, planes_out, 1, net))
-    groups.append(edge_stages("x", edge_l, edge_l_got, planes_out, 0, net))
+    groups.append(edge_stages("x", edge_l, edge_l_got, planes_out, net))
     def advance(g, k):
         if k > 0:
             groups[g][k - 1].finish()
@@ -523,35 +518,39 @@
 
         v_bias = row_of(qv_b_ref, d, d)
 
-        def token_norm(t):
+        def token_norm(t, x1_buf):
             img, slot = t // 4, t % 4
             tok = tn(pt_s[t], wp_s[...]) + pos_s[slot]
             dx_s[img] = tok
             hat, inv = norm(tok)
             hat_s[t] = hat
             inv_s[...] = jnp.where(inv_lane == t, inv, inv_s[...])
-            x1_s[...] = (hat * (1.0 + mod_s[1, pl.ds(img, 1), :]) + mod_s[0, pl.ds(img, 1), :]).astype(BF16)
-
-        token_norm(jnp.int32(3))
-        loads[0].wait()
-
-        def reverse(n):
-            return n // 4 * 4 + 3 - n % 4
-
-        def tokens(n, carry):
-            t = reverse(n)
+            x1_buf[...] = (hat * (1.0 + mod_s[1, pl.ds(img, 1), :]) + mod_s[0, pl.ds(img, 1), :]).astype(BF16)
+
+        def token_keys(t, x1_buf):
             img, slot = t // 4, t % 4
-            x1 = x1_s[...]
-            x1t_s[t] = x1.T
+            x1 = x1_buf[...]
             keys = nn(x1, qkv_ref[:, d : 2 * d]).astype(BF16)
             vals = (nn(x1, qkv_ref[:, 2 * d :]) + v_bias).astype(BF16)
             for p in range(pairs):
                 k_s[img * pairs + p, slot] = keys[:, p * 128 : (p + 1) * 128]
                 v_s[img * pairs + p, slot] = vals[:, p * 128 : (p + 1) * 128]
-            token_norm(reverse(jnp.minimum(n + 1, slots * 4 - 1)))
+            x1t_s[t] = x1.T
+
+        def reverse(n):
+            return n // 4 * 4 + 3 - n % 4
+
+        token_norm(jnp.int32(3), x1_s)
+        loads[0].wait()
+
+        def tokens(n, carry):
+            token_norm(reverse(2 * n + 1), x1_b)
+            token_keys(reverse(2 * n), x1_s)
+            token_norm(reverse(jnp.minimum(2 * n + 2, slots * 4 - 1)), x1_s)
+            token_keys(reverse(2 * n + 1), x1_b)
             return carry
 
-        lax.fori_loop(0, slots * 4, tokens, 0)
+        lax.fori_loop(0, slots * 2, tokens, 0)
 
         for c in gathers:
             c.wait_send()
@@ -582,8 +581,7 @@
         top = None
         for c in range(4):
             s = nt(k_s[idx, c], q_s[idx * 2 + h])
-            buf[2 * c] = s[:, :128]
-            buf[2 * c + 1] = s[:, 128:]
+            buf[c] = s
             m = jnp.max(s, axis=0, keepdims=True)
             top = m if top is None else jnp.maximum(top, m)
         top_s[h] = top
@@ -592,7 +590,7 @@
         head = idx * 2 + h
         top, total, acc = top_s[h], None, None
         for c in range(4):
-            e = jnp.exp(jnp.concatenate([buf[2 * c], buf[2 * c + 1]], axis=1) - top)
+            e = jnp.exp(buf[c] - top)
             l = col_sum(e)
             total = l if total is None else total + l
             eb = e.astype(BF16)
@@ -618,7 +616,7 @@
         c.wait()
     proj_b, fc1_b, fc2_b = row_of(proj_b_ref, 0, d), row_of(fc1_b_ref, 0, ff), row_of(fc2_b_ref, 0, d)
 
-    def closing(hat2_s, dot_s, dom_s, dq_s, dxq_s, acc_s, dx1_s):
+    def closing(dot_s, dom_s, dq_s, dxq_s, acc_s, dx1_s):
         def pair_row(k):
             return 2 * ff + k * (d + d // 3)
 
@@ -630,15 +628,17 @@
             for img in range(2, slots):
                 total = total + tn(wide(a_s, img, b), dm_s[img])
             grads_ref[rows_at(b * d, d), :] = total.astype(BF16)
-            started(b, FC)
+            started(b, 0)
             return carry
 
-        def started(b, first):
-            for k in range(1, blocks):
-
-                @pl.when(b == k)
-                def _():
-                    advance(first + k - 1, 0)
+        def started(b, before):
+            for g in range(FC, PAIR):
+                last = -(-(g + 1) * (2 * ff // 3) // d) - 1 - before
+                if 0 <= last < blocks:
+
+                    @pl.when(b == last)
+                    def _():
+                        advance(g, 0)
 
         def when_at(i, plan):
             for at, events in plan.items():
@@ -666,26 +666,33 @@
             g1 = mod_row(2)
             resid = dx_s[img] + g1 * branch
             hat2, inv2 = norm(resid)
-            hat2_s[img] = hat2
+            sa_s[img] = hat2[:, :toks]
+            sb_s[img, :, : d - toks] = hat2[:, toks:]
             inv_s[...] = jnp.where(inv_lane == slots * 4 + img, inv2, inv_s[...])
             x2 = (hat2 * (1.0 + mod_row(4)) + mod_row(3)).astype(BF16)
             x2t_s[img] = x2.T
             mlp = jnp.zeros((toks, d), F32)
             k0, k1 = 0.7978845608028654, 0.044715
+            def first(b):
+                return nn(x2, fc1_ref[:, b * d : (b + 1) * d])
+
+            u = first(0)
             for b in range(blocks):
                 at_b = slice(b * d, (b + 1) * d)
-                u = nn(x2, fc1_ref[:, at_b]) + fc1_b[:, at_b]
+                ahead = first(b + 1) if b + 1 < blocks else None
+                u = u + fc1_b[:, at_b]
                 sq = u * u
-                cdf = 0.5 + 0.5 * jnp.tanh(u * (k0 + (k0 * k1) * sq))
+                inner = k0 + (k0 * k1) * sq
+                cdf = 0.5 + 0.5 * jnp.tanh(u * inner)
                 hidden = u * cdf
-                slope = cdf + hidden * (1.0 - cdf) * ((2.0 * k0) + (6.0 * k0 * k1) * sq)
+                slope = cdf + (hidden - hidden * cdf) * (6.0 * inner - 4.0 * k0)
+                hidden = hidden.astype(BF16)
                 slope = slope.astype(BF16)
                 for j in range(3):
+                    a_s[img * 12 + b * 3 + j] = hidden[:, j * 128 : (j + 1) * 128]
                     b_s[img * 12 + b * 3 + j] = slope[:, j * 128 : (j + 1) * 128]
-                hidden = hidden.astype(BF16)
-                for j in range(3):
-                    a_s[img * 12 + b * 3 + j] = hidden[:, j * 128 : (j + 1) * 128]
                 mlp = mlp + nn(hidden, fc2_ref[at_b, :])
+                u = ahead
             mlp = mlp + fc2_b
             g2 = mod_row(5)
             x3 = resid + g2 * mlp
@@ -723,17 +730,23 @@
             def put_mod(p, v):
                 early_ref[pl.ds(E_MOD + (p - 2) * slots + img, 1), :] = v
 
-            g1, dm, hat2 = mod_row(2), dm_s[img], hat2_s[img]
+            g1, dm = mod_row(2), dm_s[img]
+            hat2 = jnp.concatenate([sa_s[img], sb_s[img, :, : d - toks]], axis=1)
             inv2 = inv_at(slots * 4 + img)
             dx2 = jnp.zeros((toks, d), F32)
+            def second(b):
+                return nt(dm, fc2_ref[b * d : (b + 1) * d, :])
+
+            dh = second(0)
             for b in range(blocks):
-                at_b = slice(b * d, (b + 1) * d)
+                ahead = second(b + 1) if b + 1 < blocks else None
                 slope = jnp.concatenate([b_s[img * 12 + b * 3 + j] for j in range(3)], axis=1).astype(F32)
-                du = (nt(dm, fc2_ref[at_b, :]) * slope).astype(BF16)
+                du = (dh * slope).astype(BF16)
                 for j in range(3):
                     b_s[img * 12 + b * 3 + j] = du[:, j * 128 : (j + 1) * 128]
                 early_ref[E_FC1_B + b : E_FC1_B + b + 1, :] += col_sum(du.astype(F32))
-                dx2 = dx2 + nt(du, fc1_ref[:, at_b])
+                dx2 = dx2 + nt(du, fc1_ref[:, b * d : (b + 1) * d])
+                dh = ahead
             put_mod(3, col_sum(dx2))
             put_mod(4, col_sum(dx2 * hat2))
             dx = dx_s[img] + norm_back(hat2, inv2, dx2 * (1.0 + mod_row(4)))
@@ -765,7 +778,7 @@
             for img in range(2, slots):
                 total = total + nn(x2t_s[img], wide(b_s, img, b))
             grads_ref[rows_at(ff + b * d, d), :] = total.astype(BF16)
-            started(b, FC + blocks - 1)
+            started(b, blocks)
             return carry
 
         lax.fori_loop(0, blocks, fc1_grad, 0)
@@ -780,9 +793,8 @@
         for i in range(slots):
             out = shift_out([edge_s[4, i], blank, blank, blank], masks)
             for s in range(4):
-                edge_y[s, i * 16 : (i + 1) * 16, :] = out[s].astype(BF16)
+                edge_l[s, 1, i * 16 : (i + 1) * 16, :] = out[s].astype(BF16)
         early_16[...] = early_ref[...].astype(BF16)
-        advance(EDGE_Y, 0)
         advance(EARLY, 0)
 
         acc_s[...] = jnp.zeros_like(acc_s)
@@ -871,9 +883,10 @@
             own = jnp.where(slot == 0, 1.0, 0.0)
             dtok = norm_back(hat, inv_at(t), dx1 * (1.0 + mod_s[1, pl.ds(img, 1), :])) + dx_s[img] * own
             late_ref[L_PATCH_B : L_PATCH_B + 1, :] += col_sum(dtok)
-            hi, lo = parts(dtok, 2)
-            late_ref[L_PATCH : L_PATCH + 16, :] += nn(pt_s[t], hi) + nn(pt_s[t], lo)
-            edge_s[slot, img] = nt(wp_s[...], hi) + nt(wp_s[...], lo)
+            dtok = dtok.astype(BF16)
+            late_ref[L_PATCH : L_PATCH + 16, :] += nn(pt_s[t], dtok)
+            for p in range(pairs):
+                a_s[(img * pairs + p) * 4 + slot] = dtok[:, p * 128 : (p + 1) * 128]
             dx1_s[...] = ahead
             return carry
 
@@ -881,7 +894,6 @@
 
     pl.run_scoped(
         closing,
-        pltpu.VMEM((slots, toks, d), F32),
         pltpu.VMEM((slots * HEADS, 128, toks), BF16),
         pltpu.VMEM((slots * HEADS, toks, 128), BF16),
         pltpu.VMEM((slots * pairs, toks, 128), BF16),
@@ -892,24 +904,37 @@
 
     late_16[...] = late_ref[...].astype(BF16)
     advance(LATE, 0)
+
+    def edges(t, carry):
+        img, slot = t // 4, t % 4
+        dtok = jnp.concatenate([a_s[(img * pairs + p) * 4 + slot] for p in range(pairs)], axis=1)
+        edge_s[slot, img] = nt(wp_s[...], dtok)
+        return carry
+
+    lax.fori_loop(0, slots * 4, edges, 0)
     for i in range(slots):
         lat = shift_out([edge_s[s, i] for s in range(4)], masks)
         for s in range(4):
-            edge_l[s, i * 16 : (i + 1) * 16, :] = lat[s].astype(BF16)
+            edge_l[s, 0, i * 16 : (i + 1) * 16, :] = lat[s].astype(BF16)
     advance(EDGE_L, 0)
     state = {g: 1 for g in (LATE, EDGE_L)}
-    for g in (*range(FC, PAIR + 3), EARLY, EDGE_Y):
+    for g in (*range(FC, PAIR + 3), EARLY):
         done = [k for events in (IMAGE_EVENTS, GRAD_EVENTS, BACK_EVENTS, TAIL_EVENTS) for _, h, k in events if h == g]
         assert done == list(range(1, len(done) + 1))
         state[g] = len(done) + 1
-    order = [LATE, EDGE_L, LATE] + [g for g, _ in END_EVENTS]
+    order = list(END_EVENTS)
     order += [g for g in state for _ in range(len(groups[g]))]
+    drained = {g: 0 for g in state}
     for g in order:
         if state[g] <= len(groups[g]):
+            for h, stages in enumerate(groups):
+                while drained[h] < state[h] - 1 - (h == g):
+                    stages[drained[h]].drain()
+                    drained[h] += 1
             advance(g, state[g])
             state[g] += 1
-    for stages in groups:
-        for stage in stages:
+    for h, stages in enumerate(groups):
+        for stage in stages[drained[h] :]:
             stage.drain()
     assert len(net.known) <= count
 
@@ -931,16 +956,15 @@
     )
     scratch = [(w.shape, w.dtype) for w in bigs[4:]] + [
         ((4, 2, planes, toks), BF16), ((8, 8, d), F32), ((slots * 4, 16, toks), BF16),
-        ((slots, 16, toks), BF16), ((16, d), BF16), ((16, d), BF16), ((toks, d), BF16), ((slots * 4, d, toks), BF16),
+        ((slots, 16, toks), BF16), ((16, d), BF16), ((16, d), BF16), ((toks, d), BF16), ((toks, d), BF16), ((slots * 4, d, toks), BF16),
         ((slots * 4, toks, d), F32), ((toks, 128), F32), ((slots * pairs, 4, toks, 128), BF16),
         ((slots * pairs, 4, toks, 128), BF16), ((heads, toks, 128), BF16), ((heads, 4, toks, toks), BF16),
-        ((8, toks, 128), F32), ((8, toks, 128), F32), ((2, 1, toks), F32), ((heads, 1, toks), F32), ((heads, 1, toks), F32),
+        ((4, toks, toks), F32), ((4, toks, toks), F32), ((2, 1, toks), F32), ((heads, 1, toks), F32), ((heads, 1, toks), F32),
         ((heads, 64, toks), F32), ((slots * 12, toks, 128), BF16), ((slots * 12, toks, 128), BF16),
         ((slots, toks, d), BF16), ((slots, d, toks), BF16), ((slots, toks, d), BF16),
         ((slots, toks, d), F32), ((5, slots, 16, toks), F32),
-        ((2 * ff + 4 * d, d), BF16), ((E_ROWS, d), F32), ((L_ROWS, d), F32), ((E_ROWS, d), BF16), ((L_ROWS, d), BF16), ((4, planes, toks), BF16), ((4, planes, toks), BF16),
-        ((3, E_ROWS, d), BF16), ((E_ROWS, d), BF16), ((3, L_ROWS, d), BF16), ((L_ROWS, d), BF16), ((3, planes, toks), BF16),
-        ((3, planes, toks), BF16),
+        ((2 * ff + 4 * d, d), BF16), ((E_ROWS, d), F32), ((L_ROWS, d), F32), ((E_ROWS, d), BF16), ((L_ROWS, d), BF16), ((4, 2, planes, toks), BF16),
+        ((3, E_ROWS, d), BF16), ((E_ROWS, d), BF16), ((3, L_ROWS, d), BF16), ((L_ROWS, d), BF16), ((3, 2, planes, toks), BF16),
     ]
     dma = pltpu.SemaphoreType.DMA
     parts_of = group_list(d, ff)
@@ -1011,13 +1035,24 @@
     all_early = early_ref[...].reshape(groups * E_ROWS, d)
     all_late = late_ref[...].reshape(groups * L_ROWS, d)
 
-    def chosen(block, rows, at):
-        out_row, src = iota((held, groups * rows), 0), iota((held, groups * rows), 1)
-        sel = (out_row < images) & (src // rows == out_row // slots) & (src % rows == at(out_row % slots))
-        return nn(flag(sel).astype(BF16), block)
-
-    cond = chosen(all_early, E_ROWS, lambda i: E_COND + i) + chosen(all_early, E_ROWS, lambda i: E_COND + slots + i)
-    ids = chosen(all_early, E_ROWS, lambda i: E_IDS)
+    def chosen(block, rows, starts, steps):
+        many = len(starts) * held
+        line = iota((many, 1), 0)
+        image = line % held
+        item = line // held
+        start, step = jnp.zeros_like(line), jnp.zeros_like(line)
+        for k, (at, by) in enumerate(zip(starts, steps)):
+            start = jnp.where(item == k, at, start)
+            step = jnp.where(item == k, by, step)
+        want = jnp.where(image < images, image // slots * rows + start + step * (image % slots), -1)
+        return nn(flag(iota((many, groups * rows), 1) == want).astype(BF16), block)
+
+    starts = [E_COND, E_COND + slots, E_IDS] + [E_MOD + k * slots for k in range(6)]
+    picked = chosen(all_early, E_ROWS, starts, [1, 1, 0] + [1] * 6)
+    items = [picked[k * held : (k + 1) * held] for k in range(9)]
+    cond, ids = items[0] + items[1], items[2]
+    picked = chosen(all_late, L_ROWS, [L_MOD, L_MOD + slots], [1, 1])
+    dmods = [picked[:held], picked[held:]] + items[3:]
     img_row, lane = iota((held, d), 0), iota((held, d), 1)
 
     def id_part(k):
@@ -1025,40 +1060,35 @@
 
     time_id, class_id = id_part(0), 256.0 * id_part(1) + id_part(2)
 
-    a1, a2, a3 = parts(swish(cond), 3)
-    left = jnp.concatenate([a1, a2, a3], axis=0).T
+    left = jnp.concatenate(parts(swish(cond), 2), axis=0).T
     loads[3].wait()
     loads[4].wait()
     dact = jnp.zeros((held, d), F32)
-    bias_rows = []
-    for p in range(8):
-        if p < 2:
-            dmod = chosen(all_late, L_ROWS, lambda i: L_MOD + p * slots + i)
+    for p in range(0, 8, 2):
+        pair = jnp.concatenate([dmods[p], dmods[p + 1]], axis=1).astype(BF16)
+        grad = nn(left, jnp.concatenate([pair, pair], axis=0))
+        if p < 6:
+            lanes = slice(p * d, (p + 2) * d)
+            ada_g_ref[:, lanes] = grad
+            w = ada_ref[:, lanes]
         else:
-            dmod = chosen(all_early, E_ROWS, lambda i: E_MOD + (p - 2) * slots + i)
-        dmod16 = dmod.astype(BF16)
-        grad = nn(left, jnp.concatenate([dmod16] * 3, axis=0))
-        if p < 6:
-            ada_g_ref[:, p * d : (p + 1) * d] = grad
-            w = ada_ref[:, p * d : (p + 1) * d]
-        else:
-            fada_g_ref[:, (p - 6) * d : (p - 5) * d] = grad
-            w = fada_ref[:, (p - 6) * d : (p - 5) * d]
-        bias_rows.append(col_sum(dmod))
-        dact = dact + nt(dmod16, w)
-        if p == 5:
+            fada_g_ref[...] = grad
+            w = fada_ref[...]
+        dact = dact + nt(pair, w)
+        if p == 4:
             send(ada_g_ref, ada_g_hbm)
     send(fada_g_ref, fada_g_hbm)
+    bias_rows = [col_sum(v) for v in dmods]
     ada_b_ref[...] = jnp.concatenate(bias_rows[:6], axis=1).reshape(6 * d)
     fada_b_ref[...] = jnp.concatenate(bias_rows[6:], axis=1).reshape(2 * d)
     sig = 1.0 / (1.0 + jnp.exp(-cond))
     dcond = dact * (sig * (1.0 + cond * (1.0 - sig)))
-    stack = jnp.concatenate(parts(dcond, 3), axis=0)
+    stack = jnp.concatenate(parts(dcond, 2), axis=0)
     for ref, ids_col, many in ((class_ref, class_id, classes), (time_ref, time_id, bins)):
         wide = -(-many // 128) * 128
         at = iota((held, wide), 1).astype(F32)
         hit = flag((at == ids_col) & (iota((held, wide), 0) < images)).astype(BF16)
-        ref[...] = tn(jnp.concatenate([hit, hit, hit], axis=0), stack)[:many]
+        ref[...] = tn(jnp.concatenate([hit, hit], axis=0), stack)[:many]
         if many == classes:
             send(class_ref, class_hbm)
 

time: 126 us -> 114 us (0.905)
  Pallas kernels: 125 us -> 113 us
    pallas_call x1, Pallas kernels: 115 us -> 103 us  [step(): pl.pallas_call(functools.partial(step_kernel, images, count), out_shape=o...]
where the time goes in v4:
time: 114 us; the launch traced here: 113 us
  Pallas kernels  113 us (99%)
    pallas_call x1, Pallas kernels, step(): pl.pallas_call(functools.partial(step_kernel, images, count), out_shape=o...  103 us
    pallas_call x1, Pallas kernels, finish(): pl.pallas_call(functools.partial(finish_kernel, bins, classes), out_shape...  9.27 us

profile of v4, /device:TPU:0, one launch (start us, length us, event | category | flops | bytes accessed | tf_op | source)
XLA Modules:
  0.0 113.3 jit_solution(12671259015672423148)
XLA Ops:
  0.7 103.2 %step.1 = (bf16[4608,384]{1,0:T(8,128)(2,1)}, bf16[8,48,384]{2,1,0:T(8,128)(2,1)}, bf16[8,32,384]{2,1,0:T(8,128)(2,1)}, f32[2,48,256]{2,1,0:T(8,128)}) custom-call(s32[3]{0:T(128)} %refs_0_.1, s32[3]{0:T(128)} %refs_1_.1, s32[3]{0:T(128)} %refs_2_.1, bf16[3,4,32,32]{3,2,1,0:T(8,128)(2,1)} %refs_3_.1, bf16[3,4,32,32]{3,2,1,0:T(8,128)(2,1)} %refs_4_.1, ...), custom_call_target="tpu_custom_call" | custom-call | tf_op jit(solution)/shard_map/step/pallas_call | solution.py:973
  103.9 9.3 %finish.1 = (bf16[3,4,32,32]{3,2,1,0:T(8,128)(2,1)}, f32[3,4,32,32]{3,2,1,0:T(8,128)}, f32[100,384]{1,0:T(8,128)}, f32[1001,384]{1,0:T(8,128)}, f32[16,384]{1,0:...) custom-call(bf16[4608,384]{1,0:T(8,128)(2,1)} %get-tuple-element.44., ...), custom_call_target="tpu_custom_call" | custom-call | tf_op jit(solution)/shard_map/finish/pallas_call | solution.py:1141

commit v5 on v4

--- a/solution.py
+++ b/solution.py
@@ -368,12 +368,12 @@
 
 
 SLOW = (("c", "r", "0", "12"), ("c", "0", "1", "r2"), ("c", "1", "r", "02"))
-FAST = (("c", "r0", "12"), ("c", "01", "r2"), ("c", "r1", "02"))
+FAST = (("c", "r0", "12"), ("c", "01", "r2"), ("c", "r012"))
 FC, PAIR, EARLY, LATE, EDGE_L = 0, 3, 6, 7, 8
 IMAGE_EVENTS = ((2, 0, 1),)
 GRAD_EVENTS = ()
 BACK_EVENTS = ((1, 0, 2), (1, 1, 1), (1, 2, 1), (3, 0, 3), (3, 6, 1), (4, 1, 2), (4, 2, 2), (5, 0, 4), (5, 3, 1), (6, 1, 3), (6, 2, 3), (7, 0, 5), (7, 3, 2), (8, 1, 4), (8, 2, 4), (8, 4, 1), (8, 6, 2))
-TAIL_EVENTS = ((0, 0, 6), (0, 3, 3), (2, 1, 5), (2, 2, 5), (4, 5, 1), (8, 0, 7), (8, 1, 6), (8, 2, 6), (8, 3, 4), (8, 4, 2), (11, 0, 8), (11, 5, 2))
+TAIL_EVENTS = ((0, 0, 6), (0, 3, 3), (2, 1, 5), (2, 2, 5), (4, 5, 1), (8, 0, 7), (8, 1, 6), (8, 2, 6), (8, 3, 4), (8, 4, 2), (11, 0, 8))
 END_EVENTS = (4, 3, 5, 1, 2, 7, 8, 4, 3, 1, 2, 5, 7, 4, 5, 4, 5)
 
 
@@ -985,12 +985,12 @@
     )(*smalls, *bigs)
 
 
-def finish_kernel(
-    bins, classes, grads_hbm, early_ref, late_ref, planes_ref, ada_hbm, fada_hbm,
-    out_ref, lat_ref, time_ref, class_hbm, patch_ref, patch_b_ref, ada_g_hbm, ada_b_ref, qkv_g_hbm, qv_b_ref, proj_g_ref,
-    proj_b_ref, fc1_g_hbm, fc1_b_ref, fc2_g_hbm, fc2_b_ref, fada_g_hbm, fada_b_ref, out_gt_ref, out_b_ref,
-    grads_ref, ada_ref, fada_ref, class_ref, ada_g_ref, qkv_g_ref, fc1_g_ref, fc2_g_ref, fada_g_ref, in_sem, out_sem,
-):
+def finish_kernel(bins, classes, *refs):
+    hbm_in, hbm_out, refs = refs[:6], refs[6:26], refs[26:]
+    grads_ref, early_ref, late_ref, planes_ref, ada_ref, fada_ref = refs[:6]
+    (out_ref, lat_ref, time_ref, class_ref, patch_ref, patch_b_ref, ada_g_ref, ada_b_ref, qkv_g_ref, qv_b_ref, proj_g_ref,
+     proj_b_ref, fc1_g_ref, fc1_b_ref, fc2_g_ref, fc2_b_ref, fada_g_ref, fada_b_ref, out_gt_ref, out_b_ref) = outs = refs[6:26]
+    in_sem, out_sem = refs[26:]
     d = ada_ref.shape[0]
     ff = fc1_g_ref.shape[1]
     blocks = ff // d
@@ -1000,37 +1000,32 @@
     images = groups * slots
     held = -(-images // 32) * 32
 
-    bounds = [0, ff, 2 * ff, 2 * ff + 4 * d]
-    loads = [
-        pltpu.make_async_copy(grads_hbm.at[a:b, :], grads_ref.at[a:b, :], in_sem.at[i])
-        for i, (a, b) in enumerate(zip(bounds[:-1], bounds[1:]))
-    ]
-    loads += [pltpu.make_async_copy(ada_hbm, ada_ref, in_sem.at[3]), pltpu.make_async_copy(fada_hbm, fada_ref, in_sem.at[4])]
-    for c in loads:
+    loads = []
+
+    def fetch(src, dst):
+        c = pltpu.make_async_copy(src, dst, in_sem.at[len(loads)])
         c.start()
+        loads.append(c)
+
+    for k in (1, 2):
+        fetch(hbm_in[k], refs[k])
+    bounds = [b * d for b in range(2 * blocks + 1)] + [2 * ff + 4 * d]
+    for a, b in zip(bounds[:-1], bounds[1:]):
+        fetch(hbm_in[0].at[a:b, :], grads_ref.at[a:b, :])
+    for k in (4, 5, 3):
+        fetch(hbm_in[k], refs[k])
     stores = []
 
-    def send(src, dst):
+    def send(k, *at):
+        src, dst = outs[k], hbm_out[k]
+        if at:
+            src, dst = src.at[at], dst.at[at]
         c = pltpu.make_async_copy(src, dst, out_sem.at[len(stores)])
         c.start()
         stores.append(c)
 
     loads[0].wait()
-    fc2_g_ref[...] = grads_ref[0:ff, :].astype(F32)
-    send(fc2_g_ref, fc2_g_hbm)
     loads[1].wait()
-    for b in range(blocks):
-        fc1_g_ref[:, b * d : (b + 1) * d] = grads_ref[ff + b * d : ff + (b + 1) * d, :].astype(F32)
-    send(fc1_g_ref, fc1_g_hbm)
-    loads[2].wait()
-    third = d // 3
-    for p in range(pairs):
-        at = 2 * ff + p * (d + third)
-        proj_g_ref[p * third : (p + 1) * third, :] = grads_ref[at + d : at + d + third, :].astype(F32)
-        for k in range(3):
-            lanes = slice(k * d + p * 128, k * d + (p + 1) * 128)
-            qkv_g_ref[:, lanes] = grads_ref[at : at + d, k * 128 : (k + 1) * 128].astype(F32)
-    send(qkv_g_ref, qkv_g_hbm)
 
     all_early = early_ref[...].reshape(groups * E_ROWS, d)
     all_late = late_ref[...].reshape(groups * L_ROWS, d)
@@ -1061,23 +1056,44 @@
     time_id, class_id = id_part(0), 256.0 * id_part(1) + id_part(2)
 
     left = jnp.concatenate(parts(swish(cond), 2), axis=0).T
-    loads[3].wait()
-    loads[4].wait()
-    dact = jnp.zeros((held, d), F32)
-    for p in range(0, 8, 2):
-        pair = jnp.concatenate([dmods[p], dmods[p + 1]], axis=1).astype(BF16)
+    pairs_of = [jnp.concatenate([dmods[p], dmods[p + 1]], axis=1).astype(BF16) for p in range(0, 8, 2)]
+    for k, pair in enumerate(pairs_of):
         grad = nn(left, jnp.concatenate([pair, pair], axis=0))
-        if p < 6:
-            lanes = slice(p * d, (p + 2) * d)
+        if k < 3:
+            lanes = slice(2 * k * d, 2 * (k + 1) * d)
             ada_g_ref[:, lanes] = grad
-            w = ada_ref[:, lanes]
+            send(6, slice(None), lanes)
         else:
             fada_g_ref[...] = grad
-            w = fada_ref[...]
+            send(16)
+
+    for b in range(blocks):
+        at = slice(b * d, (b + 1) * d)
+        loads[2 + b].wait()
+        fc2_g_ref[at, :] = grads_ref[at, :].astype(F32)
+        send(14, at, slice(None))
+    for b in range(blocks):
+        at = slice(b * d, (b + 1) * d)
+        loads[2 + blocks + b].wait()
+        fc1_g_ref[:, at] = grads_ref[ff + b * d : ff + (b + 1) * d, :].astype(F32)
+        send(12, slice(None), at)
+    loads[2 + 2 * blocks].wait()
+    third = d // 3
+    for p in range(pairs):
+        at = 2 * ff + p * (d + third)
+        proj_g_ref[p * third : (p + 1) * third, :] = grads_ref[at + d : at + d + third, :].astype(F32)
+        for k in range(3):
+            lanes = slice(k * d + p * 128, k * d + (p + 1) * 128)
+            qkv_g_ref[:, lanes] = grads_ref[at : at + d, k * 128 : (k + 1) * 128].astype(F32)
+    send(8)
+    send(10)
+
+    for c in loads[3 + 2 * blocks :]:
+        c.wait()
+    dact = jnp.zeros((held, d), F32)
+    for k, pair in enumerate(pairs_of):
+        w = ada_ref[:, 2 * k * d : 2 * (k + 1) * d] if k < 3 else fada_ref[...]
         dact = dact + nt(pair, w)
-        if p == 4:
-            send(ada_g_ref, ada_g_hbm)
-    send(fada_g_ref, fada_g_hbm)
     bias_rows = [col_sum(v) for v in dmods]
     ada_b_ref[...] = jnp.concatenate(bias_rows[:6], axis=1).reshape(6 * d)
     fada_b_ref[...] = jnp.concatenate(bias_rows[6:], axis=1).reshape(2 * d)
@@ -1089,8 +1105,8 @@
         at = iota((held, wide), 1).astype(F32)
         hit = flag((at == ids_col) & (iota((held, wide), 0) < images)).astype(BF16)
         ref[...] = tn(jnp.concatenate([hit, hit], axis=0), stack)[:many]
-        if many == classes:
-            send(class_ref, class_hbm)
+    send(3)
+    send(2)
 
     early, late = jnp.sum(early_ref[...].astype(F32), axis=0), jnp.sum(late_ref[...].astype(F32), axis=0)
     swap = flag(iota((16, 16), 0) == (iota((16, 16), 1) ^ 3)).astype(BF16)
@@ -1116,14 +1132,19 @@
 
     half = side // 2
     keep, spread, pick = plane_maps(slots, chans, side, half)
+    for k in (4, 5, 7, 9, 11, 13, 15, 17, 18, 19):
+        send(k)
     for k, ref in ((0, lat_ref), (1, out_ref)):
-        total = None
-        for piece in parts(planes_ref[k], 3 if k == 0 else 1):
-            for j in range(2):
-                wide = (tn(pick[j], piece) * keep).astype(BF16)
-                term = nt(wide, spread[j])
-                total = term if total is None else total + term
+        many = 2 - k
+        planes = jnp.concatenate(parts(planes_ref[k], many), axis=0)
+        pieces, maps = [], []
+        for j in range(2):
+            wide = tn(jnp.concatenate([pick[j]] * many, axis=0), planes) * keep
+            pieces += parts(wide, many)
+            maps += [spread[j]] * many
+        total = nt(jnp.concatenate(pieces, axis=1), jnp.concatenate(maps, axis=1))
         ref[...] = total.reshape(ref.shape).astype(ref.dtype)
+        send(1 - k)
     for c in stores:
         c.wait()
 
@@ -1136,19 +1157,18 @@
         f(d, 6 * d), f(6 * d), f(d, 3 * d), f(2 * d), f(d, d), f(d), f(d, ff), f(ff), f(ff, d), f(d), f(d, 2 * d), f(2 * d),
         f(16, d), f(16),
     )
-    large = (3, 6, 8, 12, 14, 16)
+    ins = (grads, early, late, planes, ada_weight, fada_weight)
     dma = pltpu.SemaphoreType.DMA
     return pl.pallas_call(
         functools.partial(finish_kernel, bins, classes),
         out_shape=out_shape,
-        in_specs=[ANY] + [VMEM] * 3 + [ANY] * 2,
-        out_specs=tuple(ANY if i in large else VMEM for i in range(len(out_shape))),
-        scratch_shapes=[pltpu.VMEM(x.shape, x.dtype) for x in (grads, ada_weight, fada_weight)]
-        + [pltpu.VMEM(out_shape[i].shape, F32) for i in large]
-        + [dma((5,)), dma((len(large),))],
+        in_specs=[ANY] * 6,
+        out_specs=(ANY,) * len(out_shape),
+        scratch_shapes=[pltpu.VMEM(x.shape, x.dtype) for x in ins + out_shape]
+        + [dma((6 + 2 * (ff // d),)), dma((20 + 2 * (ff // d),))],
         compiler_params=pltpu.CompilerParams(vmem_limit_bytes=60 * 1024 * 1024),
         name="finish",
-    )(grads, early, late, planes, ada_weight, fada_weight)
+    )(*ins)
 
 
 def local(

time: 114 us -> 111 us (0.974)
  Pallas kernels: 113 us -> 110 us
    pallas_call x1, Pallas kernels: 9.27 us -> 7.02 us  [finish(): pl.pallas_call(functools.partial(finish_kernel, bins, classes), out_shape...]
where the time goes in v5:
time: 111 us
  Pallas kernels  110 us (99%)
    pallas_call x1, Pallas kernels, step(): pl.pallas_call(functools.partial(step_kernel, images, count), out_shape=o...  103 us
    pallas_call x1, Pallas kernels, finish(): pl.pallas_call(functools.partial(finish_kernel, bins, classes), out_shape...  7.02 us

profile of v5, /device:TPU:0, one launch (start us, length us, event | category | flops | bytes accessed | tf_op | source)
XLA Modules:
  0.0 110.9 jit_solution(9337102501672347283)
XLA Ops:
  0.7 103.1 %step.1 = (bf16[4608,384]{1,0:T(8,128)(2,1)}, bf16[8,48,384]{2,1,0:T(8,128)(2,1)}, bf16[8,32,384]{2,1,0:T(8,128)(2,1)}, f32[2,48,256]{2,1,0:T(8,128)}) custom-call(s32[3]{0:T(128)} %refs_0_.1, s32[3]{0:T(128)} %refs_1_.1, s32[3]{0:T(128)} %refs_2_.1, bf16[3,4,32,32]{3,2,1,0:T(8,128)(2,1)} %refs_3_.1, bf16[3,4,32,32]{3,2,1,0:T(8,128)(2,1)} %refs_4_.2, ...), custom_call_target="tpu_custom_call" | custom-call | tf_op jit(solution)/shard_map/step/pallas_call | solution.py:973
  103.7 7.0 %finish.1 = (bf16[3,4,32,32]{3,2,1,0:T(8,128)(2,1)}, f32[3,4,32,32]{3,2,1,0:T(8,128)}, f32[100,384]{1,0:T(8,128)}, f32[1001,384]{1,0:T(8,128)}, f32[16,384]{1,0:...) custom-call(bf16[4608,384]{1,0:T(8,128)(2,1)} %get-tuple-element.44., ...), custom_call_target="tpu_custom_call" | custom-call | tf_op jit(solution)/shard_map/finish/pallas_call | solution.py:1162

commit v6 on v5

--- a/solution.py
+++ b/solution.py
@@ -372,9 +372,9 @@
 FC, PAIR, EARLY, LATE, EDGE_L = 0, 3, 6, 7, 8
 IMAGE_EVENTS = ((2, 0, 1),)
 GRAD_EVENTS = ()
-BACK_EVENTS = ((1, 0, 2), (1, 1, 1), (1, 2, 1), (3, 0, 3), (3, 6, 1), (4, 1, 2), (4, 2, 2), (5, 0, 4), (5, 3, 1), (6, 1, 3), (6, 2, 3), (7, 0, 5), (7, 3, 2), (8, 1, 4), (8, 2, 4), (8, 4, 1), (8, 6, 2))
-TAIL_EVENTS = ((0, 0, 6), (0, 3, 3), (2, 1, 5), (2, 2, 5), (4, 5, 1), (8, 0, 7), (8, 1, 6), (8, 2, 6), (8, 3, 4), (8, 4, 2), (11, 0, 8))
-END_EVENTS = (4, 3, 5, 1, 2, 7, 8, 4, 3, 1, 2, 5, 7, 4, 5, 4, 5)
+BACK_EVENTS = ((1, 0, 2), (1, 1, 1), (1, 2, 1), (3, 0, 3), (3, 6, 1), (4, 1, 2), (4, 2, 2), (5, 0, 4), (5, 3, 1), (6, 1, 3), (6, 2, 3), (8, 0, 5), (8, 3, 2), (8, 4, 1), (8, 6, 2))
+TAIL_EVENTS = ((0, 1, 4), (0, 2, 4), (2, 0, 6), (4, 3, 3), (4, 5, 1), (6, 1, 5), (6, 2, 5), (8, 4, 2))
+END_EVENTS = (0, 3, 1, 2, 4, 5, 0, 7, 8, 3, 1, 2, 4, 3, 7, 1, 2, 5, 5, 4, 4)
 
 
 def group_list(d, ff):
@@ -671,7 +671,7 @@
             inv_s[...] = jnp.where(inv_lane == slots * 4 + img, inv2, inv_s[...])
             x2 = (hat2 * (1.0 + mod_row(4)) + mod_row(3)).astype(BF16)
             x2t_s[img] = x2.T
-            mlp = jnp.zeros((toks, d), F32)
+            hiddens = []
             k0, k1 = 0.7978845608028654, 0.044715
             def first(b):
                 return nn(x2, fc1_ref[:, b * d : (b + 1) * d])
@@ -691,8 +691,9 @@
                 for j in range(3):
                     a_s[img * 12 + b * 3 + j] = hidden[:, j * 128 : (j + 1) * 128]
                     b_s[img * 12 + b * 3 + j] = slope[:, j * 128 : (j + 1) * 128]
-                mlp = mlp + nn(hidden, fc2_ref[at_b, :])
+                hiddens.append(hidden)
                 u = ahead
+            mlp = nn(jnp.concatenate(hiddens, axis=1), fc2_ref[...])
             mlp = mlp + fc2_b
             g2 = mod_row(5)
             x3 = resid + g2 * mlp
@@ -733,7 +734,7 @@
             g1, dm = mod_row(2), dm_s[img]
             hat2 = jnp.concatenate([sa_s[img], sb_s[img, :, : d - toks]], axis=1)
             inv2 = inv_at(slots * 4 + img)
-            dx2 = jnp.zeros((toks, d), F32)
+            dus = []
             def second(b):
                 return nt(dm, fc2_ref[b * d : (b + 1) * d, :])
 
@@ -745,8 +746,9 @@
                 for j in range(3):
                     b_s[img * 12 + b * 3 + j] = du[:, j * 128 : (j + 1) * 128]
                 early_ref[E_FC1_B + b : E_FC1_B + b + 1, :] += col_sum(du.astype(F32))
-                dx2 = dx2 + nt(du, fc1_ref[:, b * d : (b + 1) * d])
+                dus.append(du)
                 dh = ahead
+            dx2 = nt(jnp.concatenate(dus, axis=1), fc1_ref[...])
             put_mod(3, col_sum(dx2))
             put_mod(4, col_sum(dx2 * hat2))
             dx = dx_s[img] + norm_back(hat2, inv2, dx2 * (1.0 + mod_row(4)))
@@ -809,12 +811,13 @@
             def product(job):
                 return nn(v_s[idx, job[0]], dot_s[idx * 2 + job[1]])
 
-            dp = product(jobs[0])
+            dp, soon = product(jobs[0]), product(jobs[1])
             gathered = None
             sum_v = None
+            dkv = []
             for n, (c, h) in enumerate(jobs):
                 head = idx * 2 + h
-                ahead = product(jobs[n + 1]) if n + 1 < len(jobs) else None
+                ahead = product(jobs[n + 2]) if n + 2 < len(jobs) else None
                 if h == 0:
                     kt = k_s[idx, c].T
                     dk, dv = None, None
@@ -825,15 +828,16 @@
                 dv = dv_h if dv is None else dv + dv_h
                 dq_h = nn(kt[h * 64 : (h + 1) * 64], ds)
                 dqt[h] = dq_h if dqt[h] is None else dqt[h] + dq_h
-                dp = ahead
+                dp, soon = soon, ahead
                 if h == 1:
                     dk, dv = dk.astype(BF16), dv.astype(BF16)
                     a_s[idx * 4 + c] = dk
                     b_s[idx * 4 + c] = dv
                     sv = col_sum(dv.astype(F32))
                     sum_v = sv if sum_v is None else sum_v + sv
-                    term = nn(x1t_s[img * 4 + c], jnp.concatenate([dk, dv], axis=1))
-                    gathered = term if gathered is None else gathered + term
+                    dkv.append(jnp.concatenate([dk, dv], axis=1))
+            x1t = jnp.concatenate([x1t_s[img * 4 + c] for c in range(4)], axis=1)
+            gathered = nn(x1t, jnp.concatenate(dkv, axis=0))
             dq = (jnp.concatenate(dqt, axis=0) * 0.125).T.astype(BF16)
             dq_s[idx] = dq
             lanes = pl.ds(pl.multiple_of(p * 128, 128), 128)

time: 111 us -> 109 us (0.982)
  Pallas kernels: 110 us -> 108 us
    pallas_call x1, Pallas kernels: 103 us -> 101 us  [step(): pl.pallas_call(functools.partial(step_kernel, images, count), out_shape=o...]
where the time goes in v6:
time: 109 us
  Pallas kernels  108 us (99%)
    pallas_call x1, Pallas kernels, step(): pl.pallas_call(functools.partial(step_kernel, images, count), out_shape=o...  101 us
    pallas_call x1, Pallas kernels, finish(): pl.pallas_call(functools.partial(finish_kernel, bins, classes), out_shape...  7.02 us

profile of v6, /device:TPU:0, one launch (start us, length us, event | category | flops | bytes accessed | tf_op | source)
XLA Modules:
  0.0 109.0 jit_solution(6626665149865942582)
XLA Ops:
  0.7 101.2 %step.1 = (bf16[4608,384]{1,0:T(8,128)(2,1)}, bf16[8,48,384]{2,1,0:T(8,128)(2,1)}, bf16[8,32,384]{2,1,0:T(8,128)(2,1)}, f32[2,48,256]{2,1,0:T(8,128)}) custom-call(s32[3]{0:T(128)} %refs_0_.1, s32[3]{0:T(128)} %refs_1_.1, s32[3]{0:T(128)} %refs_2_.1, bf16[3,4,32,32]{3,2,1,0:T(8,128)(2,1)} %refs_3_.1, bf16[3,4,32,32]{3,2,1,0:T(8,128)(2,1)} %refs_4_.2, ...), custom_call_target="tpu_custom_call" | custom-call | tf_op jit(solution)/shard_map/step/pallas_call | solution.py:977
  101.9 7.0 %finish.1 = (bf16[3,4,32,32]{3,2,1,0:T(8,128)(2,1)}, f32[3,4,32,32]{3,2,1,0:T(8,128)}, f32[100,384]{1,0:T(8,128)}, f32[1001,384]{1,0:T(8,128)}, f32[16,384]{1,0:...) custom-call(bf16[4608,384]{1,0:T(8,128)(2,1)} %get-tuple-element.44., ...), custom_call_target="tpu_custom_call" | custom-call | tf_op jit(solution)/shard_map/finish/pallas_call | solution.py:1166

commit v7 on v6

--- a/solution.py
+++ b/solution.py
@@ -138,13 +138,6 @@
     return {"row": row ^ (slot >> 1), "col": col ^ (slot & 1)}
 
 
-def greet(devices):
-    barrier = pltpu.get_barrier_semaphore()
-    for device in devices:
-        pl.semaphore_signal(barrier, inc=1, device_id=device, device_id_type=MESH)
-    pl.semaphore_wait(barrier, len(devices))
-
-
 def norm(v):
     share = 1.0 / v.shape[-1]
     centred = v - jnp.sum(v, axis=-1, keepdims=True) * share
@@ -450,7 +443,10 @@
         ]
         for c in tables + loads:
             c.start()
-        greet([mate(s) for s in (1, 2, 3)] + [far(k) for k in range(1, images)])
+        peers = [mate(s) for s in (1, 2, 3)] + [far(k) for k in range(1, images)]
+        barrier = pltpu.get_barrier_semaphore()
+        for peer in peers:
+            pl.semaphore_signal(barrier, inc=1, device_id=peer, device_id_type=MESH)
         keep, spread, pick = plane_maps(slots, chans, side, half)
         for k, ref in enumerate((lat_ref, cot_ref)):
             tile = ref[...].reshape(slots * chans * side, side)
@@ -460,6 +456,7 @@
                 term = nn(pick[j], wide)
                 total = term if total is None else total + term
             planes_ref[0, k] = total.astype(BF16)
+        pl.semaphore_wait(barrier, len(peers))
         gathers = []
         for s in (1, 2, 3):
             c = pltpu.make_async_remote_copy(

time: 109 us -> 108 us (level)
  no operation moved by 1% of the time
where the time goes in v7:
time: 108 us
  Pallas kernels  107 us (99%)
    pallas_call x1, Pallas kernels, step(): pl.pallas_call(functools.partial(step_kernel, images, count), out_shape=o...  100 us
    pallas_call x1, Pallas kernels, finish(): pl.pallas_call(functools.partial(finish_kernel, bins, classes), out_shape...  7.02 us

profile of v7, /device:TPU:0, one launch (start us, length us, event | category | flops | bytes accessed | tf_op | source)
XLA Modules:
  0.0 108.2 jit_solution(7548104088996963863)
XLA Ops:
  0.7 100.3 %step.1 = (bf16[4608,384]{1,0:T(8,128)(2,1)}, bf16[8,48,384]{2,1,0:T(8,128)(2,1)}, bf16[8,32,384]{2,1,0:T(8,128)(2,1)}, f32[2,48,256]{2,1,0:T(8,128)}) custom-call(s32[3]{0:T(128)} %refs_0_.1, s32[3]{0:T(128)} %refs_1_.1, s32[3]{0:T(128)} %refs_2_.1, bf16[3,4,32,32]{3,2,1,0:T(8,128)(2,1)} %refs_3_.1, bf16[3,4,32,32]{3,2,1,0:T(8,128)(2,1)} %refs_4_.2, ...), custom_call_target="tpu_custom_call" | custom-call | tf_op jit(solution)/shard_map/step/pallas_call | solution.py:974
  101.0 7.0 %finish.1 = (bf16[3,4,32,32]{3,2,1,0:T(8,128)(2,1)}, f32[3,4,32,32]{3,2,1,0:T(8,128)}, f32[100,384]{1,0:T(8,128)}, f32[1001,384]{1,0:T(8,128)}, f32[16,384]{1,0:...) custom-call(bf16[4608,384]{1,0:T(8,128)(2,1)} %get-tuple-element.44., ...), custom_call_target="tpu_custom_call" | custom-call | tf_op jit(solution)/shard_map/finish/pallas_call | solution.py:1163
